TPU v7x, 32 devices: a whole 2x2x4 slice. The times are simulated.
32 devices in a mesh: groups: 2 (over y), shot: 4 (over z), rcv: 2 (over x), rep: 2 (over core).
Axes of the slice: x: 2, y: 2, z: 4, core: 2. Of those that a mesh axis runs over, the one named last changes fastest.
Arguments:
- records: float32 [64, 131072], P(('groups', 'rcv'), ('shot', 'rep')), parts along dimension 0, may hold values from -6 to 6
- offsets: int32 [16, 32], P(('groups', 'shot', 'rep')), parts along dimension 0, may hold values from 0 to 130560, as said below
- filter_index: int32 [16, 32], P(('groups', 'shot', 'rep')), parts along dimension 0, may hold values from 0 to 7
- signatures: bfloat16 [8, 128], replicated, may hold values from -0.5 to 0.5
- thresholds: float32 [2, 256], replicated, may hold values from 0.3 to 2
Outputs:
- model_field: float32 [16, 32, 32, 512], P(('groups', 'shot', 'rep'), 'rcv'), parts along dimension 0
- residual: float32 [64, 131072], P(('groups', 'rcv'), ('shot', 'rep')), parts along dimension 0
There are 2 independent parts, one for each index of `groups`. A program takes and returns all parts, laid end to end along the dimension named above; an argument that names none is the same for every part. Nothing has to cross between parts.
Inputs may be any that keep to these rules, and one draw needn't show every extreme that they name: Every offset is a multiple of 128. Shot (x,y) starts in slab offsets[x,y] // 16384; within one row x of the shot grid at most 8 shots start in any one slab, and this bound is reached in every row. Every shot ends inside the record.
All inputs are finite; a program needn't handle non-finite values.
Results may differ from a plain program's by a relative error of at most 0.024.
Values may be sent and summed in bfloat16 or wider, within the bound.
A program may use at most 64 MiB of HBM per device.

v0:
```python
import functools
import math

import jax
import jax.numpy as jnp
import numpy as np
from jax import lax
from jax.experimental import pallas as pl
from jax.experimental.pallas import tpu as pltpu
from jax.sharding import PartitionSpec as P

NT = 512


def from_behind(value, axis, steps):
    count = lax.axis_size(axis)
    first, last = (max(0, -steps), min(count, count - steps))
    return lax.ppermute(value, axis, [(source, source + steps) for source in range(first, last)])


def time_table(count):
    samples = jnp.arange(count)
    bin_index = jnp.arange(count // 2)[:, None]
    angles = 2.0 * math.pi / count * (bin_index * samples[None, :] % count).astype(jnp.float32)
    parity = jnp.where(samples % 2 == 0, 1.0, -1.0).astype(jnp.float32)
    cosine = jnp.where(bin_index == 0, math.sqrt(1.0 / count), math.sqrt(2.0 / count)) * jnp.cos(
        angles
    )
    sine_part = jnp.where(
        bin_index == 0,
        math.sqrt(1.0 / count) * parity[None, :],
        -math.sqrt(2.0 / count) * jnp.sin(angles),
    )
    return jnp.stack([cosine, sine_part]).astype(jnp.bfloat16)


def shot_table(count):
    positions = jnp.arange(count)
    angles = (
        2.0
        * math.pi
        / count
        * (positions[:, None] * positions[None, :] % count).astype(jnp.float32)
    )
    scaling = 1.0 / math.sqrt(count)
    cosine = scaling * jnp.cos(angles)
    sine_part = scaling * jnp.sin(angles)
    upper_half = jnp.stack([cosine, sine_part], axis=1)
    lower_half = jnp.stack([-sine_part, cosine], axis=1)
    return jnp.stack([upper_half, lower_half]).astype(jnp.bfloat16)


def toeplitz_kernel(adjoint, taps_ref, out_ref):
    tap_count = taps_ref.shape[1]
    row_index = lax.broadcasted_iota(jnp.int32, (tap_count, tap_count), 0)
    col_index = lax.broadcasted_iota(jnp.int32, (tap_count, tap_count), 1)
    taps = taps_ref[...].astype(jnp.float32)
    for index in range(taps_ref.shape[0]):
        row = jnp.broadcast_to(taps[index : index + 1, :], (tap_count, tap_count))
        turned = pltpu.roll(row, 0, 1, stride=1, stride_axis=0)
        zeros = jnp.zeros_like(turned)
        near = jnp.where(col_index >= row_index, turned, zeros)
        far = jnp.where(col_index < row_index, turned, zeros)
        near, far = (near.T, far.T) if adjoint else (near, far)
        out_ref[index, :tap_count, :] = near.astype(jnp.bfloat16)
        out_ref[index, tap_count:, :] = far.astype(jnp.bfloat16)


def toeplitz_table(signatures, adjoint):
    count, tap_count = signatures.shape
    return pl.pallas_call(
        functools.partial(toeplitz_kernel, adjoint),
        out_shape=jax.ShapeDtypeStruct((count, 2 * tap_count, tap_count), jnp.bfloat16),
        in_specs=[pl.BlockSpec(memory_space=pltpu.VMEM)],
        out_specs=pl.BlockSpec(memory_space=pltpu.VMEM),
    )(signatures)


def apply_filter(traces, table, adjoint):
    empty = jnp.zeros_like(traces[:, :1])
    if adjoint:
        other = jnp.concatenate([traces[:, 1:], empty], axis=1)
    else:
        other = jnp.concatenate([empty, traces[:, :-1]], axis=1)
    return jnp.einsum(
        "sbrp,spq->sbrq",
        jnp.concatenate([traces, other], axis=3),
        table,
        preferred_element_type=jnp.float32,
    )


def rank_in_row(owners):
    shot_count = owners.shape[1]
    same_owner = owners[:, :, None] == owners[:, None, :]
    earlier = jnp.arange(shot_count)[None, :] < jnp.arange(shot_count)[:, None]
    return jnp.sum(same_owner & earlier[None], axis=2)


def to_slabs(payload):
    return lax.all_to_all(payload, ("shot", "rep"), split_axis=0, concat_axis=0, tiled=True)


def to_shots(payload):
    return lax.all_to_all(payload, ("shot", "rep"), split_axis=0, concat_axis=0, tiled=True)


def soft_limit(coefficients, threshold_row):
    magnitude = jnp.sqrt(coefficients[0] * coefficients[0] + coefficients[1] * coefficients[1])
    threshold_view = threshold_row[None, :, None, None]
    factor = 1.0 - threshold_view / jnp.maximum(magnitude, threshold_view)
    return (coefficients * factor[None]).astype(jnp.bfloat16)


def shrink(field_data, threshold_row, tables):
    table_time, table_x, table_y, table_r = tables
    rows_here, local_rcv, shot_count, sample_count = field_data.shape
    spectrum = jnp.einsum(
        "ckt,xryt->xckry",
        table_time,
        field_data.astype(jnp.bfloat16),
        preferred_element_type=jnp.float32,
    ).astype(jnp.bfloat16)
    bin_count = spectrum.shape[2]
    spectrum = spectrum.reshape(rows_here, 2, bin_count, local_rcv * shot_count)
    section_data = jnp.einsum(
        "akbx,xbfz->akfz",
        table_x,
        lax.all_to_all(spectrum, ("shot", "rep"), split_axis=2, concat_axis=0, tiled=True),
        preferred_element_type=jnp.float32,
    ).astype(jnp.bfloat16)
    all_rows, row_bins = (section_data.shape[1], section_data.shape[2])
    section_data = section_data.reshape(2, all_rows, row_bins, local_rcv, shot_count)
    section_data = lax.all_to_all(section_data, "rcv", split_axis=2, concat_axis=3, tiled=True)
    section_data = jnp.einsum(
        "ajby,bkfry->akfrj", table_y, section_data, preferred_element_type=jnp.float32
    ).astype(jnp.bfloat16)
    coefficients = jnp.einsum(
        "aqbr,bkfrj->akfqj", table_r, section_data, preferred_element_type=jnp.float32
    )
    shrunk = soft_limit(coefficients, threshold_row)
    section_data = jnp.einsum(
        "aqbr,akfqj->bkfrj", table_r, shrunk, preferred_element_type=jnp.float32
    ).astype(jnp.bfloat16)
    section_data = jnp.einsum(
        "ajby,akfrj->bkfry", table_y, section_data, preferred_element_type=jnp.float32
    ).astype(jnp.bfloat16)
    section_data = lax.all_to_all(section_data, "rcv", split_axis=3, concat_axis=2, tiled=True)
    section_data = section_data.reshape(2, all_rows, row_bins, local_rcv * shot_count)
    section_data = jnp.einsum(
        "akbx,akfz->bxfz", table_x, section_data, preferred_element_type=jnp.float32
    ).astype(jnp.bfloat16)
    result = jnp.einsum(
        "ckt,cxkz->xzt",
        table_time,
        lax.all_to_all(section_data, ("shot", "rep"), split_axis=1, concat_axis=2, tiled=True),
        preferred_element_type=jnp.float32,
    )
    return result.reshape(rows_here, local_rcv, shot_count, sample_count)


def body_by_rows(records, offsets, filter_index, signatures, thresholds):
    rows_here, shot_count = offsets.shape
    local_rcv, slab_len = records.shape
    slab_count = lax.axis_size(("shot", "rep"))
    rcv_count = lax.axis_size("rcv")
    tap_count = signatures.shape[1]
    sample_count = NT
    slab_blocks = slab_len // tap_count
    trace_blocks = sample_count // tap_count
    capacity = max(2, 2 * shot_count // slab_count)
    slot_count = slab_count * rows_here * capacity
    forward_tables = toeplitz_table(signatures, False)
    adjoint_tables = toeplitz_table(signatures, True)
    flat_index = filter_index.reshape(-1)
    forward_table = forward_tables[flat_index]
    adjoint_table = adjoint_tables[flat_index]
    owners = offsets // slab_len
    row_ids = jnp.arange(rows_here, dtype=jnp.int32)[:, None]
    slot_index = (
        owners * (rows_here * capacity) + row_ids * capacity + rank_in_row(owners)
    ).reshape(-1)
    every_offset = lax.all_gather(offsets, ("shot", "rep"), axis=0, tiled=True)
    every_owner = every_offset // slab_len
    every_start = every_offset // tap_count % slab_blocks
    every_rank = rank_in_row(every_owner)
    mine_mask = every_owner == lax.axis_index(("shot", "rep"))
    levels = jnp.arange(capacity, dtype=jnp.int32)
    picked = mine_mask[:, :, None] & (every_rank[:, :, None] == levels[None, None, :])
    table_in = jnp.sum(jnp.where(picked, every_start[:, :, None] + 1, 0), axis=1).reshape(-1)
    filled = table_in > 0
    block_steps = jnp.arange(trace_blocks, dtype=jnp.int32)
    target = jnp.where(
        filled[:, None],
        table_in[:, None] - 1 + block_steps[None, :],
        slab_blocks + trace_blocks - 1,
    )

    def correlate(record_field):
        record_low = (
            record_field.astype(jnp.bfloat16)
            .reshape(local_rcv, slab_blocks, tap_count)
            .transpose(1, 0, 2)
        )
        rim_blocks = from_behind(record_low[: trace_blocks - 1], ("shot", "rep"), -1)
        extended = jnp.concatenate(
            [record_low, rim_blocks, jnp.zeros((1, local_rcv, tap_count), jnp.bfloat16)], axis=0
        )
        windows = extended[target.reshape(-1)].reshape(
            slot_count, trace_blocks, local_rcv, tap_count
        )
        returned = to_shots(windows)
        traces = returned[slot_index]
        terms = apply_filter(traces, adjoint_table, True)
        terms = terms.reshape(rows_here, shot_count, trace_blocks, local_rcv, tap_count).transpose(
            0, 3, 1, 2, 4
        )
        return terms.reshape(rows_here, local_rcv, shot_count, sample_count)

    tables = (
        time_table(sample_count),
        shot_table(slab_count * rows_here),
        shot_table(shot_count),
        shot_table(local_rcv * rcv_count),
    )
    row_bins = sample_count // 2 // slab_count
    rcv_bins = row_bins // rcv_count
    bin_start = lax.axis_index(("shot", "rep")) * row_bins + lax.axis_index("rcv") * rcv_bins

    def threshold_for(level_index):
        return lax.dynamic_slice_in_dim(thresholds[level_index], bin_start, rcv_bins)

    model_field = shrink(correlate(records), threshold_for(0), tables)
    level_index = 1
    traces = model_field.astype(jnp.bfloat16).reshape(
        rows_here, local_rcv, shot_count, trace_blocks, tap_count
    )
    traces = traces.transpose(0, 2, 3, 1, 4).reshape(
        rows_here * shot_count, trace_blocks, local_rcv, tap_count
    )
    shots = apply_filter(traces, forward_table, False).astype(jnp.bfloat16)
    outgoing = (
        jnp.zeros((slot_count, trace_blocks, local_rcv, tap_count), jnp.bfloat16)
        .at[slot_index]
        .set(shots)
    )
    arrived = to_slabs(outgoing)
    slab_total = jnp.zeros((slab_blocks + trace_blocks, local_rcv, tap_count), jnp.float32)
    for block_step in range(trace_blocks):
        slab_total = slab_total.at[target[:, block_step]].add(
            arrived[:, block_step].astype(jnp.float32)
        )
    spill_over = slab_total[slab_blocks : slab_blocks + trace_blocks - 1]
    carried = from_behind(spill_over, ("shot", "rep"), 1)
    blended = slab_total[:slab_blocks].at[: trace_blocks - 1].add(carried)
    residual = records - blended.transpose(1, 0, 2).reshape(local_rcv, slab_len)
    model_field = shrink(model_field + correlate(residual), threshold_for(level_index), tables)
    return (model_field, residual)


def dot(left, right, left_dim=1, right_dim=0):
    return lax.dot_general(
        left, right, (((left_dim,), (right_dim,)), ((), ())), preferred_element_type=jnp.float32
    )


def fixed_time_table(count):
    samples = np.arange(count)
    bins = np.arange(count // 2)[:, None]
    angles = 2.0 * np.pi / count * (bins * samples[None, :] % count)
    scale = math.sqrt(2.0 / count)
    cosine = scale * np.cos(angles)
    sine = -scale * np.sin(angles)
    cosine[0] = math.sqrt(1.0 / count)
    sine[0] = math.sqrt(1.0 / count) * np.where(samples % 2 == 0, 1.0, -1.0)
    return np.stack([cosine, sine]).astype(jnp.bfloat16)


def fixed_shot_table(count):
    positions = np.arange(count)
    angles = 2.0 * np.pi / count * (positions[:, None] * positions[None, :] % count)
    cosine = np.cos(angles) / math.sqrt(count)
    sine = np.sin(angles) / math.sqrt(count)
    table = np.stack([np.stack([cosine, sine], 1), np.stack([-sine, cosine], 1)])
    return table.astype(jnp.bfloat16).astype(np.float32)


def analyse(with_model, starts_ref, picks_ref, blocks_ref, taps_ref, table_ref, *rest):
    model_ref = rest[0] if with_model else None
    out_ref, held_ref = rest[-2:]
    rcv, taps = blocks_ref.shape[1:]
    parts, _, bins, lanes = out_ref.shape
    slots = lanes // 2
    rows = held_ref.shape[0] // slots
    steps = rows // rcv
    half = parts * bins

    def one(slot, carry):
        window = blocks_ref[pl.ds(starts_ref[slot], steps)].reshape(rows, taps)
        later = jnp.concatenate([window[rcv:], jnp.zeros((rcv, taps), window.dtype)], axis=0)
        pair = jnp.concatenate([window, later], axis=1)
        terms = dot(pair, taps_ref[picks_ref[slot]])
        where = pl.ds(pl.multiple_of(slot * rows, rows), rows)
        if with_model:
            terms = terms + model_ref[where]
        held_ref[where] = terms
        return carry

    lax.fori_loop(0, slots, one, 0, unroll=8)
    together = math.gcd(rcv, 4)
    for first in range(0, rcv, together):
        traces = jnp.concatenate(
            [
                jnp.concatenate(
                    [
                        held_ref[pl.ds(step * rcv + line, slots, stride=rows), :].astype(jnp.bfloat16)
                        for step in range(steps)
                    ],
                    axis=1,
                )
                for line in range(first, first + together)
            ],
            axis=0,
        )
        both = dot(table_ref[...], traces, 1, 1)
        for line in range(together):
            piece = both[:, line * slots : (line + 1) * slots]
            joined = jnp.concatenate([piece[:half], piece[half:]], axis=1)
            out_ref[:, first + line] = joined.reshape(parts, bins, lanes).astype(jnp.bfloat16)


def slots_to_spectra(starts, picks, blocks, taps, table, model, parts, slots):
    rcv, width = blocks.shape[1:]
    samples = table.shape[1]
    vmem = pl.BlockSpec(memory_space=pltpu.VMEM)
    smem = pl.BlockSpec(memory_space=pltpu.SMEM)
    extra = () if model is None else (model,)
    return pl.pallas_call(
        functools.partial(analyse, model is not None),
        out_shape=jax.ShapeDtypeStruct((parts, rcv, samples // 2 // parts, 2 * slots), jnp.bfloat16),
        in_specs=[smem, smem, vmem, vmem, vmem] + [vmem] * len(extra),
        out_specs=vmem,
        scratch_shapes=[pltpu.VMEM((slots * rcv * samples // width, width), jnp.float32)],
    )(starts, picks, blocks, taps, table, *extra)


def upright(spectra_ref, lines, group_lanes):
    parts, _, bins, _ = spectra_ref.shape
    pieces = []
    for line in lines:
        turned = spectra_ref[:, line].reshape(parts * bins, -1).astype(jnp.float32).T
        turned = turned.astype(jnp.bfloat16)
        count = group_lanes // 2
        for low in range(0, turned.shape[0], group_lanes):
            pieces.append(
                jnp.concatenate(
                    [turned[low : low + count], turned[low + count : low + 2 * count]], axis=1
                )
            )
    return jnp.concatenate(pieces, axis=0)


def synthesise(starts_ref, picks_ref, spectra_ref, taps_ref, table_ref, model_ref, total_ref):
    rcv, lanes = spectra_ref.shape[1], spectra_ref.shape[3]
    slots = lanes // 2
    taps = model_ref.shape[1]
    rows = model_ref.shape[0] // slots
    steps = rows // rcv
    together = math.gcd(rcv, 4)
    for first in range(0, rcv, together):
        lines = range(first, first + together)
        fields = dot(upright(spectra_ref, lines, lanes), table_ref[...])
        for line in lines:
            low = (line - first) * slots
            for step in range(steps):
                model_ref[pl.ds(step * rcv + line, slots, stride=rows), :] = fields[
                    low : low + slots, step * taps : (step + 1) * taps
                ]
    total_ref[...] = jnp.zeros_like(total_ref)

    def one(slot, carry):
        trace = model_ref[pl.ds(pl.multiple_of(slot * rows, rows), rows)].astype(jnp.bfloat16)
        earlier = jnp.concatenate([jnp.zeros((rcv, taps), trace.dtype), trace[:-rcv]], axis=0)
        pair = jnp.concatenate([trace, earlier], axis=1)
        shot = dot(pair, taps_ref[picks_ref[slot]]).astype(jnp.bfloat16).astype(jnp.float32)
        where = pl.ds(starts_ref[slot], steps)
        total_ref[where] = total_ref[where] + shot.reshape(steps, rcv, taps)
        return carry

    lax.fori_loop(0, slots, one, 0, unroll=8)


def spectra_to_slab(starts, picks, spectra, taps, table, slab_blocks):
    _, rcv, _, lanes = spectra.shape
    width = taps.shape[2]
    steps = table.shape[1] // width
    vmem = pl.BlockSpec(memory_space=pltpu.VMEM)
    smem = pl.BlockSpec(memory_space=pltpu.SMEM)
    return pl.pallas_call(
        synthesise,
        out_shape=(
            jax.ShapeDtypeStruct((lanes // 2 * rcv * steps, width), jnp.float32),
            jax.ShapeDtypeStruct((slab_blocks + steps, rcv, width), jnp.float32),
        ),
        in_specs=[smem, smem, vmem, vmem, vmem],
        out_specs=(vmem, vmem),
    )(starts, picks, spectra, taps, table)


def record_kernel(groups, spectra_ref, table_ref, out_ref):
    count = out_ref.shape[2]
    together = spectra_ref.shape[1]
    fields = dot(upright(spectra_ref, range(together), 2 * count), table_ref[...])
    for line in range(together):
        for group in range(groups):
            low = (line * groups + group) * count
            out_ref[group, line] = fields[low : low + count]


def records_of(spectra, table, groups):
    parts, rcv, bins, lanes = spectra.shape
    samples = table.shape[1]
    count = lanes // 2 // groups
    together = math.gcd(rcv, 4)
    return pl.pallas_call(
        functools.partial(record_kernel, groups),
        grid=(rcv // together,),
        out_shape=jax.ShapeDtypeStruct((groups, rcv, count, samples), jnp.float32),
        in_specs=[
            pl.BlockSpec((parts, together, bins, lanes), lambda i: (0, i, 0, 0)),
            pl.BlockSpec((samples, samples), lambda i: (0, 0)),
        ],
        out_specs=pl.BlockSpec((groups, together, count, samples), lambda i: (0, i, 0, 0)),
    )(spectra, table)


def bins_kernel(place, halves, spectra_ref, go_ref, back_ref, cosine_ref, sine_ref, level_ref, out_ref):
    _, rcv, bins, lanes = spectra_ref.shape
    rows = rcv * bins
    rcv_count, slab_count = place.shape
    joined = jnp.concatenate(
        [
            jnp.concatenate(
                [spectra_ref[int(index)].reshape(rows, lanes) for index in line], axis=1
            )
            for line in place
        ],
        axis=0,
    )
    section = dot(joined, go_ref[...]).astype(jnp.bfloat16)
    half = section.shape[1] // 2
    near = dot(cosine_ref[...], section)
    far = dot(sine_ref[...], section)
    real = near[:, :half] + far[:, half:]
    imag = near[:, half:] - far[:, :half]
    level = level_ref[...]
    factor = 1.0 - level / jnp.maximum(jnp.sqrt(real * real + imag * imag), level)
    shrunk = jnp.concatenate([real * factor, imag * factor], axis=1).astype(jnp.bfloat16)
    near = dot(cosine_ref[...], shrunk)
    far = dot(sine_ref[...], shrunk)
    section = jnp.concatenate(
        [near[:, :half] - far[:, half:], far[:, :half] + near[:, half:]], axis=1
    ).astype(jnp.bfloat16)
    result = dot(section, back_ref[...], 1, 1).astype(jnp.bfloat16)
    width = result.shape[1] // slab_count
    for line in range(rcv_count):
        for slab in range(slab_count):
            piece = result[line * rows : (line + 1) * rows, slab * width : (slab + 1) * width]
            if halves == 2:
                piece = jnp.concatenate([piece[: rows // 2], piece[rows // 2 :]], axis=1)
            out_ref[int(place[line, slab])] = piece.reshape(rcv // halves, bins, halves * width)


def bins_stage(spectra, go, back, cosine, sine, level, place, halves):
    parts, rcv, bins, _ = spectra.shape
    width = halves * back.shape[0] // place.shape[1]
    vmem = pl.BlockSpec(memory_space=pltpu.VMEM)
    return pl.pallas_call(
        functools.partial(bins_kernel, place, halves),
        out_shape=jax.ShapeDtypeStruct((parts, rcv // halves, bins, width), jnp.bfloat16),
        in_specs=[vmem] * 6,
        out_specs=vmem,
    )(spectra, go, back, cosine, sine, level)


def body_by_slots(records, offsets, filter_index, signatures, thresholds):
    rows_here, shot_count = offsets.shape
    local_rcv, slab_len = records.shape
    slab_count = lax.axis_size(("shot", "rep"))
    rep_count = lax.axis_size("rep")
    rcv_count = lax.axis_size("rcv")
    parts = slab_count * rcv_count
    everyone = ("shot", "rcv", "rep")
    tap_count = signatures.shape[1]
    slab_blocks = slab_len // tap_count
    steps = NT // tap_count
    capacity = max(2, 2 * shot_count // slab_count)
    row_count = rows_here * slab_count
    slots = row_count * capacity
    bins = NT // 2 // parts
    place = np.array(
        [
            [((slab // rep_count) * rcv_count + line) * rep_count + slab % rep_count for slab in range(slab_count)]
            for line in range(rcv_count)
        ]
    )

    time_table_fixed = jnp.asarray(fixed_time_table(NT).reshape(NT, NT))
    table_x, table_y, table_r = (
        fixed_shot_table(count) for count in (row_count, shot_count, local_rcv * rcv_count)
    )
    grid_table = np.einsum("ajby,bkcx->cxyakj", table_y, table_x).astype(jnp.bfloat16)
    row_table = np.ascontiguousarray(grid_table.transpose(1, 0, 2, 3, 4, 5))
    points = 2 * row_count * shot_count
    grid_table = jnp.asarray(grid_table.reshape(points, points))
    row_table = jnp.asarray(row_table.reshape(points, points))
    same = np.eye(bins, dtype=np.float32)
    cosine = jnp.asarray(np.kron(table_r[0, :, 0], same).astype(jnp.bfloat16))
    sine = jnp.asarray(np.kron(table_r[0, :, 1], same).astype(jnp.bfloat16))

    shots = jnp.stack([offsets, filter_index])
    every = lax.all_to_all(
        jnp.broadcast_to(shots[None], (slab_count,) + shots.shape), ("shot", "rep"), 0, 0, tiled=True
    )
    every_offset = every[:, 0].reshape(row_count, shot_count)
    every_pick = every[:, 1].reshape(row_count, shot_count)
    every_owner = every_offset // slab_len
    every_rank = rank_in_row(every_owner)
    slabs = jnp.arange(slab_count, dtype=jnp.int32)
    ranks = jnp.arange(capacity, dtype=jnp.int32)
    taken = (every_owner[None, :, None, :] == slabs[:, None, None, None]) & (
        every_rank[None, :, None, :] == ranks[None, None, :, None]
    )
    point_of = jnp.arange(row_count * shot_count, dtype=jnp.int32).reshape(row_count, shot_count)
    code = jnp.sum(jnp.where(taken, point_of[None, :, None, :] + 1, 0), axis=3).reshape(
        slab_count, 1, slots
    )
    code = jnp.where(
        code > 0, code - 1 + row_count * shot_count * jnp.arange(2, dtype=jnp.int32)[None, :, None], -1
    ).reshape(-1)
    chosen = (code[:, None] == jnp.arange(points, dtype=jnp.int32)[None, :]).astype(jnp.bfloat16)
    slot_table = dot(chosen, grid_table).astype(jnp.bfloat16)
    mine = (every_owner == lax.axis_index(("shot", "rep")))[:, None, :] & (
        every_rank[:, None, :] == ranks[None, :, None]
    )
    every_start = every_offset // tap_count % slab_blocks
    starts = jnp.sum(jnp.where(mine, every_start[:, None, :], 0), axis=2).reshape(-1)
    picks = jnp.sum(jnp.where(mine, every_pick[:, None, :], 0), axis=2).reshape(-1)
    adjoint_tables = toeplitz_table(signatures, True)

    def correlate(blocks, rim, model):
        low = blocks.astype(jnp.bfloat16)
        extended = jnp.concatenate([low, rim, jnp.zeros_like(low[:1])], axis=0)
        return slots_to_spectra(
            starts, picks, extended, adjoint_tables, time_table_fixed, model, parts, slots
        )

    bin_start = lax.axis_index(everyone) * bins

    def swap(value):
        return lax.all_to_all(value, everyone, 0, 0, tiled=True)

    def shrink_at(spectra, index, back, halves):
        level = lax.dynamic_slice_in_dim(thresholds[index], bin_start, bins)
        level = jnp.tile(level, local_rcv * rcv_count)[:, None]
        return bins_stage(swap(spectra), slot_table, back, cosine, sine, level, place, halves)

    record_blocks = records.reshape(local_rcv, slab_blocks, tap_count).transpose(1, 0, 2)
    rim = from_behind(record_blocks[: steps - 1].astype(jnp.bfloat16), ("shot", "rep"), -1)
    spectra = shrink_at(correlate(record_blocks, rim, None), 0, slot_table, 1)
    spectra, taps = lax.optimization_barrier((spectra, signatures))
    forward_tables = toeplitz_table(taps, False)
    model, total = spectra_to_slab(
        starts, picks, swap(spectra), forward_tables, time_table_fixed, slab_blocks
    )
    spill = total[slab_blocks : slab_blocks + steps - 1]
    left = record_blocks - total[:slab_blocks]
    carried = from_behind(spill, ("shot", "rep"), 1)
    ahead = from_behind(left[: steps - 1], ("shot", "rep"), -1)
    left = left.at[: steps - 1].add(-carried)
    rim = (ahead - spill).astype(jnp.bfloat16)
    residual = left.transpose(1, 0, 2).reshape(local_rcv, slab_len)
    spectra = swap(shrink_at(correlate(left, rim, model), 1, row_table, 2))
    model = records_of(spectra, time_table_fixed, 2)
    return (model.reshape(rows_here, local_rcv, shot_count, NT), residual)


def body(records, offsets, filter_index, signatures, thresholds):
    rows_here, shot_count = offsets.shape
    slab_count = lax.axis_size(("shot", "rep"))
    parts = slab_count * lax.axis_size("rcv")
    slots = rows_here * slab_count * max(2, 2 * shot_count // slab_count)
    table_rows = 2 * rows_here * slab_count * shot_count
    fits = table_rows <= 1024 and rows_here == 1 and slots == 64 and 4 * shot_count == 128
    fits = fits and records.shape[0] == 16 and NT // 2 // parts == 16
    run = body_by_slots if fits else body_by_rows
    return run(records, offsets, filter_index, signatures, thresholds)


def solution(mesh):
    in_specs = (
        P(("groups", "rcv"), ("shot", "rep")),
        P(("groups", "shot", "rep"), None),
        P(("groups", "shot", "rep"), None),
        P(),
        P(),
    )
    out_specs = (
        P(("groups", "shot", "rep"), "rcv", None, None),
        P(("groups", "rcv"), ("shot", "rep")),
    )
    return jax.shard_map(body, mesh=mesh, in_specs=in_specs, out_specs=out_specs, check_vma=False)
```

profile of v0, /device:TPU:0, one launch (start us, length us, event | category | flops | bytes accessed | tf_op | source)
XLA Modules:
  0.0 175.1 jit_solution(9196672602870873777)
XLA Ops:
  2.0 6.4 %all-to-all-start = ((s32[8,2,1,32]{3,2,1,0:T(1,128)}), s32[8,2,1,32]{3,2,1,0:T(1,128)S(1)}, u32[]{:S(2)}, u32[]{:S(2)}) async-start(s32[8,2,1,32]{3,2,1,0:T(1,128)} %broadcast_in_dim.68), calls=%async_computation | async-start | bytes 16384 | tf_op jit(solution)/shard_map/all_to_all | solution.py:522
  8.5 1.3 collective-permute-start
  9.8 1.8 %shard_map.113.taps_ref = bf16[8,256,128]{2,1,0:T(8,128)(2,1)} custom-call(bf16[8,128]{1,0:T(8,128)(2,1)} %taps_ref.2), custom_call_target="tpu_custom_call" | custom-call | tf_op jit(solution)/shard_map/pallas_call | solution.py:71
  11.6 2.3 %all-to-all-done = s32[8,2,1,32]{3,2,1,0:T(1,128)S(1)} async-done(((s32[8,2,1,32]{3,2,1,0:T(1,128)}), s32[8,2,1,32]{3,2,1,0:T(1,128)S(1)}, u32[]{:S(2)}, u32[]{:S(2)}) %all-to-all-start) | async-done | bytes 2080 | tf_op jit(solution)/shard_map/all_to_all | solution.py:522
  16.9 5.8 %shard_map.114 = bf16[16,16,16,128]{3,2,1,0:T(8,128)(2,1)} custom-call(s32[64]{0:T(128)} %reshape.273.starts_ref, s32[64]{0:T(128)} %reshape.274.picks_ref, bf16[132,16,128]{2,1,0:T(8,128)(2,1)} %maximum_maximum_fusion.blocks_ref, bf16[8,256,128]{2,1,0:T(8,128)(2,1)} %shard_map.113.taps_ref, bf16[512,512]{1,0:T(8,128)(2,1)} %constant.109.clone.table_ref), custom_call_target="tpu_custom_call" | custom-call | tf_op jit(solution)/shard_map/pallas_call | solution.py:338
  22.7 4.7 %all-to-all-start.1 = ((bf16[16,16,16,128]{3,2,1,0:T(8,128)(2,1)}), bf16[16,16,16,128]{3,2,1,0:T(8,128)(2,1)S(1)}, u32[]{:S(2)}, u32[]{:S(2)}) async-start(bf16[16,16,16,128]{3,2,1,0:T(8,128)(2,1)} %shard_map.114), calls=%async_computation.1 | async-start | bytes 2097152 | tf_op jit(solution)/shard_map/all_to_all | solution.py:561
  29.9 1.7 fusion.1.go_ref.back_ref
  31.7 18.6 %all-to-all-done.1.spectra_ref = bf16[16,16,16,128]{3,2,1,0:T(8,128)(2,1)S(1)} async-done(((bf16[16,16,16,128]{3,2,1,0:T(8,128)(2,1)}), bf16[16,16,16,128]{3,2,1,0:T(8,128)(2,1)S(1)}, u32[]{:S(2)}, u32[]{:S(2)}) %all-to-all-start.1) | async-done | bytes 1048608 | tf_op jit(solution)/shard_map/all_to_all | solution.py:561
  51.2 6.3 %shard_map.115 = bf16[16,16,16,128]{3,2,1,0:T(8,128)(2,1)} custom-call(bf16[16,16,16,128]{3,2,1,0:T(8,128)(2,1)} %copy-done.3, bf16[1024,512]{1,0:T(8,128)(2,1)} %fusion.1.go_ref.back_ref, bf16[1024,512]{1,0:T(8,128)(2,1)} %fusion.1.go_ref.back_ref, bf16[512,512]{1,0:T(8,128)(2,1)} %constant.112.clone.cosine_ref, bf16[512,512]{1,0:T(8,128)(2,1)} %constant.113.clone.sine_ref, ...), custom_call_target="tpu_custom_call" | custom-call | tf_op jit(solution)/shard_map/pallas_call | solution.py:478
  57.5 6.8 %all-to-all-start.2 = ((bf16[16,16,16,128]{3,2,1,0:T(8,128)(2,1)}), bf16[16,16,16,128]{3,2,1,0:T(8,128)(2,1)S(1)}, u32[]{:S(2)}, u32[]{:S(2)}) async-start(bf16[16,16,16,128]{3,2,1,0:T(8,128)(2,1)} %shard_map.115), calls=%async_computation.2 | async-start | bytes 2097152 | tf_op jit(solution)/shard_map/all_to_all | solution.py:561
  64.3 1.6 shard_map.116.taps_ref
  66.0 21.3 %all-to-all-done.2.spectra_ref = bf16[16,16,16,128]{3,2,1,0:T(8,128)(2,1)S(1)} async-done(((bf16[16,16,16,128]{3,2,1,0:T(8,128)(2,1)}), bf16[16,16,16,128]{3,2,1,0:T(8,128)(2,1)S(1)}, u32[]{:S(2)}, u32[]{:S(2)}) %all-to-all-start.2) | async-done | bytes 1048608 | tf_op jit(solution)/shard_map/all_to_all | solution.py:561
  88.2 7.2 %shard_map.117 = (f32[4096,128]{1,0:T(8,128)}, f32[132,16,128]{2,1,0:T(8,128)}) custom-call(s32[64]{0:T(128)} %reshape.273.starts_ref, s32[64]{0:T(128)} %reshape.274.picks_ref, bf16[16,16,16,128]{3,2,1,0:T(8,128)(2,1)} %copy-done.2, bf16[8,256,128]{2,1,0:T(8,128)(2,1)} %shard_map.116.taps_ref, bf16[512,512]{1,0:T(8,128)(2,1)} %constant.109.clone.table_ref), custom_call_target="tpu_custom_call" | custom-call | tf_op jit(solution)/shard_map/pallas_call | solution.py:399
  95.4 1.3 fusion.2
  96.7 1.3 collective-permute-start.2
  98.0 2.0 %collective-permute-done.2 = f32[3,16,128]{2,1,0:T(8,128)S(1)} collective-permute-done((f32[3,16,128]{2,1,0:T(8,128)S(1)}, f32[3,16,128]{2,1,0:T(8,128)S(1)}, u32[]{:S(2)}, u32[]{:S(2)}) %collective-permute-start.2) | collective-permute-done | bytes 24608 | tf_op jit(solution)/shard_map/ppermute | solution.py:18
  100.7 5.2 %collective-permute-start.1 = (f32[3,16,128]{2,1,0:T(8,128)S(1)}, f32[3,16,128]{2,1,0:T(8,128)S(1)}, u32[]{:S(2)}, u32[]{:S(2)}) collective-permute-start(f32[3,16,128]{2,1,0:T(8,128)S(1)} %get-tuple-element.26), channel_id=1, source_target_pairs={{0,1},{1,4},{4,5},{5,8},{8,9},{9,12},{12,13},{2,3},{3,6},{6,7},{7,... | collective-permute-start | bytes 73736 | tf_op jit(solution)/shard_map/ppermute | solution.py:18
  107.9 6.4 %shard_map.118 = bf16[16,16,16,128]{3,2,1,0:T(8,128)(2,1)} custom-call(s32[64]{0:T(128)} %reshape.273.starts_ref, s32[64]{0:T(128)} %reshape.274.picks_ref, bf16[132,16,128]{2,1,0:T(8,128)(2,1)} %maximum_maximum_fusion.1.blocks_ref, bf16[8,256,128]{2,1,0:T(8,128)(2,1)} %shard_map.113.taps_ref, bf16[512,512]{1,0:T(8,128)(2,1)} %constant.109.clone.table_ref, ...), custom_call_target="tpu_custom_call" | custom-call | tf_op jit(solution)/shard_map/pallas_call | solution.py:338
  114.4 6.6 %all-to-all-start.3 = ((bf16[16,16,16,128]{3,2,1,0:T(8,128)(2,1)}), bf16[16,16,16,128]{3,2,1,0:T(8,128)(2,1)S(1)}, u32[]{:S(2)}, u32[]{:S(2)}) async-start(bf16[16,16,16,128]{3,2,1,0:T(8,128)(2,1)} %shard_map.118), calls=%async_computation.3 | async-start | bytes 2097152 | tf_op jit(solution)/shard_map/all_to_all | solution.py:561
  121.8 22.0 %all-to-all-done.3.spectra_ref = bf16[16,16,16,128]{3,2,1,0:T(8,128)(2,1)S(1)} async-done(((bf16[16,16,16,128]{3,2,1,0:T(8,128)(2,1)}), bf16[16,16,16,128]{3,2,1,0:T(8,128)(2,1)S(1)}, u32[]{:S(2)}, u32[]{:S(2)}) %all-to-all-start.3) | async-done | bytes 1048608 | tf_op jit(solution)/shard_map/all_to_all | solution.py:561
  144.8 5.8 %shard_map.119 = bf16[16,8,16,128]{3,2,1,0:T(8,128)(2,1)} custom-call(bf16[16,16,16,128]{3,2,1,0:T(8,128)(2,1)} %copy-done.1, bf16[1024,512]{1,0:T(8,128)(2,1)} %fusion.1.go_ref.back_ref, bf16[512,512]{1,0:T(8,128)(2,1)} %constant.111.clone.back_ref, bf16[512,512]{1,0:T(8,128)(2,1)} %constant.112.clone.cosine_ref, ...), custom_call_target="tpu_custom_call" | custom-call | tf_op jit(solution)/shard_map/pallas_call | solution.py:478
  150.5 6.8 %all-to-all-start.4 = ((bf16[16,8,16,128]{3,2,1,0:T(8,128)(2,1)}), bf16[16,8,16,128]{3,2,1,0:T(8,128)(2,1)S(1)}, u32[]{:S(2)}, u32[]{:S(2)}) async-start(bf16[16,8,16,128]{3,2,1,0:T(8,128)(2,1)} %shard_map.119), calls=%async_computation.4 | async-start | bytes 1048576 | tf_op jit(solution)/shard_map/all_to_all | solution.py:561
  158.4 13.2 %all-to-all-done.4.spectra_ref = bf16[16,8,16,128]{3,2,1,0:T(8,128)(2,1)S(1)} async-done(((bf16[16,8,16,128]{3,2,1,0:T(8,128)(2,1)}), bf16[16,8,16,128]{3,2,1,0:T(8,128)(2,1)S(1)}, u32[]{:S(2)}, u32[]{:S(2)}) %all-to-all-start.4) | async-done | bytes 524320 | tf_op jit(solution)/shard_map/all_to_all | solution.py:561
  172.4 2.7 %shard_map.120 = f32[2,8,32,512]{3,2,1,0:T(8,128)} custom-call(bf16[16,8,16,128]{3,2,1,0:T(8,128)(2,1)} %copy-done.4, bf16[512,512]{1,0:T(8,128)(2,1)} %constant.109.clone.table_ref), custom_call_target="tpu_custom_call" | custom-call | tf_op jit(solution)/shard_map/pallas_call | solution.py:425
  (52 shorter events, 15.3 us)
Async XLA Ops:
  0.6 7.7 %copy-start = (f32[16,16384]{1,0:T(8,128)S(1)}, f32[16,16384]{1,0:T(8,128)}, u32[]{:S(2)}) copy-start(f32[16,16384]{1,0:T(8,128)} %param.12) | copy-start | bytes 3145732
  2.0 12.0 %all-to-all-start = ((s32[8,2,1,32]{3,2,1,0:T(1,128)}), s32[8,2,1,32]{3,2,1,0:T(1,128)S(1)}, u32[]{:S(2)}, u32[]{:S(2)}) async-start(s32[8,2,1,32]{3,2,1,0:T(1,128)} %broadcast_in_dim.68), calls=%async_computation | async-start | bytes 16384 | tf_op jit(solution)/shard_map/all_to_all | solution.py:522
  8.5 7.4 %collective-permute-start = (bf16[3,16,128]{2,1,0:T(8,128)(2,1)S(1)}, bf16[3,16,128]{2,1,0:T(8,128)(2,1)S(1)}, u32[]{:S(2)}, u32[]{:S(2)}) collective-permute-start(bf16[3,16,128]{2,1,0:T(8,128)(2,1)S(1)} %slice.57), channel_id=1, source_target_pairs={{1,0},{4,1},{5,4},{8,5},{9,8},{12,9},{13,12},{3,2},{6,3},{7,6},{10... | collective-permute-start | bytes 36872 | tf_op jit(solution)/shard_map/ppermute | solution.py:18
  16.9 10.5 %copy-start.5 = (f32[2,256]{1,0:T(2,128)S(1)}, f32[2,256]{1,0:T(2,128)}, u32[]{:S(2)}) copy-start(f32[2,256]{1,0:T(2,128)} %param.16) | copy-start | bytes 6148
  16.9 13.0 %copy-start.6 = (bf16[512,512]{1,0:T(8,128)(2,1)S(1)}, bf16[512,512]{1,0:T(8,128)(2,1)}, u32[]{:S(2)}) copy-start(bf16[512,512]{1,0:T(8,128)(2,1)} %constant.110.clone) | copy-start | bytes 1572868
  22.7 27.6 %all-to-all-start.1 = ((bf16[16,16,16,128]{3,2,1,0:T(8,128)(2,1)}), bf16[16,16,16,128]{3,2,1,0:T(8,128)(2,1)S(1)}, u32[]{:S(2)}, u32[]{:S(2)}) async-start(bf16[16,16,16,128]{3,2,1,0:T(8,128)(2,1)} %shard_map.114), calls=%async_computation.1 | async-start | bytes 2097152 | tf_op jit(solution)/shard_map/all_to_all | solution.py:561
  50.3 1.0 copy-start.3
  57.5 29.7 %all-to-all-start.2 = ((bf16[16,16,16,128]{3,2,1,0:T(8,128)(2,1)}), bf16[16,16,16,128]{3,2,1,0:T(8,128)(2,1)S(1)}, u32[]{:S(2)}, u32[]{:S(2)}) async-start(bf16[16,16,16,128]{3,2,1,0:T(8,128)(2,1)} %shard_map.115), calls=%async_computation.2 | async-start | bytes 2097152 | tf_op jit(solution)/shard_map/all_to_all | solution.py:561
  87.2 1.0 copy-start.2
  96.7 3.3 %collective-permute-start.2 = (f32[3,16,128]{2,1,0:T(8,128)S(1)}, f32[3,16,128]{2,1,0:T(8,128)S(1)}, u32[]{:S(2)}, u32[]{:S(2)}) collective-permute-start(f32[3,16,128]{2,1,0:T(8,128)S(1)} %slice.58), channel_id=1, source_target_pairs={{1,0},{4,1},{5,4},{8,5},{9,8},{12,9},{13,12},{3,2},{6,3},{7,6},{10... | collective-permute-start | bytes 73736 | tf_op jit(solution)/shard_map/ppermute | solution.py:18
  100.7 6.0 %collective-permute-start.1 = (f32[3,16,128]{2,1,0:T(8,128)S(1)}, f32[3,16,128]{2,1,0:T(8,128)S(1)}, u32[]{:S(2)}, u32[]{:S(2)}) collective-permute-start(f32[3,16,128]{2,1,0:T(8,128)S(1)} %get-tuple-element.26), channel_id=1, source_target_pairs={{0,1},{1,4},{4,5},{5,8},{8,9},{9,12},{12,13},{2,3},{3,6},{6,7},{7,... | collective-permute-start | bytes 73736 | tf_op jit(solution)/shard_map/ppermute | solution.py:18
  114.4 29.5 %all-to-all-start.3 = ((bf16[16,16,16,128]{3,2,1,0:T(8,128)(2,1)}), bf16[16,16,16,128]{3,2,1,0:T(8,128)(2,1)S(1)}, u32[]{:S(2)}, u32[]{:S(2)}) async-start(bf16[16,16,16,128]{3,2,1,0:T(8,128)(2,1)} %shard_map.118), calls=%async_computation.3 | async-start | bytes 2097152 | tf_op jit(solution)/shard_map/all_to_all | solution.py:561
  143.8 1.0 copy-start.1
  150.5 21.1 %all-to-all-start.4 = ((bf16[16,8,16,128]{3,2,1,0:T(8,128)(2,1)}), bf16[16,8,16,128]{3,2,1,0:T(8,128)(2,1)S(1)}, u32[]{:S(2)}, u32[]{:S(2)}) async-start(bf16[16,8,16,128]{3,2,1,0:T(8,128)(2,1)} %shard_map.119), calls=%async_computation.4 | async-start | bytes 1048576 | tf_op jit(solution)/shard_map/all_to_all | solution.py:561
  171.6 0.8 copy-start.4
where the time goes:
time: 176 us; the launch traced here: 175 us
  waiting for transfers between devices  80.3 us (46%)
  starting transfers between devices  39 us (22%)
  Pallas kernels  37.5 us (21%)
  local copies, waits for them, and re-layouts  8.85 us (5%)
  other arithmetic  6.91 us (4%)
    all_to_all x4, waiting for transfers between devices, swap(): return lax.all_to_all(value, everyone, 0, 0, tiled=True)  75.1 us
    all_to_all x4, starting transfers between devices, swap(): return lax.all_to_all(value, everyone, 0, 0, tiled=True)  24.8 us
    pallas_call x2, Pallas kernels, slots_to_spectra(): pl.pallas_call(functools.partial(analyse, model is not None), out_shape=j...  12.2 us
    pallas_call x2, Pallas kernels, bins_stage(): pl.pallas_call(functools.partial(bins_kernel, place, halves), out_shape=j...  12.1 us
    ppermute x3, starting transfers between devices, from_behind(): lax.ppermute(value, axis, [(source, source + steps) for source in range(f...  7.79 us
    pallas_call x1, Pallas kernels, spectra_to_slab(): pl.pallas_call(synthesise, out_shape=(jax.ShapeDtypeStruct((lanes // 2 *...  7.16 us
    all_to_all x1, starting transfers between devices, body_by_slots(): lax.all_to_all(jnp.broadcast_to(shots[None], (slab_count,) + shots.shape)...  6.35 us
    unnamed x14, local copies, waits for them, and re-layouts  3.72 us
  transfers between devices with their start and end apart: 8, of which 7 were waited for; matrix products, arithmetic and copies ran while one was open for 5% of the time, Pallas kernels for 2%

commit v1 on v0

--- a/solution.py
+++ b/solution.py
@@ -285,15 +285,53 @@
     return table.astype(jnp.bfloat16).astype(np.float32)
 
 
-def analyse(with_model, starts_ref, picks_ref, blocks_ref, taps_ref, table_ref, *rest):
-    model_ref = rest[0] if with_model else None
-    out_ref, held_ref = rest[-2:]
+MESH = pl.DeviceIdType.MESH
+AXES = ("shot", "rcv", "rep")
+
+
+def neighbours(sizes):
+    every = [(a, b, c) for a in range(sizes[0]) for b in range(sizes[1]) for c in range(sizes[2])]
+    far = sizes[0] // 2
+    return sorted(every[1:], key=lambda step: (abs(step[0] - far), -step[1], -step[2]))
+
+
+def device_at(sizes, step):
+    spot = [lax.rem(lax.axis_index(axis) + hop, size) for axis, hop, size in zip(AXES, step, sizes)]
+    index = (spot[0] * sizes[1] + spot[1]) * sizes[2] + spot[2]
+    return dict(zip(AXES, spot)), index
+
+
+def greet(sizes):
+    barrier = pltpu.get_barrier_semaphore()
+    steps = neighbours(sizes)
+    for step in steps:
+        pl.semaphore_signal(barrier, inc=1, device_id=device_at(sizes, step)[0], device_id_type=MESH)
+    pl.semaphore_wait(barrier, len(steps))
+
+
+def copies(sizes, source, target, send_sem, recv_sem):
+    mine = device_at(sizes, (0, 0, 0))[1]
+    made = []
+    for number, step in enumerate(neighbours(sizes)):
+        device, index = device_at(sizes, step)
+        made.append(
+            pltpu.make_async_remote_copy(
+                src_ref=source.at[index],
+                dst_ref=target.at[mine],
+                send_sem=send_sem.at[number],
+                recv_sem=recv_sem.at[number],
+                device_id=device,
+                device_id_type=MESH,
+            )
+        )
+    return made
+
+
+def correlate_slots(starts_ref, picks_ref, blocks_ref, taps_ref, model_ref, held_ref):
     rcv, taps = blocks_ref.shape[1:]
-    parts, _, bins, lanes = out_ref.shape
-    slots = lanes // 2
+    slots = starts_ref.shape[0]
     rows = held_ref.shape[0] // slots
     steps = rows // rcv
-    half = parts * bins
 
     def one(slot, carry):
         window = blocks_ref[pl.ds(starts_ref[slot], steps)].reshape(rows, taps)
@@ -301,67 +339,176 @@
         pair = jnp.concatenate([window, later], axis=1)
         terms = dot(pair, taps_ref[picks_ref[slot]])
         where = pl.ds(pl.multiple_of(slot * rows, rows), rows)
-        if with_model:
+        if model_ref is not None:
             terms = terms + model_ref[where]
         held_ref[where] = terms
         return carry
 
     lax.fori_loop(0, slots, one, 0, unroll=8)
+
+
+def gather_traces(held_ref, traces_ref, rcv, slots):
+    rows = held_ref.shape[0] // slots
+    steps = rows // rcv
+    for line in range(rcv):
+        traces_ref[line * slots : (line + 1) * slots] = jnp.concatenate(
+            [
+                held_ref[pl.ds(step * rcv + line, slots, stride=rows), :].astype(jnp.bfloat16)
+                for step in range(steps)
+            ],
+            axis=1,
+        )
+
+
+def spectra_chunk(table, traces_ref, out_ref, rcv, slots):
+    parts, rows, lanes = out_ref.shape
+    bins = rows // rcv
+    half = parts * bins
+    pack = max(1, 16 // bins)
     together = math.gcd(rcv, 4)
     for first in range(0, rcv, together):
-        traces = jnp.concatenate(
-            [
-                jnp.concatenate(
-                    [
-                        held_ref[pl.ds(step * rcv + line, slots, stride=rows), :].astype(jnp.bfloat16)
-                        for step in range(steps)
-                    ],
-                    axis=1,
-                )
-                for line in range(first, first + together)
-            ],
-            axis=0,
-        )
-        both = dot(table_ref[...], traces, 1, 1)
-        for line in range(together):
-            piece = both[:, line * slots : (line + 1) * slots]
-            joined = jnp.concatenate([piece[:half], piece[half:]], axis=1)
-            out_ref[:, first + line] = joined.reshape(parts, bins, lanes).astype(jnp.bfloat16)
-
-
-def slots_to_spectra(starts, picks, blocks, taps, table, model, parts, slots):
+        both = dot(table, traces_ref[first * slots : (first + together) * slots], 1, 1)
+        for low in range(0, together, pack):
+            pieces = []
+            for line in range(low, low + pack):
+                piece = both[:, line * slots : (line + 1) * slots]
+                joined = jnp.concatenate([piece[:half], piece[half:]], axis=1)
+                pieces.append(joined.reshape(parts, bins, lanes))
+            out_ref[:, (first + low) * bins : (first + low + pack) * bins] = jnp.concatenate(
+                pieces, axis=1
+            ).astype(jnp.bfloat16)
+
+
+def bins_chunk(place, halves, spectra_ref, go_ref, back_ref, cosine, sine, level, out_ref):
+    _, rows, _ = spectra_ref.shape
+    rcv_count, slab_count = place.shape
+    joined = jnp.concatenate(
+        [
+            jnp.concatenate([spectra_ref[int(index)] for index in line], axis=1)
+            for line in place
+        ],
+        axis=0,
+    )
+    section = dot(joined, go_ref[...]).astype(jnp.bfloat16)
+    half = section.shape[1] // 2
+    near = dot(cosine, section)
+    far = dot(sine, section)
+    real = near[:, :half] + far[:, half:]
+    imag = near[:, half:] - far[:, :half]
+    factor = 1.0 - level / jnp.maximum(jnp.sqrt(real * real + imag * imag), level)
+    shrunk = jnp.concatenate([real * factor, imag * factor], axis=1).astype(jnp.bfloat16)
+    near = dot(cosine, shrunk)
+    far = dot(sine, shrunk)
+    section = jnp.concatenate(
+        [near[:, :half] - far[:, half:], far[:, :half] + near[:, half:]], axis=1
+    ).astype(jnp.bfloat16)
+    result = dot(section, back_ref[...], 1, 1).astype(jnp.bfloat16)
+    width = result.shape[1] // slab_count
+    for line in range(rcv_count):
+        for slab in range(slab_count):
+            piece = result[line * rows : (line + 1) * rows, slab * width : (slab + 1) * width]
+            if halves == 2:
+                piece = jnp.concatenate([piece[: rows // 2], piece[rows // 2 :]], axis=1)
+            out_ref[int(place[line, slab])] = piece
+
+
+def round_trip(sizes, place, halves, with_model, starts_ref, picks_ref, blocks_ref, taps_ref, table_ref, go_ref, back_ref, cosine_ref, sine_ref, level_ref, *rest):
+    model_ref = rest[0] if with_model else None
+    out_ref, held_ref, traces_ref, sent_ref, got_ref, answer_ref = rest[-10:-4]
+    send_sems, recv_sems, back_sems, home_sems = rest[-4:]
+    rcv = blocks_ref.shape[1]
+    slots = starts_ref.shape[0]
+    chunks = table_ref.shape[0]
+    greet(sizes)
+    mine = device_at(sizes, (0, 0, 0))[1]
+    correlate_slots(starts_ref, picks_ref, blocks_ref, taps_ref, model_ref, held_ref)
+    gather_traces(held_ref, traces_ref, rcv, slots)
+    going = []
+    for chunk in range(chunks):
+        spectra_chunk(table_ref[chunk], traces_ref, sent_ref.at[chunk], rcv, slots)
+        made = copies(
+            sizes, sent_ref.at[chunk], got_ref.at[chunk], send_sems.at[chunk], recv_sems.at[chunk]
+        )
+        for copy in made:
+            copy.start()
+        got_ref[chunk, mine] = sent_ref[chunk, mine]
+        going.append(made)
+    coming = []
+    for chunk in range(chunks):
+        for copy in going[chunk]:
+            copy.wait_recv()
+        bins_chunk(
+            place, halves, got_ref.at[chunk], go_ref, back_ref, cosine_ref[...], sine_ref[...], level_ref[chunk], answer_ref.at[chunk]
+        )
+        made = copies(
+            sizes, answer_ref.at[chunk], out_ref.at[chunk], back_sems.at[chunk], home_sems.at[chunk]
+        )
+        for copy in made:
+            copy.start()
+        out_ref[chunk, mine] = answer_ref[chunk, mine]
+        coming.append(made)
+    for made in going:
+        for copy in made:
+            copy.wait_send()
+    for made in coming:
+        for copy in made:
+            copy.wait()
+
+
+def slots_round_trip(sizes, number, starts, picks, blocks, taps, table, go, back, cosine, sine, level, model, place, halves):
     rcv, width = blocks.shape[1:]
-    samples = table.shape[1]
+    chunks, _, samples = table.shape
+    slots = starts.shape[0]
+    parts = place.size
+    bins = samples // 2 // parts // chunks
+    rows = rcv * bins
     vmem = pl.BlockSpec(memory_space=pltpu.VMEM)
     smem = pl.BlockSpec(memory_space=pltpu.SMEM)
     extra = () if model is None else (model,)
+    lanes = 2 * slots
+    back_lanes = halves * back.shape[0] // place.shape[1]
+    back_shape = (chunks, parts, rows // halves, back_lanes)
+    peers = parts - 1
     return pl.pallas_call(
-        functools.partial(analyse, model is not None),
-        out_shape=jax.ShapeDtypeStruct((parts, rcv, samples // 2 // parts, 2 * slots), jnp.bfloat16),
-        in_specs=[smem, smem, vmem, vmem, vmem] + [vmem] * len(extra),
+        functools.partial(round_trip, sizes, place, halves, model is not None),
+        out_shape=jax.ShapeDtypeStruct(back_shape, jnp.bfloat16),
+        in_specs=[smem, smem] + [vmem] * (8 + len(extra)),
         out_specs=vmem,
-        scratch_shapes=[pltpu.VMEM((slots * rcv * samples // width, width), jnp.float32)],
-    )(starts, picks, blocks, taps, table, *extra)
-
-
-def upright(spectra_ref, lines, group_lanes):
-    parts, _, bins, _ = spectra_ref.shape
+        scratch_shapes=[
+            pltpu.VMEM((slots * rcv * samples // width, width), jnp.float32),
+            pltpu.VMEM((rcv * slots, samples), jnp.bfloat16),
+            pltpu.VMEM((chunks, parts, rows, lanes), jnp.bfloat16),
+            pltpu.VMEM((chunks, parts, rows, lanes), jnp.bfloat16),
+            pltpu.VMEM(back_shape, jnp.bfloat16),
+        ]
+        + [pltpu.SemaphoreType.DMA((chunks, peers))] * 4,
+        compiler_params=pltpu.CompilerParams(collective_id=number, has_side_effects=True),
+    )(starts, picks, blocks, taps, table, go, back, cosine, sine, level, *extra)
+
+
+def upright(spectra_ref, chunk, lines, bins, group_lanes):
+    parts = spectra_ref.shape[1]
+    pack = max(1, 16 // bins)
+    count = group_lanes // 2
     pieces = []
-    for line in lines:
-        turned = spectra_ref[:, line].reshape(parts * bins, -1).astype(jnp.float32).T
-        turned = turned.astype(jnp.bfloat16)
-        count = group_lanes // 2
-        for low in range(0, turned.shape[0], group_lanes):
-            pieces.append(
-                jnp.concatenate(
-                    [turned[low : low + count], turned[low + count : low + 2 * count]], axis=1
+    for low_line in range(lines[0], lines[-1] + 1, pack):
+        block = spectra_ref[chunk, :, low_line * bins : (low_line + pack) * bins].astype(jnp.float32)
+        for line in range(pack):
+            turned = block[:, line * bins : (line + 1) * bins].reshape(parts * bins, -1).T
+            turned = turned.astype(jnp.bfloat16)
+            for low in range(0, turned.shape[0], group_lanes):
+                pieces.append(
+                    jnp.concatenate(
+                        [turned[low : low + count], turned[low + count : low + 2 * count]], axis=1
+                    )
                 )
-            )
     return jnp.concatenate(pieces, axis=0)
 
 
 def synthesise(starts_ref, picks_ref, spectra_ref, taps_ref, table_ref, model_ref, total_ref):
-    rcv, lanes = spectra_ref.shape[1], spectra_ref.shape[3]
+    chunks, parts, lines_bins, lanes = spectra_ref.shape
+    rcv = total_ref.shape[1]
+    bins = lines_bins // rcv
     slots = lanes // 2
     taps = model_ref.shape[1]
     rows = model_ref.shape[0] // slots
@@ -369,7 +516,10 @@
     together = math.gcd(rcv, 4)
     for first in range(0, rcv, together):
         lines = range(first, first + together)
-        fields = dot(upright(spectra_ref, lines, lanes), table_ref[...])
+        fields = sum(
+            dot(upright(spectra_ref, chunk, lines, bins, lanes), table_ref[chunk])
+            for chunk in range(chunks)
+        )
         for line in lines:
             low = (line - first) * slots
             for step in range(steps):
@@ -390,10 +540,10 @@
     lax.fori_loop(0, slots, one, 0, unroll=8)
 
 
-def spectra_to_slab(starts, picks, spectra, taps, table, slab_blocks):
-    _, rcv, _, lanes = spectra.shape
+def spectra_to_slab(starts, picks, spectra, taps, table, slab_blocks, rcv):
+    lanes = spectra.shape[3]
     width = taps.shape[2]
-    steps = table.shape[1] // width
+    steps = table.shape[2] // width
     vmem = pl.BlockSpec(memory_space=pltpu.VMEM)
     smem = pl.BlockSpec(memory_space=pltpu.SMEM)
     return pl.pallas_call(
@@ -407,80 +557,39 @@
     )(starts, picks, spectra, taps, table)
 
 
-def record_kernel(groups, spectra_ref, table_ref, out_ref):
+def record_kernel(groups, bins, spectra_ref, table_ref, out_ref):
+    chunks, parts, rows, lanes = spectra_ref.shape
     count = out_ref.shape[2]
-    together = spectra_ref.shape[1]
-    fields = dot(upright(spectra_ref, range(together), 2 * count), table_ref[...])
+    together = rows // bins
+    fields = sum(
+        dot(upright(spectra_ref, chunk, range(together), bins, 2 * count), table_ref[chunk])
+        for chunk in range(chunks)
+    )
     for line in range(together):
         for group in range(groups):
             low = (line * groups + group) * count
             out_ref[group, line] = fields[low : low + count]
 
 
-def records_of(spectra, table, groups):
-    parts, rcv, bins, lanes = spectra.shape
-    samples = table.shape[1]
+def records_of(spectra, table, groups, rcv):
+    chunks, parts, rows, lanes = spectra.shape
+    samples = table.shape[2]
+    bins = rows // rcv
     count = lanes // 2 // groups
     together = math.gcd(rcv, 4)
     return pl.pallas_call(
-        functools.partial(record_kernel, groups),
+        functools.partial(record_kernel, groups, bins),
         grid=(rcv // together,),
         out_shape=jax.ShapeDtypeStruct((groups, rcv, count, samples), jnp.float32),
         in_specs=[
-            pl.BlockSpec((parts, together, bins, lanes), lambda i: (0, i, 0, 0)),
-            pl.BlockSpec((samples, samples), lambda i: (0, 0)),
+            pl.BlockSpec((chunks, parts, together * bins, lanes), lambda i: (0, 0, i, 0)),
+            pl.BlockSpec(table.shape, lambda i: (0, 0, 0)),
         ],
         out_specs=pl.BlockSpec((groups, together, count, samples), lambda i: (0, i, 0, 0)),
     )(spectra, table)
 
 
-def bins_kernel(place, halves, spectra_ref, go_ref, back_ref, cosine_ref, sine_ref, level_ref, out_ref):
-    _, rcv, bins, lanes = spectra_ref.shape
-    rows = rcv * bins
-    rcv_count, slab_count = place.shape
-    joined = jnp.concatenate(
-        [
-            jnp.concatenate(
-                [spectra_ref[int(index)].reshape(rows, lanes) for index in line], axis=1
-            )
-            for line in place
-        ],
-        axis=0,
-    )
-    section = dot(joined, go_ref[...]).astype(jnp.bfloat16)
-    half = section.shape[1] // 2
-    near = dot(cosine_ref[...], section)
-    far = dot(sine_ref[...], section)
-    real = near[:, :half] + far[:, half:]
-    imag = near[:, half:] - far[:, :half]
-    level = level_ref[...]
-    factor = 1.0 - level / jnp.maximum(jnp.sqrt(real * real + imag * imag), level)
-    shrunk = jnp.concatenate([real * factor, imag * factor], axis=1).astype(jnp.bfloat16)
-    near = dot(cosine_ref[...], shrunk)
-    far = dot(sine_ref[...], shrunk)
-    section = jnp.concatenate(
-        [near[:, :half] - far[:, half:], far[:, :half] + near[:, half:]], axis=1
-    ).astype(jnp.bfloat16)
-    result = dot(section, back_ref[...], 1, 1).astype(jnp.bfloat16)
-    width = result.shape[1] // slab_count
-    for line in range(rcv_count):
-        for slab in range(slab_count):
-            piece = result[line * rows : (line + 1) * rows, slab * width : (slab + 1) * width]
-            if halves == 2:
-                piece = jnp.concatenate([piece[: rows // 2], piece[rows // 2 :]], axis=1)
-            out_ref[int(place[line, slab])] = piece.reshape(rcv // halves, bins, halves * width)
-
-
-def bins_stage(spectra, go, back, cosine, sine, level, place, halves):
-    parts, rcv, bins, _ = spectra.shape
-    width = halves * back.shape[0] // place.shape[1]
-    vmem = pl.BlockSpec(memory_space=pltpu.VMEM)
-    return pl.pallas_call(
-        functools.partial(bins_kernel, place, halves),
-        out_shape=jax.ShapeDtypeStruct((parts, rcv // halves, bins, width), jnp.bfloat16),
-        in_specs=[vmem] * 6,
-        out_specs=vmem,
-    )(spectra, go, back, cosine, sine, level)
+CHUNKS = 2
 
 
 def body_by_slots(records, offsets, filter_index, signatures, thresholds):
@@ -489,8 +598,8 @@
     slab_count = lax.axis_size(("shot", "rep"))
     rep_count = lax.axis_size("rep")
     rcv_count = lax.axis_size("rcv")
+    sizes = tuple(lax.axis_size(axis) for axis in AXES)
     parts = slab_count * rcv_count
-    everyone = ("shot", "rcv", "rep")
     tap_count = signatures.shape[1]
     slab_blocks = slab_len // tap_count
     steps = NT // tap_count
@@ -498,6 +607,8 @@
     row_count = rows_here * slab_count
     slots = row_count * capacity
     bins = NT // 2 // parts
+    chunks = CHUNKS
+    few = bins // chunks
     place = np.array(
         [
             [((slab // rep_count) * rcv_count + line) * rep_count + slab % rep_count for slab in range(slab_count)]
@@ -505,7 +616,10 @@
         ]
     )
 
-    time_table_fixed = jnp.asarray(fixed_time_table(NT).reshape(NT, NT))
+    time_table_fixed = fixed_time_table(NT).reshape(2, parts, chunks, few, NT)
+    time_table_fixed = jnp.asarray(
+        np.ascontiguousarray(time_table_fixed.transpose(2, 0, 1, 3, 4)).reshape(chunks, NT // chunks, NT)
+    )
     table_x, table_y, table_r = (
         fixed_shot_table(count) for count in (row_count, shot_count, local_rcv * rcv_count)
     )
@@ -514,7 +628,7 @@
     points = 2 * row_count * shot_count
     grid_table = jnp.asarray(grid_table.reshape(points, points))
     row_table = jnp.asarray(row_table.reshape(points, points))
-    same = np.eye(bins, dtype=np.float32)
+    same = np.eye(few, dtype=np.float32)
     cosine = jnp.asarray(np.kron(table_r[0, :, 0], same).astype(jnp.bfloat16))
     sine = jnp.asarray(np.kron(table_r[0, :, 1], same).astype(jnp.bfloat16))
 
@@ -547,31 +661,23 @@
     starts = jnp.sum(jnp.where(mine, every_start[:, None, :], 0), axis=2).reshape(-1)
     picks = jnp.sum(jnp.where(mine, every_pick[:, None, :], 0), axis=2).reshape(-1)
     adjoint_tables = toeplitz_table(signatures, True)
-
-    def correlate(blocks, rim, model):
+    bin_start = lax.axis_index(AXES) * bins
+
+    def trip(number, blocks, rim, model, back, halves):
         low = blocks.astype(jnp.bfloat16)
         extended = jnp.concatenate([low, rim, jnp.zeros_like(low[:1])], axis=0)
-        return slots_to_spectra(
-            starts, picks, extended, adjoint_tables, time_table_fixed, model, parts, slots
-        )
-
-    bin_start = lax.axis_index(everyone) * bins
-
-    def swap(value):
-        return lax.all_to_all(value, everyone, 0, 0, tiled=True)
-
-    def shrink_at(spectra, index, back, halves):
-        level = lax.dynamic_slice_in_dim(thresholds[index], bin_start, bins)
-        level = jnp.tile(level, local_rcv * rcv_count)[:, None]
-        return bins_stage(swap(spectra), slot_table, back, cosine, sine, level, place, halves)
+        level = lax.dynamic_slice_in_dim(thresholds[number], bin_start, bins).reshape(chunks, 1, few)
+        level = jnp.broadcast_to(level, (chunks, local_rcv * rcv_count, few)).reshape(chunks, -1, 1)
+        return slots_round_trip(
+            sizes, number, starts, picks, extended, adjoint_tables, time_table_fixed, slot_table, back, cosine, sine, level, model, place, halves
+        )
 
     record_blocks = records.reshape(local_rcv, slab_blocks, tap_count).transpose(1, 0, 2)
     rim = from_behind(record_blocks[: steps - 1].astype(jnp.bfloat16), ("shot", "rep"), -1)
-    spectra = shrink_at(correlate(record_blocks, rim, None), 0, slot_table, 1)
-    spectra, taps = lax.optimization_barrier((spectra, signatures))
-    forward_tables = toeplitz_table(taps, False)
+    spectra = trip(0, record_blocks, rim, None, slot_table, 1)
+    forward_tables = toeplitz_table(signatures, False)
     model, total = spectra_to_slab(
-        starts, picks, swap(spectra), forward_tables, time_table_fixed, slab_blocks
+        starts, picks, spectra, forward_tables, time_table_fixed, slab_blocks, local_rcv
     )
     spill = total[slab_blocks : slab_blocks + steps - 1]
     left = record_blocks - total[:slab_blocks]
@@ -580,8 +686,8 @@
     left = left.at[: steps - 1].add(-carried)
     rim = (ahead - spill).astype(jnp.bfloat16)
     residual = left.transpose(1, 0, 2).reshape(local_rcv, slab_len)
-    spectra = swap(shrink_at(correlate(left, rim, model), 1, row_table, 2))
-    model = records_of(spectra, time_table_fixed, 2)
+    spectra = trip(1, left, rim, model, row_table, 2)
+    model = records_of(spectra, time_table_fixed, 2, local_rcv // 2)
     return (model.reshape(rows_here, local_rcv, shot_count, NT), residual)
 
 

time: 176 us -> 149 us (0.85)
  Pallas kernels: 37.5 us -> 117 us
  waiting for transfers between devices: 80.3 us -> 1.8 us
  starting transfers between devices: 39 us -> 14.6 us
  local copies, waits for them, and re-layouts: 8.85 us -> 6.03 us
    pallas_call x5 -> x3, Pallas kernels: 26.9 us -> 106 us  [the longest x2 103 us: slots_round_trip(): pl.pallas_call(functools.partial(round_trip, sizes, place, halves, model...]
    all_to_all x4 -> x0, waiting for transfers between devices: 75.1 us -> none  [swap(): return lax.all_to_all(value, everyone, 0, 0, tiled=True)]
    all_to_all x4 -> x0, starting transfers between devices: 24.8 us -> none  [swap(): return lax.all_to_all(value, everyone, 0, 0, tiled=True)]
    unnamed x14 -> x4, local copies, waits for them, and re-layouts: 3.72 us -> 0.02 us
    all_to_all x1, waiting for transfers between devices: 2.35 us -> 0.01 us  [body_by_slots(): lax.all_to_all(jnp.broadcast_to(shots[None], (slab_count,) + shots.shape)...]
    another operation x6 -> x1, local copies, waits for them, and re-layouts: 1.85 us -> 0.01 us  [the longest x5 1.85 us: shrink_at(): level = jnp.tile(level, local_rcv * rcv_count)[:, None]]
  transfers between devices with their start and end apart: 8 -> 4, of which waited for: 7 -> 1; matrix products, arithmetic and copies ran while one was open for 5% -> 5% of each run, Pallas kernels for 2% -> 2%
where the time goes in v1:
time: 149 us; the launch traced here: 148 us
  Pallas kernels  117 us (79%)
  starting transfers between devices  14.6 us (10%)
  other arithmetic  6.91 us (5%)
  local copies, waits for them, and re-layouts  6.03 us (4%)
  waiting for transfers between devices  1.8 us (1%)
  matrix products  1.73 us (1%)
    pallas_call x2, Pallas kernels, slots_round_trip(): pl.pallas_call(functools.partial(round_trip, sizes, place, halves, model...  103 us
    ppermute x3, starting transfers between devices, from_behind(): lax.ppermute(value, axis, [(source, source + steps) for source in range(f...  8.29 us
    pallas_call x1, Pallas kernels, spectra_to_slab(): pl.pallas_call(synthesise, out_shape=(jax.ShapeDtypeStruct((lanes // 2 *...  7.13 us
    all_to_all x1, starting transfers between devices, body_by_slots(): lax.all_to_all(jnp.broadcast_to(shots[None], (slab_count,) + shots.shape)...  6.35 us
    pallas_call x2, Pallas kernels, toeplitz_table(): pl.pallas_call(functools.partial(toeplitz_kernel, adjoint), out_shape=jax...  3.41 us
  transfers between devices with their start and end apart: 4, of which 1 were waited for; matrix products, arithmetic and copies ran while one was open for 5% of the time, Pallas kernels for 2%

profile of v1, /device:TPU:0, one launch (start us, length us, event | category | flops | bytes accessed | tf_op | source)
XLA Modules:
  0.0 148.5 jit_solution(15889284724371174395)
XLA Ops:
  0.7 0.8 pad_add_fusion
  1.4 0.6 broadcast_in_dim.82
  2.1 6.4 %all-to-all-start = ((s32[8,2,1,32]{3,2,1,0:T(1,128)}), s32[8,2,1,32]{3,2,1,0:T(1,128)S(1)}, u32[]{:S(2)}, u32[]{:S(2)}) async-start(s32[8,2,1,32]{3,2,1,0:T(1,128)} %broadcast_in_dim.82), calls=%async_computation | async-start | bytes 16384 | tf_op jit(solution)/shard_map/all_to_all | solution.py:636
  8.5 1.3 collective-permute-start
  9.8 0.8 fusion.14
  10.6 1.8 %shard_map.113.taps_ref = bf16[8,256,128]{2,1,0:T(8,128)(2,1)} custom-call(bf16[8,128]{1,0:T(8,128)(2,1)} %taps_ref.3), custom_call_target="tpu_custom_call" | custom-call | tf_op jit(solution)/shard_map/pallas_call | solution.py:71
  12.4 1.6 %shard_map.115.taps_ref = bf16[8,256,128]{2,1,0:T(8,128)(2,1)} custom-call(bf16[8,128]{1,0:T(8,128)(2,1)} %taps_ref.3), custom_call_target="tpu_custom_call" | custom-call | tf_op jit(solution)/shard_map/pallas_call | solution.py:71
  14.2 0.8 reshape.290.level_ref
  15.4 1.2 select_reduce_fusion
  17.0 1.7 %fusion.1.go_ref.back_ref = bf16[1024,512]{1,0:T(8,128)(2,1)} fusion(bf16[512,512]{1,0:T(8,128)(2,1)S(1)} %copy-done.1, s32[1024]{0:T(1024)S(1)} %select_n.71), kind=kOutput, calls=%fused_computation.2 | convolution fusion | flops 537919488 | bytes 1576960 | tf_op jit(solution)/shard_map/dot_general | solution.py:262
  19.1 0.7 reshape.283.starts_ref
  20.3 1.0 maximum_maximum_fusion.blocks_ref
  21.3 57.2 %shard_map.114.spectra_ref = bf16[2,16,128,128]{3,2,1,0:T(8,128)(2,1)} custom-call(s32[64]{0:T(128)} %reshape.283.starts_ref, s32[64]{0:T(128)} %reshape.284.picks_ref, bf16[132,16,128]{2,1,0:T(8,128)(2,1)} %maximum_maximum_fusion.blocks_ref, bf16[8,256,128]{2,1,0:T(8,128)(2,1)} %shard_map.113.taps_ref, bf16[2,256,512]{2,1,0:T(8,128)(2,1)} %constant.109.clone.table_ref, ...), custom_call_target="tpu_custom_call" | custom-call | tf_op jit(solution)/shard_map/pallas_call | solution.py:472
  78.6 7.1 %shard_map.116 = (f32[4096,128]{1,0:T(8,128)}, f32[132,16,128]{2,1,0:T(8,128)}) custom-call(s32[64]{0:T(128)} %reshape.283.starts_ref, s32[64]{0:T(128)} %reshape.284.picks_ref, bf16[2,16,128,128]{3,2,1,0:T(8,128)(2,1)} %shard_map.114.spectra_ref, bf16[8,256,128]{2,1,0:T(8,128)(2,1)} %shard_map.115.taps_ref, bf16[2,256,512]{2,1,0:T(8,128)(2,1)} %constant.109.clone.table_ref), custom_call_target="tpu_custom_call" | custom-call | tf_op jit(solution)/shard_map/pallas_call | solution.py:549
  85.7 1.3 fusion.2
  87.0 1.3 collective-permute-start.2
  88.3 1.8 %collective-permute-done.2 = f32[3,16,128]{2,1,0:T(8,128)S(1)} collective-permute-done((f32[3,16,128]{2,1,0:T(8,128)S(1)}, f32[3,16,128]{2,1,0:T(8,128)S(1)}, u32[]{:S(2)}, u32[]{:S(2)}) %collective-permute-start.2) | collective-permute-done | bytes 24608 | tf_op jit(solution)/shard_map/ppermute | solution.py:18
  90.1 0.7 fusion.12
  90.9 5.7 %collective-permute-start.1 = (f32[3,16,128]{2,1,0:T(8,128)S(1)}, f32[3,16,128]{2,1,0:T(8,128)S(1)}, u32[]{:S(2)}, u32[]{:S(2)}) collective-permute-start(f32[3,16,128]{2,1,0:T(8,128)S(1)} %get-tuple-element.22), channel_id=1, source_target_pairs={{0,1},{1,4},{4,5},{5,8},{8,9},{9,12},{12,13},{2,3},{3,6},{6,7},{7,... | collective-permute-start | bytes 73736 | tf_op jit(solution)/shard_map/ppermute | solution.py:18
  96.7 0.8 reshape.291.level_ref
  97.6 1.0 copy_bitcast_fusion
  98.6 1.0 maximum_maximum_fusion.1.blocks_ref
  99.7 46.1 %shard_map.117.spectra_ref = bf16[2,16,64,128]{3,2,1,0:T(8,128)(2,1)} custom-call(s32[64]{0:T(128)} %reshape.283.starts_ref, s32[64]{0:T(128)} %reshape.284.picks_ref, bf16[132,16,128]{2,1,0:T(8,128)(2,1)} %maximum_maximum_fusion.1.blocks_ref, bf16[8,256,128]{2,1,0:T(8,128)(2,1)} %shard_map.113.taps_ref, bf16[2,256,512]{2,1,0:T(8,128)(2,1)} %constant.109.clone.table_ref, ...), custom_call_target="tpu_custom_call" | custom-call | tf_op jit(solution)/shard_map/pallas_call | solution.py:472
  145.7 2.7 %shard_map.118 = f32[2,8,32,512]{3,2,1,0:T(8,128)} custom-call(bf16[2,16,64,128]{3,2,1,0:T(8,128)(2,1)} %shard_map.117.spectra_ref, bf16[2,256,512]{2,1,0:T(8,128)(2,1)} %constant.109.clone.table_ref), custom_call_target="tpu_custom_call" | custom-call | tf_op jit(solution)/shard_map/pallas_call | solution.py:580
  (34 shorter events, 2.1 us)
Async XLA Ops:
  0.6 7.8 %copy-start = (f32[16,16384]{1,0:T(8,128)S(1)}, f32[16,16384]{1,0:T(8,128)}, u32[]{:S(2)}) copy-start(f32[16,16384]{1,0:T(8,128)} %param.12) | copy-start | bytes 3145732
  0.6 16.3 %copy-start.1 = (bf16[512,512]{1,0:T(8,128)(2,1)S(1)}, bf16[512,512]{1,0:T(8,128)(2,1)}, u32[]{:S(2)}) copy-start(bf16[512,512]{1,0:T(8,128)(2,1)} %constant.110.clone) | copy-start | bytes 1572868
  2.1 13.0 %all-to-all-start = ((s32[8,2,1,32]{3,2,1,0:T(1,128)}), s32[8,2,1,32]{3,2,1,0:T(1,128)S(1)}, u32[]{:S(2)}, u32[]{:S(2)}) async-start(s32[8,2,1,32]{3,2,1,0:T(1,128)} %broadcast_in_dim.82), calls=%async_computation | async-start | bytes 16384 | tf_op jit(solution)/shard_map/all_to_all | solution.py:636
  8.5 11.8 %collective-permute-start = (bf16[3,16,128]{2,1,0:T(8,128)(2,1)S(1)}, bf16[3,16,128]{2,1,0:T(8,128)(2,1)S(1)}, u32[]{:S(2)}, u32[]{:S(2)}) collective-permute-start(bf16[3,16,128]{2,1,0:T(8,128)(2,1)S(1)} %slice.57), channel_id=1, source_target_pairs={{1,0},{4,1},{5,4},{8,5},{9,8},{12,9},{13,12},{3,2},{6,3},{7,6},{10... | collective-permute-start | bytes 36872 | tf_op jit(solution)/shard_map/ppermute | solution.py:18
  87.0 3.1 %collective-permute-start.2 = (f32[3,16,128]{2,1,0:T(8,128)S(1)}, f32[3,16,128]{2,1,0:T(8,128)S(1)}, u32[]{:S(2)}, u32[]{:S(2)}) collective-permute-start(f32[3,16,128]{2,1,0:T(8,128)S(1)} %slice.58), channel_id=1, source_target_pairs={{1,0},{4,1},{5,4},{8,5},{9,8},{12,9},{13,12},{3,2},{6,3},{7,6},{10... | collective-permute-start | bytes 73736 | tf_op jit(solution)/shard_map/ppermute | solution.py:18
  90.9 6.7 %collective-permute-start.1 = (f32[3,16,128]{2,1,0:T(8,128)S(1)}, f32[3,16,128]{2,1,0:T(8,128)S(1)}, u32[]{:S(2)}, u32[]{:S(2)}) collective-permute-start(f32[3,16,128]{2,1,0:T(8,128)S(1)} %get-tuple-element.22), channel_id=1, source_target_pairs={{0,1},{1,4},{4,5},{5,8},{8,9},{9,12},{12,13},{2,3},{3,6},{6,7},{7,... | collective-permute-start | bytes 73736 | tf_op jit(solution)/shard_map/ppermute | solution.py:18

commit v2 on v1

--- a/solution.py
+++ b/solution.py
@@ -301,72 +301,66 @@
     return dict(zip(AXES, spot)), index
 
 
-def greet(sizes):
-    barrier = pltpu.get_barrier_semaphore()
-    steps = neighbours(sizes)
-    for step in steps:
-        pl.semaphore_signal(barrier, inc=1, device_id=device_at(sizes, step)[0], device_id_type=MESH)
-    pl.semaphore_wait(barrier, len(steps))
-
-
-def copies(sizes, source, target, send_sem, recv_sem):
-    mine = device_at(sizes, (0, 0, 0))[1]
-    made = []
-    for number, step in enumerate(neighbours(sizes)):
-        device, index = device_at(sizes, step)
-        made.append(
-            pltpu.make_async_remote_copy(
-                src_ref=source.at[index],
-                dst_ref=target.at[mine],
-                send_sem=send_sem.at[number],
-                recv_sem=recv_sem.at[number],
-                device_id=device,
-                device_id_type=MESH,
-            )
-        )
-    return made
-
-
-def correlate_slots(starts_ref, picks_ref, blocks_ref, taps_ref, model_ref, held_ref):
-    rcv, taps = blocks_ref.shape[1:]
-    slots = starts_ref.shape[0]
-    rows = held_ref.shape[0] // slots
-    steps = rows // rcv
-
-    def one(slot, carry):
-        window = blocks_ref[pl.ds(starts_ref[slot], steps)].reshape(rows, taps)
-        later = jnp.concatenate([window[rcv:], jnp.zeros((rcv, taps), window.dtype)], axis=0)
-        pair = jnp.concatenate([window, later], axis=1)
-        terms = dot(pair, taps_ref[picks_ref[slot]])
-        where = pl.ds(pl.multiple_of(slot * rows, rows), rows)
-        if model_ref is not None:
-            terms = terms + model_ref[where]
-        held_ref[where] = terms
-        return carry
-
-    lax.fori_loop(0, slots, one, 0, unroll=8)
-
-
-def gather_traces(held_ref, traces_ref, rcv, slots):
-    rows = held_ref.shape[0] // slots
-    steps = rows // rcv
-    for line in range(rcv):
-        traces_ref[line * slots : (line + 1) * slots] = jnp.concatenate(
-            [
-                held_ref[pl.ds(step * rcv + line, slots, stride=rows), :].astype(jnp.bfloat16)
-                for step in range(steps)
-            ],
-            axis=1,
-        )
-
-
-def spectra_chunk(table, traces_ref, out_ref, rcv, slots):
+def build_taps(signature_ref, adjoint, out_ref):
+    count, taps = signature_ref.shape
+    row_index = lax.broadcasted_iota(jnp.int32, (taps, taps), 0)
+    col_index = lax.broadcasted_iota(jnp.int32, (taps, taps), 1)
+    values = signature_ref[...].astype(jnp.float32)
+    for index in range(count):
+        row = jnp.broadcast_to(values[index : index + 1, :], (taps, taps))
+        turned = pltpu.roll(row, 0, 1, stride=1, stride_axis=0)
+        zeros = jnp.zeros_like(turned)
+        near = jnp.where(col_index >= row_index, turned, zeros)
+        far = jnp.where(col_index < row_index, turned, zeros)
+        near, far = (near.T, far.T) if adjoint else (near, far)
+        where = slice(index * taps, (index + 1) * taps)
+        out_ref[:taps, where] = near.astype(jnp.bfloat16)
+        out_ref[taps:, where] = far.astype(jnp.bfloat16)
+
+
+def pick_signature(every, picks_ref):
+    slots, width = picks_ref.shape
+    picks = jnp.concatenate([picks_ref[...]] * (every.shape[0] // slots), axis=0)
+    chosen = every[:, :width]
+    for index in range(1, every.shape[1] // width):
+        chosen = jnp.where(picks == index, every[:, index * width : (index + 1) * width], chosen)
+    return chosen
+
+
+def correlate_line(line, select_ref, blocks_ref, taps_ref, picks_ref, field_ref, traces_ref):
+    slots, width = picks_ref.shape
+    window = dot(select_ref[...], blocks_ref[line]).astype(jnp.bfloat16)
+    later = jnp.concatenate([window[slots:], jnp.zeros((slots, width), window.dtype)], axis=0)
+    terms = pick_signature(dot(jnp.concatenate([window, later], axis=1), taps_ref[...]), picks_ref)
+    steps = terms.shape[0] // slots
+    terms = jnp.concatenate(
+        [terms[step * slots : (step + 1) * slots] for step in range(steps)], axis=1
+    )
+    where = pl.ds(pl.multiple_of(line * slots, slots), slots)
+    if field_ref is not None:
+        terms = terms + field_ref[where]
+    traces_ref[where] = terms.astype(jnp.bfloat16)
+
+
+def blend_line(line, place_ref, field_ref, taps_ref, picks_ref):
+    slots, width = picks_ref.shape
+    trace = field_ref[pl.ds(pl.multiple_of(line * slots, slots), slots)].astype(jnp.bfloat16)
+    steps = trace.shape[1] // width
+    stacked = jnp.concatenate(
+        [trace[:, step * width : (step + 1) * width] for step in range(steps)], axis=0
+    )
+    earlier = jnp.concatenate([jnp.zeros((slots, width), trace.dtype), stacked[:-slots]], axis=0)
+    shots = pick_signature(dot(jnp.concatenate([stacked, earlier], axis=1), taps_ref[...]), picks_ref)
+    return dot(place_ref[...], shots.astype(jnp.bfloat16))
+
+
+def spectra_chunk(table, traces_ref, out_ref, lines, rcv, slots):
     parts, rows, lanes = out_ref.shape
     bins = rows // rcv
     half = parts * bins
     pack = max(1, 16 // bins)
-    together = math.gcd(rcv, 4)
-    for first in range(0, rcv, together):
+    together = math.gcd(len(lines), 4)
+    for first in range(lines[0], lines[-1] + 1, together):
         both = dot(table, traces_ref[first * slots : (first + together) * slots], 1, 1)
         for low in range(0, together, pack):
             pieces = []
@@ -412,78 +406,13 @@
             out_ref[int(place[line, slab])] = piece
 
 
-def round_trip(sizes, place, halves, with_model, starts_ref, picks_ref, blocks_ref, taps_ref, table_ref, go_ref, back_ref, cosine_ref, sine_ref, level_ref, *rest):
-    model_ref = rest[0] if with_model else None
-    out_ref, held_ref, traces_ref, sent_ref, got_ref, answer_ref = rest[-10:-4]
-    send_sems, recv_sems, back_sems, home_sems = rest[-4:]
-    rcv = blocks_ref.shape[1]
-    slots = starts_ref.shape[0]
-    chunks = table_ref.shape[0]
-    greet(sizes)
-    mine = device_at(sizes, (0, 0, 0))[1]
-    correlate_slots(starts_ref, picks_ref, blocks_ref, taps_ref, model_ref, held_ref)
-    gather_traces(held_ref, traces_ref, rcv, slots)
-    going = []
-    for chunk in range(chunks):
-        spectra_chunk(table_ref[chunk], traces_ref, sent_ref.at[chunk], rcv, slots)
-        made = copies(
-            sizes, sent_ref.at[chunk], got_ref.at[chunk], send_sems.at[chunk], recv_sems.at[chunk]
-        )
-        for copy in made:
-            copy.start()
-        got_ref[chunk, mine] = sent_ref[chunk, mine]
-        going.append(made)
-    coming = []
-    for chunk in range(chunks):
-        for copy in going[chunk]:
-            copy.wait_recv()
-        bins_chunk(
-            place, halves, got_ref.at[chunk], go_ref, back_ref, cosine_ref[...], sine_ref[...], level_ref[chunk], answer_ref.at[chunk]
-        )
-        made = copies(
-            sizes, answer_ref.at[chunk], out_ref.at[chunk], back_sems.at[chunk], home_sems.at[chunk]
-        )
-        for copy in made:
-            copy.start()
-        out_ref[chunk, mine] = answer_ref[chunk, mine]
-        coming.append(made)
-    for made in going:
-        for copy in made:
-            copy.wait_send()
-    for made in coming:
-        for copy in made:
-            copy.wait()
-
-
-def slots_round_trip(sizes, number, starts, picks, blocks, taps, table, go, back, cosine, sine, level, model, place, halves):
-    rcv, width = blocks.shape[1:]
-    chunks, _, samples = table.shape
-    slots = starts.shape[0]
-    parts = place.size
-    bins = samples // 2 // parts // chunks
-    rows = rcv * bins
-    vmem = pl.BlockSpec(memory_space=pltpu.VMEM)
-    smem = pl.BlockSpec(memory_space=pltpu.SMEM)
-    extra = () if model is None else (model,)
-    lanes = 2 * slots
-    back_lanes = halves * back.shape[0] // place.shape[1]
-    back_shape = (chunks, parts, rows // halves, back_lanes)
-    peers = parts - 1
-    return pl.pallas_call(
-        functools.partial(round_trip, sizes, place, halves, model is not None),
-        out_shape=jax.ShapeDtypeStruct(back_shape, jnp.bfloat16),
-        in_specs=[smem, smem] + [vmem] * (8 + len(extra)),
-        out_specs=vmem,
-        scratch_shapes=[
-            pltpu.VMEM((slots * rcv * samples // width, width), jnp.float32),
-            pltpu.VMEM((rcv * slots, samples), jnp.bfloat16),
-            pltpu.VMEM((chunks, parts, rows, lanes), jnp.bfloat16),
-            pltpu.VMEM((chunks, parts, rows, lanes), jnp.bfloat16),
-            pltpu.VMEM(back_shape, jnp.bfloat16),
-        ]
-        + [pltpu.SemaphoreType.DMA((chunks, peers))] * 4,
-        compiler_params=pltpu.CompilerParams(collective_id=number, has_side_effects=True),
-    )(starts, picks, blocks, taps, table, go, back, cosine, sine, level, *extra)
+def level_of(levels_ref, index, first, bins, copies_of):
+    width = levels_ref.shape[1]
+    lane = lax.broadcasted_iota(jnp.int32, (bins, width), 1)
+    row = lax.broadcasted_iota(jnp.int32, (bins, width), 0)
+    values = jnp.broadcast_to(levels_ref[index : index + 1, :], (bins, width))
+    column = jnp.sum(jnp.where(lane == row + first, values, 0.0), axis=1, keepdims=True)
+    return jnp.concatenate([column] * copies_of, axis=0)
 
 
 def upright(spectra_ref, chunk, lines, bins, group_lanes):
@@ -505,91 +434,272 @@
     return jnp.concatenate(pieces, axis=0)
 
 
-def synthesise(starts_ref, picks_ref, spectra_ref, taps_ref, table_ref, model_ref, total_ref):
-    chunks, parts, lines_bins, lanes = spectra_ref.shape
-    rcv = total_ref.shape[1]
-    bins = lines_bins // rcv
-    slots = lanes // 2
-    taps = model_ref.shape[1]
-    rows = model_ref.shape[0] // slots
-    steps = rows // rcv
-    together = math.gcd(rcv, 4)
-    for first in range(0, rcv, together):
-        lines = range(first, first + together)
-        fields = sum(
-            dot(upright(spectra_ref, chunk, lines, bins, lanes), table_ref[chunk])
-            for chunk in range(chunks)
-        )
-        for line in lines:
-            low = (line - first) * slots
-            for step in range(steps):
-                model_ref[pl.ds(step * rcv + line, slots, stride=rows), :] = fields[
-                    low : low + slots, step * taps : (step + 1) * taps
-                ]
-    total_ref[...] = jnp.zeros_like(total_ref)
-
-    def one(slot, carry):
-        trace = model_ref[pl.ds(pl.multiple_of(slot * rows, rows), rows)].astype(jnp.bfloat16)
-        earlier = jnp.concatenate([jnp.zeros((rcv, taps), trace.dtype), trace[:-rcv]], axis=0)
-        pair = jnp.concatenate([trace, earlier], axis=1)
-        shot = dot(pair, taps_ref[picks_ref[slot]]).astype(jnp.bfloat16).astype(jnp.float32)
-        where = pl.ds(starts_ref[slot], steps)
-        total_ref[where] = total_ref[where] + shot.reshape(steps, rcv, taps)
-        return carry
-
-    lax.fori_loop(0, slots, one, 0, unroll=8)
-
-
-def spectra_to_slab(starts, picks, spectra, taps, table, slab_blocks, rcv):
-    lanes = spectra.shape[3]
-    width = taps.shape[2]
-    steps = table.shape[2] // width
-    vmem = pl.BlockSpec(memory_space=pltpu.VMEM)
-    smem = pl.BlockSpec(memory_space=pltpu.SMEM)
-    return pl.pallas_call(
-        synthesise,
-        out_shape=(
-            jax.ShapeDtypeStruct((lanes // 2 * rcv * steps, width), jnp.float32),
-            jax.ShapeDtypeStruct((slab_blocks + steps, rcv, width), jnp.float32),
-        ),
-        in_specs=[smem, smem, vmem, vmem, vmem],
-        out_specs=(vmem, vmem),
-    )(starts, picks, spectra, taps, table)
-
-
-def record_kernel(groups, bins, spectra_ref, table_ref, out_ref):
-    chunks, parts, rows, lanes = spectra_ref.shape
-    count = out_ref.shape[2]
-    together = rows // bins
-    fields = sum(
-        dot(upright(spectra_ref, chunk, range(together), bins, 2 * count), table_ref[chunk])
-        for chunk in range(chunks)
-    )
-    for line in range(together):
-        for group in range(groups):
-            low = (line * groups + group) * count
-            out_ref[group, line] = fields[low : low + count]
-
-
-def records_of(spectra, table, groups, rcv):
-    chunks, parts, rows, lanes = spectra.shape
-    samples = table.shape[2]
-    bins = rows // rcv
-    count = lanes // 2 // groups
-    together = math.gcd(rcv, 4)
-    return pl.pallas_call(
-        functools.partial(record_kernel, groups, bins),
-        grid=(rcv // together,),
-        out_shape=jax.ShapeDtypeStruct((groups, rcv, count, samples), jnp.float32),
-        in_specs=[
-            pl.BlockSpec((chunks, parts, together * bins, lanes), lambda i: (0, 0, i, 0)),
-            pl.BlockSpec(table.shape, lambda i: (0, 0, 0)),
-        ],
-        out_specs=pl.BlockSpec((groups, together, count, samples), lambda i: (0, i, 0, 0)),
-    )(spectra, table)
-
-
+HALVES = 2
 CHUNKS = 2
+
+
+def whole_kernel(
+    sizes,
+    place,
+    starts_ref,
+    picks_ref,
+    records_ref,
+    blocks_ref,
+    signatures_ref,
+    levels_ref,
+    table_ref,
+    slot_table_ref,
+    row_table_ref,
+    cosine_ref,
+    sine_ref,
+    model_ref,
+    left_ref,
+    adjoint_ref,
+    forward_ref,
+    select_ref,
+    place_ref,
+    traces_ref,
+    field_ref,
+    rest_ref,
+    head_ref,
+    spill_ref,
+    carried_ref,
+    ahead_ref,
+    sent_ref,
+    got_ref,
+    answer_ref,
+    home_ref,
+    reply_ref,
+    final_ref,
+    go_sends,
+    go_recvs,
+    back_sends,
+    back_recvs,
+    rim_sends,
+    rim_recvs,
+):
+    slots, width = picks_ref.shape
+    rcv, padded, _ = blocks_ref.shape
+    blocks = records_ref.shape[1]
+    chunks = table_ref.shape[0]
+    samples = table_ref.shape[2]
+    steps = samples // width
+    parts = place.size
+    few = samples // 2 // parts // chunks
+    lines_in_half = rcv // HALVES
+    rows_in_half = lines_in_half * few
+    edge = head_ref.shape[1]
+    all_rcv = rcv * place.shape[0]
+    halves = [range(half * lines_in_half, (half + 1) * lines_in_half) for half in range(HALVES)]
+
+    barrier = pltpu.get_barrier_semaphore()
+    hops = neighbours(sizes)
+    for hop in hops:
+        pl.semaphore_signal(barrier, inc=1, device_id=device_at(sizes, hop)[0], device_id_type=MESH)
+    mine = device_at(sizes, (0, 0, 0))[1]
+    slab = lax.axis_index("shot") * sizes[2] + lax.axis_index("rep")
+    last_slab = sizes[0] * sizes[2] - 1
+
+    def slab_device(shift):
+        other = lax.rem(slab + shift + last_slab + 1, last_slab + 1)
+        return {
+            "shot": other // sizes[2],
+            "rcv": lax.axis_index("rcv"),
+            "rep": lax.rem(other, sizes[2]),
+        }
+
+    build_taps(signatures_ref, True, adjoint_ref)
+    block_index = lax.broadcasted_iota(jnp.int32, (slots, padded), 1)
+    first_block = jnp.broadcast_to(starts_ref[:, :1], (slots, padded))
+    select = jnp.concatenate(
+        [(block_index == first_block + step).astype(jnp.float32) for step in range(steps)], axis=0
+    )
+    select_ref[...] = select.astype(jnp.bfloat16)
+    place_ref[...] = select.T.astype(jnp.bfloat16)
+    pl.semaphore_wait(barrier, len(hops))
+
+    def exchange(source, target, send_sems, recv_sems, low, rows):
+        made = []
+        where = pl.ds(low, rows)
+        for number, hop in enumerate(hops):
+            device, index = device_at(sizes, hop)
+            copy = pltpu.make_async_remote_copy(
+                src_ref=source.at[index, where],
+                dst_ref=target.at[mine, where],
+                send_sem=send_sems.at[number],
+                recv_sem=recv_sems.at[number],
+                device_id=device,
+                device_id_type=MESH,
+            )
+            copy.start()
+            made.append(copy)
+        target[mine, where] = source[mine, where]
+        return made
+
+    def send_half(half, from_ref, model):
+        def one(line, carry):
+            correlate_line(line, select_ref, from_ref, adjoint_ref, picks_ref, model, traces_ref)
+            return carry
+
+        lax.fori_loop(half * lines_in_half, (half + 1) * lines_in_half, one, 0)
+        made = []
+        for chunk in range(chunks):
+            spectra_chunk(
+                table_ref[chunk], traces_ref, sent_ref.at[chunk], halves[half], rcv, slots
+            )
+            made.append(
+                exchange(
+                    sent_ref.at[chunk],
+                    got_ref.at[chunk],
+                    go_sends.at[half, chunk],
+                    go_recvs.at[half, chunk],
+                    half * rows_in_half,
+                    rows_in_half,
+                )
+            )
+        return made
+
+    def level(index, chunk):
+        return level_of(levels_ref, index, (mine * chunks + chunk) * few, few, all_rcv)
+
+    going = [send_half(half, blocks_ref, None) for half in range(HALVES)]
+    build_taps(signatures_ref, False, forward_ref)
+    coming = {}
+    for chunk in range(chunks):
+        for half in range(HALVES):
+            for copy in going[half][chunk]:
+                copy.wait_recv()
+        bins_chunk(
+            place, 1, got_ref.at[chunk], slot_table_ref, slot_table_ref, cosine_ref[...], sine_ref[...], level(0, chunk), answer_ref.at[chunk]
+        )
+        coming[0, chunk] = exchange(
+            answer_ref.at[chunk], home_ref.at[chunk], back_sends.at[0, chunk], back_recvs.at[0, chunk], 0, rows_in_half
+        )
+    for half in range(1, HALVES):
+        for chunk in range(chunks):
+            coming[half, chunk] = exchange(
+                answer_ref.at[chunk],
+                home_ref.at[chunk],
+                back_sends.at[half, chunk],
+                back_recvs.at[half, chunk],
+                half * rows_in_half,
+                rows_in_half,
+            )
+    for made in going:
+        for chunk in made:
+            for copy in chunk:
+                copy.wait_send()
+
+    again = []
+    for half in range(HALVES):
+        low, high = half * lines_in_half, (half + 1) * lines_in_half
+        for chunk in range(chunks):
+            for copy in coming[half, chunk]:
+                copy.wait_recv()
+        together = math.gcd(lines_in_half, 4)
+        for first in range(low, high, together):
+            lines = range(first, first + together)
+            field_ref[first * slots : (first + together) * slots] = sum(
+                dot(upright(home_ref, chunk, lines, few, 2 * slots), table_ref[chunk])
+                for chunk in range(chunks)
+            )
+
+        def one(line, carry):
+            blended = blend_line(line, place_ref, field_ref, forward_ref, picks_ref)
+            left = records_ref[line] - blended[:blocks]
+            left_ref[line] = left
+            head_ref[line] = left[:edge]
+            spill_ref[line] = blended[blocks : blocks + edge]
+            return carry
+
+        lax.fori_loop(low, high, one, 0)
+        where = pl.ds(low, lines_in_half)
+        onward = pltpu.make_async_remote_copy(
+            src_ref=spill_ref.at[where],
+            dst_ref=carried_ref.at[where],
+            send_sem=rim_sends.at[half, 0],
+            recv_sem=rim_recvs.at[half, 0],
+            device_id=slab_device(1),
+            device_id_type=MESH,
+        )
+        backward = pltpu.make_async_remote_copy(
+            src_ref=head_ref.at[where],
+            dst_ref=ahead_ref.at[where],
+            send_sem=rim_sends.at[half, 1],
+            recv_sem=rim_recvs.at[half, 1],
+            device_id=slab_device(-1),
+            device_id_type=MESH,
+        )
+
+        @pl.when(slab < last_slab)
+        def _():
+            onward.start()
+
+        @pl.when(slab > 0)
+        def _():
+            backward.start()
+            onward.wait_recv()
+            left_ref[where, :edge] = left_ref[where, :edge] - carried_ref[where]
+
+        rest_ref[where, :blocks] = left_ref[where].astype(jnp.bfloat16)
+        rest_ref[where, blocks:] = jnp.zeros(
+            (lines_in_half, padded - blocks, width), jnp.bfloat16
+        )
+
+        @pl.when(slab < last_slab)
+        def _():
+            backward.wait_recv()
+            rim = ahead_ref[where] - spill_ref[where]
+            rim = jnp.concatenate(
+                [rim, jnp.zeros((lines_in_half, padded - blocks - edge, width), jnp.float32)], axis=1
+            )
+            rest_ref[where, blocks:] = rim.astype(jnp.bfloat16)
+            onward.wait_send()
+
+        @pl.when(slab > 0)
+        def _():
+            backward.wait_send()
+
+        again.append(send_half(half, rest_ref, field_ref))
+
+    for half in range(HALVES):
+        for chunk in range(chunks):
+            for copy in coming[half, chunk]:
+                copy.wait_send()
+    final = []
+    for chunk in range(chunks):
+        for half in range(HALVES):
+            for copy in again[half][chunk]:
+                copy.wait_recv()
+        bins_chunk(
+            place, 2, got_ref.at[chunk], slot_table_ref, row_table_ref, cosine_ref[...], sine_ref[...], level(1, chunk), reply_ref.at[chunk]
+        )
+        final.append(
+            exchange(
+                reply_ref.at[chunk], final_ref.at[chunk], back_sends.at[0, chunk], back_recvs.at[0, chunk], 0, reply_ref.shape[2]
+            )
+        )
+    for made in again:
+        for chunk in made:
+            for copy in chunk:
+                copy.wait_send()
+    groups, lines_there, count, _ = model_ref.shape
+    together = math.gcd(lines_there, 4)
+    for chunk in range(chunks):
+        for copy in final[chunk]:
+            copy.wait()
+        for first in range(0, lines_there, together):
+            fields = dot(
+                upright(final_ref, chunk, range(first, first + together), few, 2 * count),
+                table_ref[chunk],
+            )
+            for line in range(together):
+                for group in range(groups):
+                    low = (line * groups + group) * count
+                    piece = fields[low : low + count]
+                    if chunk:
+                        piece = piece + model_ref[group, first + line]
+                    model_ref[group, first + line] = piece
 
 
 def body_by_slots(records, offsets, filter_index, signatures, thresholds):
@@ -658,37 +768,55 @@
         every_rank[:, None, :] == ranks[None, :, None]
     )
     every_start = every_offset // tap_count % slab_blocks
-    starts = jnp.sum(jnp.where(mine, every_start[:, None, :], 0), axis=2).reshape(-1)
+    starts = jnp.sum(jnp.where(mine, every_start[:, None, :] + 1, 0), axis=2).reshape(-1)
+    starts = jnp.where(starts > 0, starts - 1, -NT)
     picks = jnp.sum(jnp.where(mine, every_pick[:, None, :], 0), axis=2).reshape(-1)
-    adjoint_tables = toeplitz_table(signatures, True)
-    bin_start = lax.axis_index(AXES) * bins
-
-    def trip(number, blocks, rim, model, back, halves):
-        low = blocks.astype(jnp.bfloat16)
-        extended = jnp.concatenate([low, rim, jnp.zeros_like(low[:1])], axis=0)
-        level = lax.dynamic_slice_in_dim(thresholds[number], bin_start, bins).reshape(chunks, 1, few)
-        level = jnp.broadcast_to(level, (chunks, local_rcv * rcv_count, few)).reshape(chunks, -1, 1)
-        return slots_round_trip(
-            sizes, number, starts, picks, extended, adjoint_tables, time_table_fixed, slot_table, back, cosine, sine, level, model, place, halves
-        )
-
-    record_blocks = records.reshape(local_rcv, slab_blocks, tap_count).transpose(1, 0, 2)
-    rim = from_behind(record_blocks[: steps - 1].astype(jnp.bfloat16), ("shot", "rep"), -1)
-    spectra = trip(0, record_blocks, rim, None, slot_table, 1)
-    forward_tables = toeplitz_table(signatures, False)
-    model, total = spectra_to_slab(
-        starts, picks, spectra, forward_tables, time_table_fixed, slab_blocks, local_rcv
-    )
-    spill = total[slab_blocks : slab_blocks + steps - 1]
-    left = record_blocks - total[:slab_blocks]
-    carried = from_behind(spill, ("shot", "rep"), 1)
-    ahead = from_behind(left[: steps - 1], ("shot", "rep"), -1)
-    left = left.at[: steps - 1].add(-carried)
-    rim = (ahead - spill).astype(jnp.bfloat16)
-    residual = left.transpose(1, 0, 2).reshape(local_rcv, slab_len)
-    spectra = trip(1, left, rim, model, row_table, 2)
-    model = records_of(spectra, time_table_fixed, 2, local_rcv // 2)
-    return (model.reshape(rows_here, local_rcv, shot_count, NT), residual)
+    starts = jnp.broadcast_to(starts[:, None], (slots, tap_count))
+    picks = jnp.broadcast_to(picks[:, None], (slots, tap_count))
+
+    edge = 8
+    padded = slab_blocks + 2 * edge
+    record_blocks = records.reshape(local_rcv, slab_blocks, tap_count)
+    rim = from_behind(
+        record_blocks[:, :edge].astype(jnp.bfloat16), ("shot", "rep"), -1
+    )
+    extended = jnp.concatenate(
+        [record_blocks.astype(jnp.bfloat16), rim, jnp.zeros_like(rim)], axis=1
+    )
+    vmem = pl.BlockSpec(memory_space=pltpu.VMEM)
+    rows = local_rcv * few
+    table_width = tap_count * signatures.shape[0]
+    low, wide = jnp.bfloat16, jnp.float32
+    model, residual = pl.pallas_call(
+        functools.partial(whole_kernel, sizes, place),
+        out_shape=(
+            jax.ShapeDtypeStruct((2, local_rcv // 2, shot_count, NT), wide),
+            jax.ShapeDtypeStruct(record_blocks.shape, wide),
+        ),
+        in_specs=[vmem] * 11,
+        out_specs=(vmem, vmem),
+        scratch_shapes=[
+            pltpu.VMEM((2 * tap_count, table_width), low),
+            pltpu.VMEM((2 * tap_count, table_width), low),
+            pltpu.VMEM((slots * steps, padded), low),
+            pltpu.VMEM((padded, slots * steps), low),
+            pltpu.VMEM((local_rcv * slots, NT), low),
+            pltpu.VMEM((local_rcv * slots, NT), wide),
+            pltpu.VMEM(extended.shape, low),
+        ]
+        + [pltpu.VMEM((local_rcv, edge, tap_count), wide)] * 4
+        + [pltpu.VMEM((chunks, parts, rows, 2 * slots), low)] * 4
+        + [pltpu.VMEM((chunks, parts, rows // 2, 4 * shot_count), low)] * 2
+        + [pltpu.SemaphoreType.DMA((HALVES, chunks, parts - 1))] * 4
+        + [pltpu.SemaphoreType.DMA((HALVES, 2))] * 2,
+        compiler_params=pltpu.CompilerParams(collective_id=0, has_side_effects=True),
+    )(
+        starts, picks, record_blocks, extended, signatures, thresholds, time_table_fixed, slot_table, row_table, cosine, sine
+    )
+    return (
+        model.reshape(rows_here, local_rcv, shot_count, NT),
+        residual.reshape(local_rcv, slab_len),
+    )
 
 
 def body(records, offsets, filter_index, signatures, thresholds):

time: 149 us -> 124 us (0.83)
  Pallas kernels: 117 us -> 99.2 us
  starting transfers between devices: 14.6 us -> 7.78 us
  other arithmetic: 6.91 us -> 3.72 us
  local copies, waits for them, and re-layouts: 6.03 us -> 7.76 us
    pallas_call x6 -> x1, Pallas kernels: 117 us -> 99.2 us  [body_by_slots(): pl.pallas_call(functools.partial(whole_kernel, sizes, place), out_shape=(...]
    ppermute x3 -> x1, starting transfers between devices: 8.29 us -> 1.42 us  [from_behind(): lax.ppermute(value, axis, [(source, source + steps) for source in range(f...]
    unnamed x4 -> x9, local copies, waits for them, and re-layouts: 0.02 us -> 5.31 us
    reshape x5 -> x0, local copies, waits for them, and re-layouts: 3.98 us -> none  [the longest x2 1.68 us: trip(): jnp.broadcast_to(level, (chunks, local_rcv * rcv_count, few))]
    all_to_all x1, waiting for transfers between devices: 0.01 us -> 2.5 us  [body_by_slots(): lax.all_to_all(jnp.broadcast_to(shots[None], (slab_count,) + shots.shape)...]
    ppermute x3 -> x1, waiting for transfers between devices: 1.79 us -> 0.01 us  [from_behind(): lax.ppermute(value, axis, [(source, source + steps) for source in range(f...]
  transfers between devices with their start and end apart: 4 -> 2, of which waited for: 1 -> 1; matrix products, arithmetic and copies ran while one was open for 5% -> 5% of each run, Pallas kernels for 2% -> 0%
where the time goes in v2:
time: 124 us; the launch traced here: 123 us
  Pallas kernels  99.2 us (80%)
  starting transfers between devices  7.78 us (6%)
  local copies, waits for them, and re-layouts  7.76 us (6%)
  other arithmetic  3.72 us (3%)
  waiting for transfers between devices  2.5 us (2%)
  matrix products  1.73 us (1%)
    pallas_call x1, Pallas kernels, body_by_slots(): pl.pallas_call(functools.partial(whole_kernel, sizes, place), out_shape=(...  99.2 us
    all_to_all x1, starting transfers between devices, body_by_slots(): lax.all_to_all(jnp.broadcast_to(shots[None], (slab_count,) + shots.shape)...  6.35 us
    unnamed x9, local copies, waits for them, and re-layouts  5.31 us
    all_to_all x1, waiting for transfers between devices, body_by_slots(): lax.all_to_all(jnp.broadcast_to(shots[None], (slab_count,) + shots.shape)...  2.5 us
  transfers between devices with their start and end apart: 2, of which 1 were waited for; matrix products, arithmetic and copies ran while one was open for 5% of the time, Pallas kernels for 0%

profile of v2, /device:TPU:0, one launch (start us, length us, event | category | flops | bytes accessed | tf_op | source)
XLA Modules:
  0.0 123.5 jit_solution(11977436342122552913)
XLA Ops:
  0.6 0.7 pad_add_fusion
  1.3 0.6 broadcast_in_dim.88
  1.9 6.4 %all-to-all-start = ((s32[8,2,1,32]{3,2,1,0:T(1,128)}), s32[8,2,1,32]{3,2,1,0:T(1,128)S(1)}, u32[]{:S(2)}, u32[]{:S(2)}) async-start(s32[8,2,1,32]{3,2,1,0:T(1,128)} %broadcast_in_dim.88), calls=%async_computation | async-start | bytes 16384 | tf_op jit(solution)/shard_map/all_to_all | solution.py:746
  8.3 1.4 %copy.12 = f32[2,8,128,128]{3,2,1,0:T(8,128)S(1)} copy(f32[2,8,128,128]{3,1,2,0:T(8,128)} %bitcast.15) | data formatting | bytes 2097152
  9.7 0.1 bitcast_convert_fusion
  9.8 1.4 %collective-permute-start = (bf16[16,8,128]{2,1,0:T(8,128)(2,1)S(1)}, bf16[16,8,128]{2,1,0:T(8,128)(2,1)S(1)}, u32[]{:S(2)}, u32[]{:S(2)}) collective-permute-start(bf16[16,8,128]{2,1,0:T(8,128)(2,1)S(1)} %slice.15), channel_id=1, source_target_pairs={{1,0},{4,1},{5,4},{8,5},{9,8},{12,9},{13,12},{3,2},{6,3},{7,6},{10... | collective-permute-start | bytes 98312 | tf_op jit(solution)/shard_map/ppermute | solution.py:18
  11.3 0.1 pad.2.clone
  11.4 2.5 %all-to-all-done = s32[8,2,1,32]{3,2,1,0:T(1,128)S(1)} async-done(((s32[8,2,1,32]{3,2,1,0:T(1,128)}), s32[8,2,1,32]{3,2,1,0:T(1,128)S(1)}, u32[]{:S(2)}, u32[]{:S(2)}) %all-to-all-start) | async-done | bytes 2080 | tf_op jit(solution)/shard_map/all_to_all | solution.py:746
  13.9 0.3 convert_reduce_fusion
  14.2 1.2 select_reduce_fusion
  15.4 0.1 gt.29
  15.5 0.1 sub.24
  15.6 0.1 add_select_fusion
  15.7 0.1 select_n.80
  15.8 1.7 %fusion.1.slot_table_ref = bf16[1024,512]{1,0:T(8,128)(2,1)} fusion(bf16[512,512]{1,0:T(8,128)(2,1)S(1)} %copy-done.2, s32[1024]{0:T(1024)S(1)} %select_n.80), kind=kOutput, calls=%fused_computation.2 | convolution fusion | flops 537919488 | bytes 1576960 | tf_op jit(solution)/shard_map/dot_general | solution.py:262
  17.5 0.3 select_reduce_fusion.1
  17.9 0.1 broadcast_in_dim.95
  17.9 0.1 select_n.76
  18.0 1.0 maximum_maximum_fusion.blocks_ref
  19.0 0.7 broadcast_in_dim.92.starts_ref
  19.7 0.7 broadcast_in_dim.96.picks_ref
  20.4 99.2 %shard_map.113 = (f32[2,8,32,512]{3,2,1,0:T(8,128)}, f32[16,128,128]{2,1,0:T(8,128)}) custom-call(s32[64,128]{1,0:T(8,128)} %broadcast_in_dim.92.starts_ref, s32[64,128]{1,0:T(8,128)} %broadcast_in_dim.96.picks_ref, f32[16,128,128]{2,1,0:T(8,128)} %bitcast.14, bf16[16,144,128]{2,1,0:T(8,128)(2,1)} %maximum_maximum_fusion.blocks_ref, ...), custom_call_target="tpu_custom_call" | custom-call | tf_op jit(solution)/shard_map/pallas_call | solution.py:790
  119.6 2.9 %copy.15 = f32[2,8,128,128]{3,1,2,0:T(8,128)} copy(f32[2,8,128,128]{3,2,1,0:T(8,128)} %bitcast.17) | data formatting | bytes 2097152
  122.5 1.0 copy.17
  (19 shorter events, 0.1 us)
Async XLA Ops:
  1.9 12.0 %all-to-all-start = ((s32[8,2,1,32]{3,2,1,0:T(1,128)}), s32[8,2,1,32]{3,2,1,0:T(1,128)S(1)}, u32[]{:S(2)}, u32[]{:S(2)}) async-start(s32[8,2,1,32]{3,2,1,0:T(1,128)} %broadcast_in_dim.88), calls=%async_computation | async-start | bytes 16384 | tf_op jit(solution)/shard_map/all_to_all | solution.py:746
  9.7 7.8 %copy-start = (f32[2,8,128,128]{3,2,1,0:T(8,128)}, f32[2,8,128,128]{3,2,1,0:T(8,128)S(1)}, u32[]{:S(2)}) copy-start(f32[2,8,128,128]{3,2,1,0:T(8,128)S(1)} %copy.12) | copy-start | bytes 3145732
  9.7 6.1 %copy-start.2 = (bf16[512,512]{1,0:T(8,128)(2,1)S(1)}, bf16[512,512]{1,0:T(8,128)(2,1)}, u32[]{:S(2)}) copy-start(bf16[512,512]{1,0:T(8,128)(2,1)} %constant.81.clone) | copy-start | bytes 1572868
  9.8 8.2 %collective-permute-start = (bf16[16,8,128]{2,1,0:T(8,128)(2,1)S(1)}, bf16[16,8,128]{2,1,0:T(8,128)(2,1)S(1)}, u32[]{:S(2)}, u32[]{:S(2)}) collective-permute-start(bf16[16,8,128]{2,1,0:T(8,128)(2,1)S(1)} %slice.15), channel_id=1, source_target_pairs={{1,0},{4,1},{5,4},{8,5},{9,8},{12,9},{13,12},{3,2},{6,3},{7,6},{10... | collective-permute-start | bytes 98312 | tf_op jit(solution)/shard_map/ppermute | solution.py:18
  119.6 2.9 %copy-start.1 = (f32[2,8,32,512]{3,2,1,0:T(8,128)S(1)}, f32[2,8,32,512]{3,2,1,0:T(8,128)}, u32[]{:S(2)}) copy-start(f32[2,8,32,512]{3,2,1,0:T(8,128)} %get-tuple-element.4) | copy-start | bytes 3145732

commit v3 on v2

--- a/solution.py
+++ b/solution.py
@@ -327,9 +327,10 @@
     return chosen
 
 
-def correlate_line(line, select_ref, blocks_ref, taps_ref, picks_ref, field_ref, traces_ref):
+def correlate_line(line, padded, select_ref, blocks_ref, taps_ref, picks_ref, field_ref, traces_ref):
     slots, width = picks_ref.shape
-    window = dot(select_ref[...], blocks_ref[line]).astype(jnp.bfloat16)
+    blocks = blocks_ref[pl.ds(pl.multiple_of(line * padded, 8), padded)].astype(jnp.bfloat16)
+    window = dot(select_ref[...], blocks).astype(jnp.bfloat16)
     later = jnp.concatenate([window[slots:], jnp.zeros((slots, width), window.dtype)], axis=0)
     terms = pick_signature(dot(jnp.concatenate([window, later], axis=1), taps_ref[...]), picks_ref)
     steps = terms.shape[0] // slots
@@ -441,25 +442,36 @@
 def whole_kernel(
     sizes,
     place,
-    starts_ref,
-    picks_ref,
-    records_ref,
-    blocks_ref,
+    offsets_ref,
+    filters_ref,
     signatures_ref,
     levels_ref,
+    records_hbm,
+    table_hbm,
+    grid_hbm,
+    row_table_hbm,
+    cosine_hbm,
+    sine_hbm,
+    model_ref,
+    left_ref,
+    records_ref,
     table_ref,
-    slot_table_ref,
+    grid_ref,
     row_table_ref,
     cosine_ref,
     sine_ref,
-    model_ref,
-    left_ref,
+    row_ref,
+    rows_ref,
+    rim_ref,
+    picks_ref,
+    slot_table_ref,
     adjoint_ref,
     forward_ref,
     select_ref,
     place_ref,
     traces_ref,
     field_ref,
+    blocks_ref,
     rest_ref,
     head_ref,
     spill_ref,
@@ -471,6 +483,9 @@
     home_ref,
     reply_ref,
     final_ref,
+    load_sems,
+    row_sends,
+    row_recvs,
     go_sends,
     go_recvs,
     back_sends,
@@ -479,44 +494,141 @@
     rim_recvs,
 ):
     slots, width = picks_ref.shape
-    rcv, padded, _ = blocks_ref.shape
-    blocks = records_ref.shape[1]
-    chunks = table_ref.shape[0]
-    samples = table_ref.shape[2]
+    rcv, slab_len = records_ref.shape
+    blocks = slab_len // width
+    padded = blocks_ref.shape[0] // rcv
+    chunks, _, samples = table_ref.shape
     steps = samples // width
     parts = place.size
+    slab_count = place.shape[1]
     few = samples // 2 // parts // chunks
     lines_in_half = rcv // HALVES
     rows_in_half = lines_in_half * few
     edge = head_ref.shape[1]
     all_rcv = rcv * place.shape[0]
-    halves = [range(half * lines_in_half, (half + 1) * lines_in_half) for half in range(HALVES)]
-
+    shot_count = offsets_ref.shape[1]
+    row_count = slab_count
+    capacity = slots // row_count
+    wide = jnp.float32
+
+    loads = [
+        pltpu.make_async_copy(source, target, load_sems.at[number])
+        for number, (source, target) in enumerate(
+            (
+                (records_hbm, records_ref),
+                (table_hbm, table_ref),
+                (grid_hbm, grid_ref),
+                (cosine_hbm, cosine_ref),
+                (sine_hbm, sine_ref),
+                (row_table_hbm, row_table_ref),
+            )
+        )
+    ]
+    for load in loads:
+        load.start()
     barrier = pltpu.get_barrier_semaphore()
     hops = neighbours(sizes)
     for hop in hops:
         pl.semaphore_signal(barrier, inc=1, device_id=device_at(sizes, hop)[0], device_id_type=MESH)
     mine = device_at(sizes, (0, 0, 0))[1]
     slab = lax.axis_index("shot") * sizes[2] + lax.axis_index("rep")
-    last_slab = sizes[0] * sizes[2] - 1
+    last_slab = slab_count - 1
 
     def slab_device(shift):
-        other = lax.rem(slab + shift + last_slab + 1, last_slab + 1)
+        other = lax.rem(slab + shift + slab_count, slab_count)
         return {
             "shot": other // sizes[2],
             "rcv": lax.axis_index("rcv"),
             "rep": lax.rem(other, sizes[2]),
         }
 
+    row_ref[...] = jnp.zeros_like(row_ref)
+    row_ref[0:1, :shot_count] = offsets_ref[...]
+    row_ref[1:2, :shot_count] = filters_ref[...]
     build_taps(signatures_ref, True, adjoint_ref)
-    block_index = lax.broadcasted_iota(jnp.int32, (slots, padded), 1)
-    first_block = jnp.broadcast_to(starts_ref[:, :1], (slots, padded))
+    pl.semaphore_wait(barrier, len(hops))
+
+    tile = row_ref.shape[0]
+    here = pl.ds(pl.multiple_of(slab * tile, tile), tile)
+    row_copies = []
+    for hop in hops:
+        if hop[1] == 0:
+            number = len(row_copies)
+            copy = pltpu.make_async_remote_copy(
+                src_ref=row_ref,
+                dst_ref=rows_ref.at[here],
+                send_sem=row_sends.at[number],
+                recv_sem=row_recvs.at[number],
+                device_id=device_at(sizes, hop)[0],
+                device_id_type=MESH,
+            )
+            copy.start()
+            row_copies.append(copy)
+    rows_ref[here] = row_ref[...]
+    loads[0].wait()
+    first_rim = pltpu.make_async_remote_copy(
+        src_ref=records_ref.at[:, pl.ds(0, rim_ref.shape[1])],
+        dst_ref=rim_ref,
+        send_sem=rim_sends.at[HALVES, 0],
+        recv_sem=rim_recvs.at[HALVES, 0],
+        device_id=slab_device(-1),
+        device_id_type=MESH,
+    )
+
+    @pl.when(slab > 0)
+    def _():
+        first_rim.start()
+
+    for line in range(rcv):
+        blocks_ref[line * padded + blocks : (line + 1) * padded] = jnp.zeros(
+            (padded - blocks, width), wide
+        )
+    for block in range(blocks):
+        blocks_ref[pl.ds(block, rcv, stride=padded), :] = records_ref[
+            :, block * width : (block + 1) * width
+        ]
+    for copy in row_copies:
+        copy.wait_recv()
+
+    lane = lax.broadcasted_iota(jnp.int32, (row_count, width), 1)
+    valid = lane < shot_count
+    zero = jnp.zeros((row_count, width), jnp.int32)
+    start_sample = jnp.where(valid, rows_ref[pl.ds(0, row_count, stride=tile), :], zero)
+    signature = jnp.where(valid, rows_ref[pl.ds(1, row_count, stride=tile), :], zero)
+    block_bits = width.bit_length() - 1
+    slab_bits = slab_len.bit_length() - 1
+    owner = lax.shift_right_logical(start_sample, slab_bits)
+    rank = zero
+    for step in range(1, shot_count):
+        same = (pltpu.roll(owner, step, 1) == owner) & (lane >= step)
+        rank = rank + same.astype(jnp.int32)
+    key = jnp.where(valid, owner * capacity + rank + 1, zero)
+    first_block = (lax.shift_right_logical(start_sample, block_bits) & (blocks - 1)).astype(wide)
+    signature = signature.astype(wide)
+    firsts, picks = [], []
+    for level in range(capacity):
+        taken = key == slab * capacity + level + 1
+        empty = jnp.zeros_like(first_block)
+        firsts.append(jnp.sum(jnp.where(taken, first_block + 1.0, empty), axis=1, keepdims=True))
+        picks.append(jnp.sum(jnp.where(taken, signature, empty), axis=1, keepdims=True))
+    firsts = jnp.broadcast_to(jnp.concatenate(firsts, axis=0), (slots, padded))
+    firsts = jnp.where(firsts > 0.5, firsts - 1.0, -float(samples))
+    picks_ref[...] = jnp.broadcast_to(jnp.concatenate(picks, axis=0), (slots, width))
+    block_index = lax.broadcasted_iota(jnp.int32, (slots, padded), 1).astype(wide)
     select = jnp.concatenate(
-        [(block_index == first_block + step).astype(jnp.float32) for step in range(steps)], axis=0
+        [(block_index == firsts + float(step)).astype(wide) for step in range(steps)], axis=0
     )
     select_ref[...] = select.astype(jnp.bfloat16)
-    place_ref[...] = select.T.astype(jnp.bfloat16)
-    pl.semaphore_wait(barrier, len(hops))
+
+    @pl.when(slab < last_slab)
+    def _():
+        first_rim.wait_recv()
+        for step in range(rim_ref.shape[1] // width):
+            blocks_ref[pl.ds(blocks + step, rcv, stride=padded), :] = rim_ref[
+                :, step * width : (step + 1) * width
+            ]
+
+    loads[1].wait()
 
     def exchange(source, target, send_sems, recv_sems, low, rows):
         made = []
@@ -536,41 +648,67 @@
         target[mine, where] = source[mine, where]
         return made
 
-    def send_half(half, from_ref, model):
+    def send_span(number, span, from_ref, model):
         def one(line, carry):
-            correlate_line(line, select_ref, from_ref, adjoint_ref, picks_ref, model, traces_ref)
+            correlate_line(
+                line, padded, select_ref, from_ref, adjoint_ref, picks_ref, model, traces_ref
+            )
             return carry
 
-        lax.fori_loop(half * lines_in_half, (half + 1) * lines_in_half, one, 0)
+        lax.fori_loop(span[0], span[1], one, 0)
         made = []
         for chunk in range(chunks):
             spectra_chunk(
-                table_ref[chunk], traces_ref, sent_ref.at[chunk], halves[half], rcv, slots
+                table_ref[chunk], traces_ref, sent_ref.at[chunk], range(*span), rcv, slots
             )
             made.append(
                 exchange(
                     sent_ref.at[chunk],
                     got_ref.at[chunk],
-                    go_sends.at[half, chunk],
-                    go_recvs.at[half, chunk],
-                    half * rows_in_half,
-                    rows_in_half,
+                    go_sends.at[number, chunk],
+                    go_recvs.at[number, chunk],
+                    span[0] * few,
+                    (span[1] - span[0]) * few,
                 )
             )
         return made
 
-    def level(index, chunk):
+    def level_at(index, chunk):
         return level_of(levels_ref, index, (mine * chunks + chunk) * few, few, all_rcv)
 
-    going = [send_half(half, blocks_ref, None) for half in range(HALVES)]
+    quarter = rcv // 4
+    spans = ((0, quarter), (quarter, 2 * quarter), (2 * quarter, rcv))
+    going = [send_span(number, span, blocks_ref, None) for number, span in enumerate(spans)]
+
+    place_ref[...] = select.T.astype(jnp.bfloat16)
     build_taps(signatures_ref, False, forward_ref)
+    repeated = key
+    for shift in range(shot_count, width, shot_count):
+        repeated = repeated + pltpu.roll(key, shift, 1)
+    points = row_count * shot_count
+    repeated = jnp.concatenate([repeated] * (points // width), axis=1)
+    point = lax.broadcasted_iota(jnp.int32, (row_count, points), 1)
+    row = lax.broadcasted_iota(jnp.int32, (row_count, points), 0)
+    shot_bits = shot_count.bit_length() - 1
+    repeated = jnp.where(lax.shift_right_logical(point, shot_bits) == row, repeated, 0)
+    chosen = jnp.concatenate(
+        [(repeated == number + 1).astype(wide) for number in range(slab_count * capacity)], axis=0
+    ).astype(jnp.bfloat16)
+    for load in loads[2:]:
+        load.wait()
+    for half in range(2):
+        part = dot(chosen, grid_ref[half * points : (half + 1) * points]).astype(jnp.bfloat16)
+        for number in range(slab_count):
+            low = (2 * number + half) * slots
+            slot_table_ref[low : low + slots] = part[number * slots : (number + 1) * slots]
+
     coming = {}
     for chunk in range(chunks):
-        for half in range(HALVES):
-            for copy in going[half][chunk]:
+        for made in going:
+            for copy in made[chunk]:
                 copy.wait_recv()
         bins_chunk(
-            place, 1, got_ref.at[chunk], slot_table_ref, slot_table_ref, cosine_ref[...], sine_ref[...], level(0, chunk), answer_ref.at[chunk]
+            place, 1, got_ref.at[chunk], slot_table_ref, slot_table_ref, cosine_ref[...], sine_ref[...], level_at(0, chunk), answer_ref.at[chunk]
         )
         coming[0, chunk] = exchange(
             answer_ref.at[chunk], home_ref.at[chunk], back_sends.at[0, chunk], back_recvs.at[0, chunk], 0, rows_in_half
@@ -585,6 +723,13 @@
                 half * rows_in_half,
                 rows_in_half,
             )
+    for copy in row_copies:
+        copy.wait_send()
+
+    @pl.when(slab > 0)
+    def _():
+        first_rim.wait_send()
+
     for made in going:
         for chunk in made:
             for copy in chunk:
@@ -606,8 +751,12 @@
 
         def one(line, carry):
             blended = blend_line(line, place_ref, field_ref, forward_ref, picks_ref)
-            left = records_ref[line] - blended[:blocks]
-            left_ref[line] = left
+            start = pl.multiple_of(line * padded, 8)
+            left = blocks_ref[pl.ds(start, blocks)] - blended[:blocks]
+            rest_ref[pl.ds(start, blocks)] = left
+            rest_ref[pl.ds(start + blocks, padded - blocks)] = jnp.zeros(
+                (padded - blocks, width), wide
+            )
             head_ref[line] = left[:edge]
             spill_ref[line] = blended[blocks : blocks + edge]
             return carry
@@ -639,29 +788,27 @@
         def _():
             backward.start()
             onward.wait_recv()
-            left_ref[where, :edge] = left_ref[where, :edge] - carried_ref[where]
-
-        rest_ref[where, :blocks] = left_ref[where].astype(jnp.bfloat16)
-        rest_ref[where, blocks:] = jnp.zeros(
-            (lines_in_half, padded - blocks, width), jnp.bfloat16
-        )
+            for line in range(low, high):
+                here = pl.ds(line * padded, edge)
+                rest_ref[here] = rest_ref[here] - carried_ref[line]
 
         @pl.when(slab < last_slab)
         def _():
             backward.wait_recv()
-            rim = ahead_ref[where] - spill_ref[where]
-            rim = jnp.concatenate(
-                [rim, jnp.zeros((lines_in_half, padded - blocks - edge, width), jnp.float32)], axis=1
-            )
-            rest_ref[where, blocks:] = rim.astype(jnp.bfloat16)
+            for line in range(low, high):
+                rest_ref[pl.ds(line * padded + blocks, edge)] = ahead_ref[line] - spill_ref[line]
             onward.wait_send()
 
         @pl.when(slab > 0)
         def _():
             backward.wait_send()
 
-        again.append(send_half(half, rest_ref, field_ref))
-
+        again.append(send_span(half, (low, high), rest_ref, field_ref))
+
+    for block in range(blocks):
+        left_ref[:, block * width : (block + 1) * width] = rest_ref[
+            pl.ds(block, rcv, stride=padded), :
+        ]
     for half in range(HALVES):
         for chunk in range(chunks):
             for copy in coming[half, chunk]:
@@ -672,7 +819,7 @@
             for copy in again[half][chunk]:
                 copy.wait_recv()
         bins_chunk(
-            place, 2, got_ref.at[chunk], slot_table_ref, row_table_ref, cosine_ref[...], sine_ref[...], level(1, chunk), reply_ref.at[chunk]
+            place, 2, got_ref.at[chunk], slot_table_ref, row_table_ref, cosine_ref[...], sine_ref[...], level_at(1, chunk), reply_ref.at[chunk]
         )
         final.append(
             exchange(
@@ -742,81 +889,49 @@
     cosine = jnp.asarray(np.kron(table_r[0, :, 0], same).astype(jnp.bfloat16))
     sine = jnp.asarray(np.kron(table_r[0, :, 1], same).astype(jnp.bfloat16))
 
-    shots = jnp.stack([offsets, filter_index])
-    every = lax.all_to_all(
-        jnp.broadcast_to(shots[None], (slab_count,) + shots.shape), ("shot", "rep"), 0, 0, tiled=True
-    )
-    every_offset = every[:, 0].reshape(row_count, shot_count)
-    every_pick = every[:, 1].reshape(row_count, shot_count)
-    every_owner = every_offset // slab_len
-    every_rank = rank_in_row(every_owner)
-    slabs = jnp.arange(slab_count, dtype=jnp.int32)
-    ranks = jnp.arange(capacity, dtype=jnp.int32)
-    taken = (every_owner[None, :, None, :] == slabs[:, None, None, None]) & (
-        every_rank[None, :, None, :] == ranks[None, None, :, None]
-    )
-    point_of = jnp.arange(row_count * shot_count, dtype=jnp.int32).reshape(row_count, shot_count)
-    code = jnp.sum(jnp.where(taken, point_of[None, :, None, :] + 1, 0), axis=3).reshape(
-        slab_count, 1, slots
-    )
-    code = jnp.where(
-        code > 0, code - 1 + row_count * shot_count * jnp.arange(2, dtype=jnp.int32)[None, :, None], -1
-    ).reshape(-1)
-    chosen = (code[:, None] == jnp.arange(points, dtype=jnp.int32)[None, :]).astype(jnp.bfloat16)
-    slot_table = dot(chosen, grid_table).astype(jnp.bfloat16)
-    mine = (every_owner == lax.axis_index(("shot", "rep")))[:, None, :] & (
-        every_rank[:, None, :] == ranks[None, :, None]
-    )
-    every_start = every_offset // tap_count % slab_blocks
-    starts = jnp.sum(jnp.where(mine, every_start[:, None, :] + 1, 0), axis=2).reshape(-1)
-    starts = jnp.where(starts > 0, starts - 1, -NT)
-    picks = jnp.sum(jnp.where(mine, every_pick[:, None, :], 0), axis=2).reshape(-1)
-    starts = jnp.broadcast_to(starts[:, None], (slots, tap_count))
-    picks = jnp.broadcast_to(picks[:, None], (slots, tap_count))
-
     edge = 8
     padded = slab_blocks + 2 * edge
-    record_blocks = records.reshape(local_rcv, slab_blocks, tap_count)
-    rim = from_behind(
-        record_blocks[:, :edge].astype(jnp.bfloat16), ("shot", "rep"), -1
-    )
-    extended = jnp.concatenate(
-        [record_blocks.astype(jnp.bfloat16), rim, jnp.zeros_like(rim)], axis=1
-    )
     vmem = pl.BlockSpec(memory_space=pltpu.VMEM)
+    anywhere = pl.BlockSpec(memory_space=pl.ANY)
     rows = local_rcv * few
     table_width = tap_count * signatures.shape[0]
     low, wide = jnp.bfloat16, jnp.float32
+    big = (records, time_table_fixed, grid_table, row_table, cosine, sine)
     model, residual = pl.pallas_call(
         functools.partial(whole_kernel, sizes, place),
         out_shape=(
             jax.ShapeDtypeStruct((2, local_rcv // 2, shot_count, NT), wide),
-            jax.ShapeDtypeStruct(record_blocks.shape, wide),
+            jax.ShapeDtypeStruct(records.shape, wide),
         ),
-        in_specs=[vmem] * 11,
+        in_specs=[vmem] * 4 + [anywhere] * len(big),
         out_specs=(vmem, vmem),
-        scratch_shapes=[
+        scratch_shapes=[pltpu.VMEM(array.shape, array.dtype) for array in big]
+        + [
+            pltpu.VMEM((edge, tap_count), jnp.int32),
+            pltpu.VMEM((slab_count * edge, tap_count), jnp.int32),
+            pltpu.VMEM((local_rcv, (steps - 1) * tap_count), wide),
+            pltpu.VMEM((slots, tap_count), wide),
+            pltpu.VMEM((slab_count * 2 * slots, points), low),
             pltpu.VMEM((2 * tap_count, table_width), low),
             pltpu.VMEM((2 * tap_count, table_width), low),
             pltpu.VMEM((slots * steps, padded), low),
             pltpu.VMEM((padded, slots * steps), low),
             pltpu.VMEM((local_rcv * slots, NT), low),
             pltpu.VMEM((local_rcv * slots, NT), wide),
-            pltpu.VMEM(extended.shape, low),
+            pltpu.VMEM((local_rcv * padded, tap_count), wide),
+            pltpu.VMEM((local_rcv * padded, tap_count), wide),
         ]
         + [pltpu.VMEM((local_rcv, edge, tap_count), wide)] * 4
         + [pltpu.VMEM((chunks, parts, rows, 2 * slots), low)] * 4
         + [pltpu.VMEM((chunks, parts, rows // 2, 4 * shot_count), low)] * 2
-        + [pltpu.SemaphoreType.DMA((HALVES, chunks, parts - 1))] * 4
-        + [pltpu.SemaphoreType.DMA((HALVES, 2))] * 2,
+        + [pltpu.SemaphoreType.DMA((len(big),))]
+        + [pltpu.SemaphoreType.DMA((slab_count - 1,))] * 2
+        + [pltpu.SemaphoreType.DMA((3, chunks, parts - 1))] * 2
+        + [pltpu.SemaphoreType.DMA((HALVES, chunks, parts - 1))] * 2
+        + [pltpu.SemaphoreType.DMA((HALVES + 1, 2))] * 2,
         compiler_params=pltpu.CompilerParams(collective_id=0, has_side_effects=True),
-    )(
-        starts, picks, record_blocks, extended, signatures, thresholds, time_table_fixed, slot_table, row_table, cosine, sine
-    )
-    return (
-        model.reshape(rows_here, local_rcv, shot_count, NT),
-        residual.reshape(local_rcv, slab_len),
-    )
+    )(offsets, filter_index, signatures, thresholds, *big)
+    return (model.reshape(rows_here, local_rcv, shot_count, NT), residual)
 
 
 def body(records, offsets, filter_index, signatures, thresholds):
@@ -827,6 +942,8 @@
     table_rows = 2 * rows_here * slab_count * shot_count
     fits = table_rows <= 1024 and rows_here == 1 and slots == 64 and 4 * shot_count == 128
     fits = fits and records.shape[0] == 16 and NT // 2 // parts == 16
+    slab_len, tap_count = records.shape[1], signatures.shape[1]
+    fits = fits and tap_count == 128 and slab_len & (slab_len - 1) == 0
     run = body_by_slots if fits else body_by_rows
     return run(records, offsets, filter_index, signatures, thresholds)
 

time: 124 us -> 108 us (0.87)
  starting transfers between devices: 7.78 us -> 0 us
  Pallas kernels: 99.2 us -> 104 us
  local copies, waits for them, and re-layouts: 7.76 us -> 3.35 us
  other arithmetic: 3.72 us -> 0 us
  waiting for transfers between devices: 2.5 us -> 0 us
  matrix products: 1.73 us -> 0 us
    all_to_all x1 -> x0, starting transfers between devices: 6.35 us -> none  [body_by_slots(): lax.all_to_all(jnp.broadcast_to(shots[None], (slab_count,) + shots.shape)...]
    pallas_call x1, Pallas kernels: 99.2 us -> 104 us  [body_by_slots(): pl.pallas_call(functools.partial(whole_kernel, sizes, place), out_shape=(...]
    all_to_all x1 -> x0, waiting for transfers between devices: 2.5 us -> none  [body_by_slots(): lax.all_to_all(jnp.broadcast_to(shots[None], (slab_count,) + shots.shape)...]
    broadcast_in_dim x5 -> x0, local copies, waits for them, and re-layouts: 2.04 us -> none  [the longest x2 0.76 us: body_by_slots(): picks = jnp.broadcast_to(picks[:, None], (slots, tap_count))]
    unnamed x9 -> x4, local copies, waits for them, and re-layouts: 5.31 us -> 3.35 us
    reduce_sum x3 -> x0, other arithmetic: 1.8 us -> none  [the longest x1 1.16 us: body_by_slots(): jnp.sum(jnp.where(taken, point_of[None, :, None, :] + 1, 0), axis=3)]
    dot_general x1 -> x0, matrix products: 1.73 us -> none  [dot(): lax.dot_general(left, right, (((left_dim,), (right_dim,)), ((), ())), pre...]
    ppermute x1 -> x0, starting transfers between devices: 1.42 us -> none  [from_behind(): lax.ppermute(value, axis, [(source, source + steps) for source in range(f...]
  transfers between devices with their start and end apart: 2 -> 0, of which waited for: 1 -> 0; matrix products, arithmetic and copies ran while one was open for 5% -> 0% of each run, Pallas kernels for 0% -> 0%
where the time goes in v3:
time: 108 us
  Pallas kernels  104 us (96%)
  local copies, waits for them, and re-layouts  3.35 us (3%)
    pallas_call x1, Pallas kernels, body_by_slots(): pl.pallas_call(functools.partial(whole_kernel, sizes, place), out_shape=(...  104 us
    unnamed x4, local copies, waits for them, and re-layouts  3.35 us

profile of v3, /device:TPU:0, one launch (start us, length us, event | category | flops | bytes accessed | tf_op | source)
XLA Modules:
  0.0 107.7 jit_solution(7957979396377163464)
XLA Ops:
  0.6 103.7 %shard_map.113 = (f32[2,8,32,512]{3,2,1,0:T(8,128)}, f32[16,16384]{1,0:T(8,128)}) custom-call(s32[1,32]{1,0:T(1,128)} %offsets_ref.1, s32[1,32]{1,0:T(1,128)} %filters_ref.1, bf16[8,128]{1,0:T(8,128)(2,1)} %signatures_ref.1, f32[2,256]{1,0:T(2,128)} %levels_ref.1, f32[16,16384]{1,0:T(8,128)} %records_hbm.1, bf16[2,256,512]{2,1,0:T(8,128)(2,1)} %constant.10.clone.table_hbm, ...), custom_call_target="tpu_custom_call" | custom-call | tf_op jit(solution)/shard_map/pallas_call | solution.py:900
  104.3 0.0 copy-start
  104.3 2.4 %copy.14 = f32[1,16,32,512]{3,2,1,0:T(8,128)} copy(f32[1,16,32,512]{3,2,1,0:T(8,128)} %bitcast.1) | data formatting | bytes 2097152
  106.7 0.0 copy-done
  106.7 1.0 copy.15
Async XLA Ops:
  104.3 2.4 %copy-start = (f32[16,16384]{1,0:T(8,128)S(1)}, f32[16,16384]{1,0:T(8,128)}, u32[]{:S(2)}) copy-start(f32[16,16384]{1,0:T(8,128)} %get-tuple-element.9) | copy-start | bytes 3145732

commit v4 on v3

--- a/solution.py
+++ b/solution.py
@@ -435,8 +435,8 @@
     return jnp.concatenate(pieces, axis=0)
 
 
-HALVES = 2
 CHUNKS = 2
+SPANS = 3
 
 
 def whole_kernel(
@@ -452,7 +452,7 @@
     row_table_hbm,
     cosine_hbm,
     sine_hbm,
-    model_ref,
+    final_ref,
     left_ref,
     records_ref,
     table_ref,
@@ -482,7 +482,6 @@
     answer_ref,
     home_ref,
     reply_ref,
-    final_ref,
     load_sems,
     row_sends,
     row_recvs,
@@ -502,8 +501,9 @@
     parts = place.size
     slab_count = place.shape[1]
     few = samples // 2 // parts // chunks
-    lines_in_half = rcv // HALVES
-    rows_in_half = lines_in_half * few
+    quarter = rcv // 4
+    early_spans = ((0, quarter), (quarter, 2 * quarter), (2 * quarter, rcv))
+    late_spans = ((0, 2 * quarter), (2 * quarter, 3 * quarter), (3 * quarter, rcv))
     edge = head_ref.shape[1]
     all_rcv = rcv * place.shape[0]
     shot_count = offsets_ref.shape[1]
@@ -569,8 +569,8 @@
     first_rim = pltpu.make_async_remote_copy(
         src_ref=records_ref.at[:, pl.ds(0, rim_ref.shape[1])],
         dst_ref=rim_ref,
-        send_sem=rim_sends.at[HALVES, 0],
-        recv_sem=rim_recvs.at[HALVES, 0],
+        send_sem=rim_sends.at[SPANS, 0],
+        recv_sem=rim_recvs.at[SPANS, 0],
         device_id=slab_device(-1),
         device_id_type=MESH,
     )
@@ -676,9 +676,9 @@
     def level_at(index, chunk):
         return level_of(levels_ref, index, (mine * chunks + chunk) * few, few, all_rcv)
 
-    quarter = rcv // 4
-    spans = ((0, quarter), (quarter, 2 * quarter), (2 * quarter, rcv))
-    going = [send_span(number, span, blocks_ref, None) for number, span in enumerate(spans)]
+    going = [
+        send_span(number, span, blocks_ref, None) for number, span in enumerate(early_spans)
+    ]
 
     place_ref[...] = select.T.astype(jnp.bfloat16)
     build_taps(signatures_ref, False, forward_ref)
@@ -703,6 +703,18 @@
             slot_table_ref[low : low + slots] = part[number * slots : (number + 1) * slots]
 
     coming = {}
+
+    def send_back(number, chunk):
+        span = late_spans[number]
+        coming[number, chunk] = exchange(
+            answer_ref.at[chunk],
+            home_ref.at[chunk],
+            back_sends.at[number, chunk],
+            back_recvs.at[number, chunk],
+            span[0] * few,
+            (span[1] - span[0]) * few,
+        )
+
     for chunk in range(chunks):
         for made in going:
             for copy in made[chunk]:
@@ -710,19 +722,10 @@
         bins_chunk(
             place, 1, got_ref.at[chunk], slot_table_ref, slot_table_ref, cosine_ref[...], sine_ref[...], level_at(0, chunk), answer_ref.at[chunk]
         )
-        coming[0, chunk] = exchange(
-            answer_ref.at[chunk], home_ref.at[chunk], back_sends.at[0, chunk], back_recvs.at[0, chunk], 0, rows_in_half
-        )
-    for half in range(1, HALVES):
+        send_back(0, chunk)
+    for number in range(1, SPANS):
         for chunk in range(chunks):
-            coming[half, chunk] = exchange(
-                answer_ref.at[chunk],
-                home_ref.at[chunk],
-                back_sends.at[half, chunk],
-                back_recvs.at[half, chunk],
-                half * rows_in_half,
-                rows_in_half,
-            )
+            send_back(number, chunk)
     for copy in row_copies:
         copy.wait_send()
 
@@ -735,13 +738,33 @@
             for copy in chunk:
                 copy.wait_send()
 
-    again = []
-    for half in range(HALVES):
-        low, high = half * lines_in_half, (half + 1) * lines_in_half
+    def halo(number):
+        low, high = late_spans[number]
+        where = pl.ds(low, high - low)
+        onward = pltpu.make_async_remote_copy(
+            src_ref=spill_ref.at[where],
+            dst_ref=carried_ref.at[where],
+            send_sem=rim_sends.at[number, 0],
+            recv_sem=rim_recvs.at[number, 0],
+            device_id=slab_device(1),
+            device_id_type=MESH,
+        )
+        backward = pltpu.make_async_remote_copy(
+            src_ref=head_ref.at[where],
+            dst_ref=ahead_ref.at[where],
+            send_sem=rim_sends.at[number, 1],
+            recv_sem=rim_recvs.at[number, 1],
+            device_id=slab_device(-1),
+            device_id_type=MESH,
+        )
+        return onward, backward
+
+    def subtract(number):
+        low, high = late_spans[number]
         for chunk in range(chunks):
-            for copy in coming[half, chunk]:
+            for copy in coming[number, chunk]:
                 copy.wait_recv()
-        together = math.gcd(lines_in_half, 4)
+        together = math.gcd(high - low, 4)
         for first in range(low, high, together):
             lines = range(first, first + together)
             field_ref[first * slots : (first + together) * slots] = sum(
@@ -762,23 +785,7 @@
             return carry
 
         lax.fori_loop(low, high, one, 0)
-        where = pl.ds(low, lines_in_half)
-        onward = pltpu.make_async_remote_copy(
-            src_ref=spill_ref.at[where],
-            dst_ref=carried_ref.at[where],
-            send_sem=rim_sends.at[half, 0],
-            recv_sem=rim_recvs.at[half, 0],
-            device_id=slab_device(1),
-            device_id_type=MESH,
-        )
-        backward = pltpu.make_async_remote_copy(
-            src_ref=head_ref.at[where],
-            dst_ref=ahead_ref.at[where],
-            send_sem=rim_sends.at[half, 1],
-            recv_sem=rim_recvs.at[half, 1],
-            device_id=slab_device(-1),
-            device_id_type=MESH,
-        )
+        onward, backward = halo(number)
 
         @pl.when(slab < last_slab)
         def _():
@@ -787,6 +794,13 @@
         @pl.when(slab > 0)
         def _():
             backward.start()
+
+    def correlate_rest(number):
+        low, high = late_spans[number]
+        onward, backward = halo(number)
+
+        @pl.when(slab > 0)
+        def _():
             onward.wait_recv()
             for line in range(low, high):
                 here = pl.ds(line * padded, edge)
@@ -803,20 +817,26 @@
         def _():
             backward.wait_send()
 
-        again.append(send_span(half, (low, high), rest_ref, field_ref))
+        return send_span(number, late_spans[number], rest_ref, field_ref)
+
+    again = []
+    subtract(0)
+    for number in range(1, SPANS):
+        subtract(number)
+        again.append(correlate_rest(number - 1))
+    again.append(correlate_rest(SPANS - 1))
 
     for block in range(blocks):
         left_ref[:, block * width : (block + 1) * width] = rest_ref[
             pl.ds(block, rcv, stride=padded), :
         ]
-    for half in range(HALVES):
-        for chunk in range(chunks):
-            for copy in coming[half, chunk]:
-                copy.wait_send()
+    for made in coming.values():
+        for copy in made:
+            copy.wait_send()
     final = []
     for chunk in range(chunks):
-        for half in range(HALVES):
-            for copy in again[half][chunk]:
+        for made in again:
+            for copy in made[chunk]:
                 copy.wait_recv()
         bins_chunk(
             place, 2, got_ref.at[chunk], slot_table_ref, row_table_ref, cosine_ref[...], sine_ref[...], level_at(1, chunk), reply_ref.at[chunk]
@@ -830,23 +850,61 @@
         for chunk in made:
             for copy in chunk:
                 copy.wait_send()
-    groups, lines_there, count, _ = model_ref.shape
-    together = math.gcd(lines_there, 4)
-    for chunk in range(chunks):
-        for copy in final[chunk]:
+    for made in final:
+        for copy in made:
             copy.wait()
-        for first in range(0, lines_there, together):
-            fields = dot(
-                upright(final_ref, chunk, range(first, first + together), few, 2 * count),
-                table_ref[chunk],
-            )
-            for line in range(together):
-                for group in range(groups):
-                    low = (line * groups + group) * count
-                    piece = fields[low : low + count]
-                    if chunk:
-                        piece = piece + model_ref[group, first + line]
-                    model_ref[group, first + line] = piece
+
+
+def finish_kernel(bins, spectra_ref, left_ref, table_ref, model_ref, out_ref, sem):
+    chunks = spectra_ref.shape[0]
+    groups, together, count, _ = model_ref.shape
+    step = pl.program_id(0)
+    copy = pltpu.make_async_copy(left_ref, out_ref, sem)
+
+    @pl.when(step == 0)
+    def _():
+        copy.start()
+
+    fields = sum(
+        dot(upright(spectra_ref, chunk, range(together), bins, 2 * count), table_ref[chunk])
+        for chunk in range(chunks)
+    )
+    for line in range(together):
+        for group in range(groups):
+            low = (line * groups + group) * count
+            model_ref[group, line] = fields[low : low + count]
+
+    @pl.when(step == pl.num_programs(0) - 1)
+    def _():
+        copy.wait()
+
+
+def finish(spectra, left, table, groups, rcv):
+    chunks, parts, rows, lanes = spectra.shape
+    samples = table.shape[2]
+    bins = rows // rcv
+    count = lanes // 2 // groups
+    together = math.gcd(rcv, 4)
+    whole = pl.BlockSpec(memory_space=pltpu.VMEM)
+    return pl.pallas_call(
+        functools.partial(finish_kernel, bins),
+        grid=(rcv // together,),
+        out_shape=(
+            jax.ShapeDtypeStruct((groups, rcv, count, samples), jnp.float32),
+            jax.ShapeDtypeStruct(left.shape, jnp.float32),
+        ),
+        in_specs=[
+            pl.BlockSpec((chunks, parts, together * bins, lanes), lambda i: (0, 0, i, 0)),
+            whole,
+            whole,
+        ],
+        out_specs=(
+            pl.BlockSpec((groups, together, count, samples), lambda i: (0, i, 0, 0)),
+            pl.BlockSpec(memory_space=pl.ANY),
+        ),
+        scratch_shapes=[pltpu.SemaphoreType.DMA],
+        compiler_params=pltpu.CompilerParams(vmem_limit_bytes=16 * 2**20),
+    )(spectra, left, table)
 
 
 def body_by_slots(records, offsets, filter_index, signatures, thresholds):
@@ -897,11 +955,11 @@
     table_width = tap_count * signatures.shape[0]
     low, wide = jnp.bfloat16, jnp.float32
     big = (records, time_table_fixed, grid_table, row_table, cosine, sine)
-    model, residual = pl.pallas_call(
+    spectra, residual = pl.pallas_call(
         functools.partial(whole_kernel, sizes, place),
         out_shape=(
-            jax.ShapeDtypeStruct((2, local_rcv // 2, shot_count, NT), wide),
-            jax.ShapeDtypeStruct(records.shape, wide),
+            pltpu.VMEM((chunks, parts, rows // 2, 4 * shot_count), low),
+            pltpu.VMEM(records.shape, wide),
         ),
         in_specs=[vmem] * 4 + [anywhere] * len(big),
         out_specs=(vmem, vmem),
@@ -923,14 +981,16 @@
         ]
         + [pltpu.VMEM((local_rcv, edge, tap_count), wide)] * 4
         + [pltpu.VMEM((chunks, parts, rows, 2 * slots), low)] * 4
-        + [pltpu.VMEM((chunks, parts, rows // 2, 4 * shot_count), low)] * 2
+        + [pltpu.VMEM((chunks, parts, rows // 2, 4 * shot_count), low)]
         + [pltpu.SemaphoreType.DMA((len(big),))]
         + [pltpu.SemaphoreType.DMA((slab_count - 1,))] * 2
-        + [pltpu.SemaphoreType.DMA((3, chunks, parts - 1))] * 2
-        + [pltpu.SemaphoreType.DMA((HALVES, chunks, parts - 1))] * 2
-        + [pltpu.SemaphoreType.DMA((HALVES + 1, 2))] * 2,
-        compiler_params=pltpu.CompilerParams(collective_id=0, has_side_effects=True),
+        + [pltpu.SemaphoreType.DMA((SPANS, chunks, parts - 1))] * 4
+        + [pltpu.SemaphoreType.DMA((SPANS + 1, 2))] * 2,
+        compiler_params=pltpu.CompilerParams(
+            collective_id=0, has_side_effects=True, vmem_limit_bytes=60 * 2**20
+        ),
     )(offsets, filter_index, signatures, thresholds, *big)
+    model, residual = finish(spectra, residual, time_table_fixed, 2, local_rcv // 2)
     return (model.reshape(rows_here, local_rcv, shot_count, NT), residual)
 
 

time: 108 us -> 109 us (level)
  Pallas kernels: 104 us -> 108 us
  local copies, waits for them, and re-layouts: 3.35 us -> 0.01 us
    unnamed x4 -> x2, local copies, waits for them, and re-layouts: 3.35 us -> 0.01 us
    pallas_call x1, Pallas kernels: 104 us -> 106 us  [body_by_slots(): pl.pallas_call(functools.partial(whole_kernel, sizes, place), out_shape=(...]
    pallas_call x0 -> x1, Pallas kernels: none -> 1.84 us  [finish(): pl.pallas_call(functools.partial(finish_kernel, bins), grid=(rcv // toget...]
where the time goes in v4:
time: 109 us; the launch traced here: 108 us
  Pallas kernels  108 us (99%)
    pallas_call x1, Pallas kernels, body_by_slots(): pl.pallas_call(functools.partial(whole_kernel, sizes, place), out_shape=(...  106 us

profile of v4, /device:TPU:0, one launch (start us, length us, event | category | flops | bytes accessed | tf_op | source)
XLA Modules:
  0.0 108.4 jit_solution(4893052098808254413)
XLA Ops:
  0.6 0.0 copy-start
  0.6 105.7 %shard_map.113 = (bf16[2,16,64,128]{3,2,1,0:T(8,128)(2,1)S(1)}, f32[16,16384]{1,0:T(8,128)S(1)}) custom-call(s32[1,32]{1,0:T(1,128)} %offsets_ref.1, s32[1,32]{1,0:T(1,128)} %filters_ref.1, bf16[8,128]{1,0:T(8,128)(2,1)} %signatures_ref.1, f32[2,256]{1,0:T(2,128)} %levels_ref.1, f32[16,16384]{1,0:T(8,128)} %records_hbm.1, ...), custom_call_target="tpu_custom_call" | custom-call | tf_op jit(solution)/shard_map/pallas_call | solution.py:958
  106.3 0.0 copy-done
  106.4 1.8 %shard_map.114 = (f32[2,8,32,512]{3,2,1,0:T(8,128)}, f32[16,16384]{1,0:T(8,128)}) custom-call(bf16[2,16,64,128]{3,2,1,0:T(8,128)(2,1)S(1)} %get-tuple-element.6.spectra_ref, f32[16,16384]{1,0:T(8,128)S(1)} %get-tuple-element.7.left_ref, bf16[2,256,512]{2,1,0:T(8,128)(2,1)S(1)} %copy-done), custom_call_target="tpu_custom_call" | custom-call | tf_op jit(solution)/shard_map/pallas_call | solution.py:889
Async XLA Ops:
  0.6 105.7 %copy-start = (bf16[2,256,512]{2,1,0:T(8,128)(2,1)S(1)}, bf16[2,256,512]{2,1,0:T(8,128)(2,1)}, u32[]{:S(2)}) copy-start(bf16[2,256,512]{2,1,0:T(8,128)(2,1)} %constant.10.clone.table_hbm.table_ref) | copy-start | bytes 1572868

commit v5 on v4

--- a/solution.py
+++ b/solution.py
@@ -437,6 +437,7 @@
 
 CHUNKS = 2
 SPANS = 3
+UNROLL = 4
 
 
 def whole_kernel(
@@ -503,7 +504,7 @@
     few = samples // 2 // parts // chunks
     quarter = rcv // 4
     early_spans = ((0, quarter), (quarter, 2 * quarter), (2 * quarter, rcv))
-    late_spans = ((0, 2 * quarter), (2 * quarter, 3 * quarter), (3 * quarter, rcv))
+    late_spans = ((0, 2 * quarter), (2 * quarter, rcv))
     edge = head_ref.shape[1]
     all_rcv = rcv * place.shape[0]
     shot_count = offsets_ref.shape[1]
@@ -655,7 +656,7 @@
             )
             return carry
 
-        lax.fori_loop(span[0], span[1], one, 0)
+        lax.fori_loop(span[0], span[1], one, 0, unroll=UNROLL)
         made = []
         for chunk in range(chunks):
             spectra_chunk(
@@ -723,7 +724,7 @@
             place, 1, got_ref.at[chunk], slot_table_ref, slot_table_ref, cosine_ref[...], sine_ref[...], level_at(0, chunk), answer_ref.at[chunk]
         )
         send_back(0, chunk)
-    for number in range(1, SPANS):
+    for number in range(1, len(late_spans)):
         for chunk in range(chunks):
             send_back(number, chunk)
     for copy in row_copies:
@@ -784,7 +785,7 @@
             spill_ref[line] = blended[blocks : blocks + edge]
             return carry
 
-        lax.fori_loop(low, high, one, 0)
+        lax.fori_loop(low, high, one, 0, unroll=UNROLL)
         onward, backward = halo(number)
 
         @pl.when(slab < last_slab)
@@ -820,11 +821,9 @@
         return send_span(number, late_spans[number], rest_ref, field_ref)
 
     again = []
-    subtract(0)
-    for number in range(1, SPANS):
+    for number in range(len(late_spans)):
         subtract(number)
-        again.append(correlate_rest(number - 1))
-    again.append(correlate_rest(SPANS - 1))
+        again.append(correlate_rest(number))
 
     for block in range(blocks):
         left_ref[:, block * width : (block + 1) * width] = rest_ref[

time: 109 us -> 104 us (0.954)
  Pallas kernels: 108 us -> 103 us
    pallas_call x1, Pallas kernels: 106 us -> 101 us  [body_by_slots(): pl.pallas_call(functools.partial(whole_kernel, sizes, place), out_shape=(...]
where the time goes in v5:
time: 104 us
  Pallas kernels  103 us (99%)
    pallas_call x1, Pallas kernels, body_by_slots(): pl.pallas_call(functools.partial(whole_kernel, sizes, place), out_shape=(...  101 us

profile of v5, /device:TPU:0, one launch (start us, length us, event | category | flops | bytes accessed | tf_op | source)
XLA Modules:
  0.0 104.0 jit_solution(6814444680205017463)
XLA Ops:
  0.6 0.0 copy-start
  0.6 101.3 %shard_map.113 = (bf16[2,16,64,128]{3,2,1,0:T(8,128)(2,1)S(1)}, f32[16,16384]{1,0:T(8,128)S(1)}) custom-call(s32[1,32]{1,0:T(1,128)} %offsets_ref.1, s32[1,32]{1,0:T(1,128)} %filters_ref.1, bf16[8,128]{1,0:T(8,128)(2,1)} %signatures_ref.1, f32[2,256]{1,0:T(2,128)} %levels_ref.1, f32[16,16384]{1,0:T(8,128)} %records_hbm.1, ...), custom_call_target="tpu_custom_call" | custom-call | tf_op jit(solution)/shard_map/pallas_call | solution.py:957
  102.0 0.0 copy-done
  102.0 1.8 %shard_map.114 = (f32[2,8,32,512]{3,2,1,0:T(8,128)}, f32[16,16384]{1,0:T(8,128)}) custom-call(bf16[2,16,64,128]{3,2,1,0:T(8,128)(2,1)S(1)} %get-tuple-element.6.spectra_ref, f32[16,16384]{1,0:T(8,128)S(1)} %get-tuple-element.7.left_ref, bf16[2,256,512]{2,1,0:T(8,128)(2,1)S(1)} %copy-done), custom_call_target="tpu_custom_call" | custom-call | tf_op jit(solution)/shard_map/pallas_call | solution.py:888
Async XLA Ops:
  0.6 101.4 %copy-start = (bf16[2,256,512]{2,1,0:T(8,128)(2,1)S(1)}, bf16[2,256,512]{2,1,0:T(8,128)(2,1)}, u32[]{:S(2)}) copy-start(bf16[2,256,512]{2,1,0:T(8,128)(2,1)} %constant.10.clone.table_hbm.table_ref) | copy-start | bytes 1572868

commit v6 on v5

--- a/solution.py
+++ b/solution.py
@@ -436,7 +436,7 @@
 
 
 CHUNKS = 2
-SPANS = 3
+SPANS = 2
 UNROLL = 4
 
 
@@ -483,6 +483,14 @@
     answer_ref,
     home_ref,
     reply_ref,
+    raw_ref,
+    other_raw_ref,
+    other_rim_ref,
+    other_blocks_ref,
+    other_picks_ref,
+    other_select_ref,
+    other_traces_ref,
+    other_sent_ref,
     load_sems,
     row_sends,
     row_recvs,
@@ -492,6 +500,9 @@
     back_recvs,
     rim_sends,
     rim_recvs,
+    near_sends,
+    near_recvs,
+    raw_sems,
 ):
     slots, width = picks_ref.shape
     rcv, slab_len = records_ref.shape
@@ -503,7 +514,7 @@
     slab_count = place.shape[1]
     few = samples // 2 // parts // chunks
     quarter = rcv // 4
-    early_spans = ((0, quarter), (quarter, 2 * quarter), (2 * quarter, rcv))
+    early_spans = ((quarter, 2 * quarter), (2 * quarter, rcv))
     late_spans = ((0, 2 * quarter), (2 * quarter, rcv))
     edge = head_ref.shape[1]
     all_rcv = rcv * place.shape[0]
@@ -546,7 +557,6 @@
     row_ref[...] = jnp.zeros_like(row_ref)
     row_ref[0:1, :shot_count] = offsets_ref[...]
     row_ref[1:2, :shot_count] = filters_ref[...]
-    build_taps(signatures_ref, True, adjoint_ref)
     pl.semaphore_wait(barrier, len(hops))
 
     tile = row_ref.shape[0]
@@ -567,6 +577,9 @@
             row_copies.append(copy)
     rows_ref[here] = row_ref[...]
     loads[0].wait()
+    apart = slab_count // 2
+    partner_slab = lax.rem(slab + apart, slab_count)
+    partner = device_at(sizes, (sizes[0] // 2, 0, 0))[1]
     first_rim = pltpu.make_async_remote_copy(
         src_ref=records_ref.at[:, pl.ds(0, rim_ref.shape[1])],
         dst_ref=rim_ref,
@@ -575,10 +588,19 @@
         device_id=slab_device(-1),
         device_id_type=MESH,
     )
+    partner_rim = pltpu.make_async_remote_copy(
+        src_ref=records_ref.at[pl.ds(0, tile), pl.ds(0, rim_ref.shape[1])],
+        dst_ref=other_rim_ref,
+        send_sem=rim_sends.at[SPANS, 1],
+        recv_sem=rim_recvs.at[SPANS, 1],
+        device_id=slab_device(apart - 1),
+        device_id_type=MESH,
+    )
 
     @pl.when(slab > 0)
     def _():
         first_rim.start()
+        partner_rim.start()
 
     for line in range(rcv):
         blocks_ref[line * padded + blocks : (line + 1) * padded] = jnp.zeros(
@@ -588,6 +610,18 @@
         blocks_ref[pl.ds(block, rcv, stride=padded), :] = records_ref[
             :, block * width : (block + 1) * width
         ]
+    for line in range(quarter):
+        raw_ref[line] = blocks_ref[line * padded : line * padded + blocks].astype(jnp.bfloat16)
+    raw = pltpu.make_async_remote_copy(
+        src_ref=raw_ref,
+        dst_ref=other_raw_ref,
+        send_sem=raw_sems.at[0],
+        recv_sem=raw_sems.at[1],
+        device_id=slab_device(apart),
+        device_id_type=MESH,
+    )
+    raw.start()
+    build_taps(signatures_ref, True, adjoint_ref)
     for copy in row_copies:
         copy.wait_recv()
 
@@ -606,20 +640,27 @@
     key = jnp.where(valid, owner * capacity + rank + 1, zero)
     first_block = (lax.shift_right_logical(start_sample, block_bits) & (blocks - 1)).astype(wide)
     signature = signature.astype(wide)
-    firsts, picks = [], []
-    for level in range(capacity):
-        taken = key == slab * capacity + level + 1
-        empty = jnp.zeros_like(first_block)
-        firsts.append(jnp.sum(jnp.where(taken, first_block + 1.0, empty), axis=1, keepdims=True))
-        picks.append(jnp.sum(jnp.where(taken, signature, empty), axis=1, keepdims=True))
-    firsts = jnp.broadcast_to(jnp.concatenate(firsts, axis=0), (slots, padded))
-    firsts = jnp.where(firsts > 0.5, firsts - 1.0, -float(samples))
-    picks_ref[...] = jnp.broadcast_to(jnp.concatenate(picks, axis=0), (slots, width))
     block_index = lax.broadcasted_iota(jnp.int32, (slots, padded), 1).astype(wide)
-    select = jnp.concatenate(
-        [(block_index == firsts + float(step)).astype(wide) for step in range(steps)], axis=0
-    )
-    select_ref[...] = select.astype(jnp.bfloat16)
+
+    def choose(owner_slab, into_picks_ref, into_select_ref):
+        firsts, picks = [], []
+        for level in range(capacity):
+            taken = key == owner_slab * capacity + level + 1
+            empty = jnp.zeros_like(first_block)
+            firsts.append(
+                jnp.sum(jnp.where(taken, first_block + 1.0, empty), axis=1, keepdims=True)
+            )
+            picks.append(jnp.sum(jnp.where(taken, signature, empty), axis=1, keepdims=True))
+        firsts = jnp.broadcast_to(jnp.concatenate(firsts, axis=0), (slots, padded))
+        firsts = jnp.where(firsts > 0.5, firsts - 1.0, -float(samples))
+        into_picks_ref[...] = jnp.broadcast_to(jnp.concatenate(picks, axis=0), (slots, width))
+        select = jnp.concatenate(
+            [(block_index == firsts + float(step)).astype(wide) for step in range(steps)], axis=0
+        )
+        into_select_ref[...] = select.astype(jnp.bfloat16)
+        return select
+
+    select = choose(slab, picks_ref, select_ref)
 
     @pl.when(slab < last_slab)
     def _():
@@ -649,14 +690,17 @@
         target[mine, where] = source[mine, where]
         return made
 
-    def send_span(number, span, from_ref, model):
+    def correlate_span(span, from_ref, model, one_select_ref, one_picks_ref, into_ref):
         def one(line, carry):
             correlate_line(
-                line, padded, select_ref, from_ref, adjoint_ref, picks_ref, model, traces_ref
+                line, padded, one_select_ref, from_ref, adjoint_ref, one_picks_ref, model, into_ref
             )
             return carry
 
         lax.fori_loop(span[0], span[1], one, 0, unroll=UNROLL)
+
+    def send_span(number, span, from_ref, model):
+        correlate_span(span, from_ref, model, select_ref, picks_ref, traces_ref)
         made = []
         for chunk in range(chunks):
             spectra_chunk(
@@ -674,6 +718,38 @@
             )
         return made
 
+    def send_near(number, from_ref, one_select_ref, one_picks_ref, into_ref, out_ref, owner):
+        span = (0, quarter)
+        correlate_span(span, from_ref, None, one_select_ref, one_picks_ref, into_ref)
+        where = pl.ds(0, quarter * few)
+        depth, place_x, core = (lax.axis_index(axis) for axis in AXES)
+        made = []
+        for chunk in range(chunks):
+            spectra_chunk(
+                table_ref[chunk], into_ref, out_ref.at[chunk], range(*span), rcv, slots
+            )
+            copies = []
+            for hop in range(1, 8):
+                spot = (
+                    depth + (hop // 4) * (1 - 2 * lax.rem(depth, 2)),
+                    lax.rem(place_x + hop // 2 % 2, sizes[1]),
+                    lax.rem(core + hop % 2, sizes[2]),
+                )
+                index = (spot[0] * sizes[1] + spot[1]) * sizes[2] + spot[2]
+                copy = pltpu.make_async_remote_copy(
+                    src_ref=out_ref.at[chunk, index, where],
+                    dst_ref=got_ref.at[chunk, owner, where],
+                    send_sem=near_sends.at[number, chunk, hop - 1],
+                    recv_sem=near_recvs.at[number, chunk, hop - 1],
+                    device_id=dict(zip(AXES, spot)),
+                    device_id_type=MESH,
+                )
+                copy.start()
+                copies.append(copy)
+            got_ref[chunk, owner, where] = out_ref[chunk, mine, where]
+            made.append(copies)
+        return made
+
     def level_at(index, chunk):
         return level_of(levels_ref, index, (mine * chunks + chunk) * few, few, all_rcv)
 
@@ -681,6 +757,28 @@
         send_span(number, span, blocks_ref, None) for number, span in enumerate(early_spans)
     ]
 
+    going.append(send_near(0, blocks_ref, select_ref, picks_ref, traces_ref, sent_ref, mine))
+    choose(partner_slab, other_picks_ref, other_select_ref)
+    raw.wait_recv()
+    for line in range(quarter):
+        other_blocks_ref[line * padded : line * padded + blocks] = other_raw_ref[line].astype(wide)
+        other_blocks_ref[line * padded + blocks : (line + 1) * padded] = jnp.zeros(
+            (padded - blocks, width), wide
+        )
+
+    @pl.when(partner_slab < last_slab)
+    def _():
+        partner_rim.wait_recv()
+        for step in range(rim_ref.shape[1] // width):
+            other_blocks_ref[pl.ds(blocks + step, quarter, stride=padded), :] = other_rim_ref[
+                :quarter, step * width : (step + 1) * width
+            ]
+
+    going.append(
+        send_near(
+            1, other_blocks_ref, other_select_ref, other_picks_ref, other_traces_ref, other_sent_ref, partner
+        )
+    )
     place_ref[...] = select.T.astype(jnp.bfloat16)
     build_taps(signatures_ref, False, forward_ref)
     repeated = key
@@ -730,9 +828,12 @@
     for copy in row_copies:
         copy.wait_send()
 
+    raw.wait_send()
+
     @pl.when(slab > 0)
     def _():
         first_rim.wait_send()
+        partner_rim.wait_send()
 
     for made in going:
         for chunk in made:
@@ -980,11 +1081,23 @@
         ]
         + [pltpu.VMEM((local_rcv, edge, tap_count), wide)] * 4
         + [pltpu.VMEM((chunks, parts, rows, 2 * slots), low)] * 4
-        + [pltpu.VMEM((chunks, parts, rows // 2, 4 * shot_count), low)]
+        + [
+            pltpu.VMEM((chunks, parts, rows // 2, 4 * shot_count), low),
+            pltpu.VMEM((local_rcv // 4, slab_blocks, tap_count), low),
+            pltpu.VMEM((local_rcv // 4, slab_blocks, tap_count), low),
+            pltpu.VMEM((edge, (steps - 1) * tap_count), wide),
+            pltpu.VMEM((local_rcv // 4 * padded, tap_count), wide),
+            pltpu.VMEM((slots, tap_count), wide),
+            pltpu.VMEM((slots * steps, padded), low),
+            pltpu.VMEM((local_rcv // 4 * slots, NT), low),
+            pltpu.VMEM((chunks, parts, rows, 2 * slots), low),
+        ]
         + [pltpu.SemaphoreType.DMA((len(big),))]
         + [pltpu.SemaphoreType.DMA((slab_count - 1,))] * 2
         + [pltpu.SemaphoreType.DMA((SPANS, chunks, parts - 1))] * 4
-        + [pltpu.SemaphoreType.DMA((SPANS + 1, 2))] * 2,
+        + [pltpu.SemaphoreType.DMA((SPANS + 1, 2))] * 2
+        + [pltpu.SemaphoreType.DMA((2, chunks, parts // 2 - 1))] * 2
+        + [pltpu.SemaphoreType.DMA((2,))],
         compiler_params=pltpu.CompilerParams(
             collective_id=0, has_side_effects=True, vmem_limit_bytes=60 * 2**20
         ),
@@ -1003,6 +1116,7 @@
     fits = fits and records.shape[0] == 16 and NT // 2 // parts == 16
     slab_len, tap_count = records.shape[1], signatures.shape[1]
     fits = fits and tap_count == 128 and slab_len & (slab_len - 1) == 0
+    fits = fits and tuple(lax.axis_size(axis) for axis in AXES) == (4, 2, 2)
     run = body_by_slots if fits else body_by_rows
     return run(records, offsets, filter_index, signatures, thresholds)
 

time: 104 us -> 98.2 us (0.944)
  Pallas kernels: 103 us -> 97.2 us
    pallas_call x1, Pallas kernels: 101 us -> 95.4 us  [body_by_slots(): pl.pallas_call(functools.partial(whole_kernel, sizes, place), out_shape=(...]
where the time goes in v6:
time: 98.2 us; the launch traced here: 98 us
  Pallas kernels  97.2 us (99%)
    pallas_call x1, Pallas kernels, body_by_slots(): pl.pallas_call(functools.partial(whole_kernel, sizes, place), out_shape=(...  95.4 us

profile of v6, /device:TPU:0, one launch (start us, length us, event | category | flops | bytes accessed | tf_op | source)
XLA Modules:
  0.0 98.0 jit_solution(17615731399324655376)
XLA Ops:
  0.6 0.0 copy-start
  0.6 95.4 %shard_map.113 = (bf16[2,16,64,128]{3,2,1,0:T(8,128)(2,1)S(1)}, f32[16,16384]{1,0:T(8,128)S(1)}) custom-call(s32[1,32]{1,0:T(1,128)} %offsets_ref.1, s32[1,32]{1,0:T(1,128)} %filters_ref.1, bf16[8,128]{1,0:T(8,128)(2,1)} %signatures_ref.1, f32[2,256]{1,0:T(2,128)} %levels_ref.1, f32[16,16384]{1,0:T(8,128)} %records_hbm.1, ...), custom_call_target="tpu_custom_call" | custom-call | tf_op jit(solution)/shard_map/pallas_call | solution.py:1058
  96.0 0.0 copy-done
  96.0 1.8 %shard_map.114 = (f32[2,8,32,512]{3,2,1,0:T(8,128)}, f32[16,16384]{1,0:T(8,128)}) custom-call(bf16[2,16,64,128]{3,2,1,0:T(8,128)(2,1)S(1)} %get-tuple-element.6.spectra_ref, f32[16,16384]{1,0:T(8,128)S(1)} %get-tuple-element.7.left_ref, bf16[2,256,512]{2,1,0:T(8,128)(2,1)S(1)} %copy-done), custom_call_target="tpu_custom_call" | custom-call | tf_op jit(solution)/shard_map/pallas_call | solution.py:989
Async XLA Ops:
  0.6 95.4 %copy-start = (bf16[2,256,512]{2,1,0:T(8,128)(2,1)S(1)}, bf16[2,256,512]{2,1,0:T(8,128)(2,1)}, u32[]{:S(2)}) copy-start(bf16[2,256,512]{2,1,0:T(8,128)(2,1)} %constant.10.clone.table_hbm.table_ref) | copy-start | bytes 1572868

commit v7 on v6

--- a/solution.py
+++ b/solution.py
@@ -436,7 +436,7 @@
 
 
 CHUNKS = 2
-SPANS = 2
+SPANS = 4
 UNROLL = 4
 
 
@@ -450,7 +450,6 @@
     records_hbm,
     table_hbm,
     grid_hbm,
-    row_table_hbm,
     cosine_hbm,
     sine_hbm,
     final_ref,
@@ -458,7 +457,6 @@
     records_ref,
     table_ref,
     grid_ref,
-    row_table_ref,
     cosine_ref,
     sine_ref,
     row_ref,
@@ -466,6 +464,7 @@
     rim_ref,
     picks_ref,
     slot_table_ref,
+    row_table_ref,
     adjoint_ref,
     forward_ref,
     select_ref,
@@ -515,7 +514,8 @@
     few = samples // 2 // parts // chunks
     quarter = rcv // 4
     early_spans = ((quarter, 2 * quarter), (2 * quarter, rcv))
-    late_spans = ((0, 2 * quarter), (2 * quarter, rcv))
+    late_halves = ((0, 2 * quarter), (2 * quarter, rcv))
+    late_spans = tuple((number * quarter, (number + 1) * quarter) for number in range(4))
     edge = head_ref.shape[1]
     all_rcv = rcv * place.shape[0]
     shot_count = offsets_ref.shape[1]
@@ -532,7 +532,6 @@
                 (grid_hbm, grid_ref),
                 (cosine_hbm, cosine_ref),
                 (sine_hbm, sine_ref),
-                (row_table_hbm, row_table_ref),
             )
         )
     ]
@@ -697,7 +696,8 @@
             )
             return carry
 
-        lax.fori_loop(span[0], span[1], one, 0, unroll=UNROLL)
+        unroll = UNROLL if model is not None or span[0] == quarter else UNROLL // 2
+        lax.fori_loop(span[0], span[1], one, 0, unroll=unroll)
 
     def send_span(number, span, from_ref, model):
         correlate_span(span, from_ref, model, select_ref, picks_ref, traces_ref)
@@ -796,6 +796,10 @@
     for load in loads[2:]:
         load.wait()
     for half in range(2):
+        for number in range(row_count):
+            low = (2 * number + half) * shot_count
+            source = half * points + number * shot_count
+            row_table_ref[low : low + shot_count] = grid_ref[source : source + shot_count]
         part = dot(chosen, grid_ref[half * points : (half + 1) * points]).astype(jnp.bfloat16)
         for number in range(slab_count):
             low = (2 * number + half) * slots
@@ -804,7 +808,7 @@
     coming = {}
 
     def send_back(number, chunk):
-        span = late_spans[number]
+        span = late_halves[number]
         coming[number, chunk] = exchange(
             answer_ref.at[chunk],
             home_ref.at[chunk],
@@ -822,7 +826,7 @@
             place, 1, got_ref.at[chunk], slot_table_ref, slot_table_ref, cosine_ref[...], sine_ref[...], level_at(0, chunk), answer_ref.at[chunk]
         )
         send_back(0, chunk)
-    for number in range(1, len(late_spans)):
+    for number in range(1, len(late_halves)):
         for chunk in range(chunks):
             send_back(number, chunk)
     for copy in row_copies:
@@ -863,9 +867,10 @@
 
     def subtract(number):
         low, high = late_spans[number]
-        for chunk in range(chunks):
-            for copy in coming[number, chunk]:
-                copy.wait_recv()
+        if number % 2 == 0:
+            for chunk in range(chunks):
+                for copy in coming[number // 2, chunk]:
+                    copy.wait_recv()
         together = math.gcd(high - low, 4)
         for first in range(low, high, together):
             lines = range(first, first + together)
@@ -922,9 +927,11 @@
         return send_span(number, late_spans[number], rest_ref, field_ref)
 
     again = []
-    for number in range(len(late_spans)):
+    for number in range(0, len(late_spans), 2):
         subtract(number)
+        subtract(number + 1)
         again.append(correlate_rest(number))
+        again.append(correlate_rest(number + 1))
 
     for block in range(blocks):
         left_ref[:, block * width : (block + 1) * width] = rest_ref[
@@ -1039,10 +1046,8 @@
         fixed_shot_table(count) for count in (row_count, shot_count, local_rcv * rcv_count)
     )
     grid_table = np.einsum("ajby,bkcx->cxyakj", table_y, table_x).astype(jnp.bfloat16)
-    row_table = np.ascontiguousarray(grid_table.transpose(1, 0, 2, 3, 4, 5))
     points = 2 * row_count * shot_count
     grid_table = jnp.asarray(grid_table.reshape(points, points))
-    row_table = jnp.asarray(row_table.reshape(points, points))
     same = np.eye(few, dtype=np.float32)
     cosine = jnp.asarray(np.kron(table_r[0, :, 0], same).astype(jnp.bfloat16))
     sine = jnp.asarray(np.kron(table_r[0, :, 1], same).astype(jnp.bfloat16))
@@ -1054,7 +1059,7 @@
     rows = local_rcv * few
     table_width = tap_count * signatures.shape[0]
     low, wide = jnp.bfloat16, jnp.float32
-    big = (records, time_table_fixed, grid_table, row_table, cosine, sine)
+    big = (records, time_table_fixed, grid_table, cosine, sine)
     spectra, residual = pl.pallas_call(
         functools.partial(whole_kernel, sizes, place),
         out_shape=(
@@ -1070,6 +1075,7 @@
             pltpu.VMEM((local_rcv, (steps - 1) * tap_count), wide),
             pltpu.VMEM((slots, tap_count), wide),
             pltpu.VMEM((slab_count * 2 * slots, points), low),
+            pltpu.VMEM((points, points), low),
             pltpu.VMEM((2 * tap_count, table_width), low),
             pltpu.VMEM((2 * tap_count, table_width), low),
             pltpu.VMEM((slots * steps, padded), low),

time: 98.2 us -> 103 us (1.049)
  Pallas kernels: 97.2 us -> 102 us
    pallas_call x1, Pallas kernels: 95.4 us -> 101 us  [body_by_slots(): pl.pallas_call(functools.partial(whole_kernel, sizes, place), out_shape=(...]
where the time goes in v7:
time: 103 us
  Pallas kernels  102 us (99%)
    pallas_call x1, Pallas kernels, body_by_slots(): pl.pallas_call(functools.partial(whole_kernel, sizes, place), out_shape=(...  101 us

profile of v7, /device:TPU:0, one launch (start us, length us, event | category | flops | bytes accessed | tf_op | source)
XLA Modules:
  0.0 103.3 jit_solution(4360621326091555093)
XLA Ops:
  0.6 0.0 copy-start
  0.6 100.6 %shard_map.104 = (bf16[2,16,64,128]{3,2,1,0:T(8,128)(2,1)S(1)}, f32[16,16384]{1,0:T(8,128)S(1)}) custom-call(s32[1,32]{1,0:T(1,128)} %offsets_ref.1, s32[1,32]{1,0:T(1,128)} %filters_ref.1, bf16[8,128]{1,0:T(8,128)(2,1)} %signatures_ref.1, f32[2,256]{1,0:T(2,128)} %levels_ref.1, f32[16,16384]{1,0:T(8,128)} %records_hbm.1, ...), custom_call_target="tpu_custom_call" | custom-call | tf_op jit(solution)/shard_map/pallas_call | solution.py:1063
  101.3 0.0 copy-done
  101.3 1.8 %shard_map.105 = (f32[2,8,32,512]{3,2,1,0:T(8,128)}, f32[16,16384]{1,0:T(8,128)}) custom-call(bf16[2,16,64,128]{3,2,1,0:T(8,128)(2,1)S(1)} %get-tuple-element.6.spectra_ref, f32[16,16384]{1,0:T(8,128)S(1)} %get-tuple-element.7.left_ref, bf16[2,256,512]{2,1,0:T(8,128)(2,1)S(1)} %copy-done), custom_call_target="tpu_custom_call" | custom-call | tf_op jit(solution)/shard_map/pallas_call | solution.py:996
Async XLA Ops:
  0.6 100.7 %copy-start = (bf16[2,256,512]{2,1,0:T(8,128)(2,1)S(1)}, bf16[2,256,512]{2,1,0:T(8,128)(2,1)}, u32[]{:S(2)}) copy-start(bf16[2,256,512]{2,1,0:T(8,128)(2,1)} %constant.8.clone.table_hbm.table_ref) | copy-start | bytes 1572868

commit v8 on v7

--- a/solution.py
+++ b/solution.py
@@ -436,7 +436,7 @@
 
 
 CHUNKS = 2
-SPANS = 4
+SPANS = 2
 UNROLL = 4
 
 
@@ -515,7 +515,7 @@
     quarter = rcv // 4
     early_spans = ((quarter, 2 * quarter), (2 * quarter, rcv))
     late_halves = ((0, 2 * quarter), (2 * quarter, rcv))
-    late_spans = tuple((number * quarter, (number + 1) * quarter) for number in range(4))
+    late_spans = late_halves
     edge = head_ref.shape[1]
     all_rcv = rcv * place.shape[0]
     shot_count = offsets_ref.shape[1]
@@ -696,26 +696,26 @@
             )
             return carry
 
-        unroll = UNROLL if model is not None or span[0] == quarter else UNROLL // 2
-        lax.fori_loop(span[0], span[1], one, 0, unroll=unroll)
-
-    def send_span(number, span, from_ref, model):
-        correlate_span(span, from_ref, model, select_ref, picks_ref, traces_ref)
+        lax.fori_loop(span[0], span[1], one, 0, unroll=UNROLL)
+
+    def span_spectra(span, chunk):
+        spectra_chunk(table_ref[chunk], traces_ref, sent_ref.at[chunk], range(*span), rcv, slots)
+
+    def span_exchange(number, span, chunk):
+        return exchange(
+            sent_ref.at[chunk],
+            got_ref.at[chunk],
+            go_sends.at[number, chunk],
+            go_recvs.at[number, chunk],
+            span[0] * few,
+            (span[1] - span[0]) * few,
+        )
+
+    def send_span(number, span):
         made = []
         for chunk in range(chunks):
-            spectra_chunk(
-                table_ref[chunk], traces_ref, sent_ref.at[chunk], range(*span), rcv, slots
-            )
-            made.append(
-                exchange(
-                    sent_ref.at[chunk],
-                    got_ref.at[chunk],
-                    go_sends.at[number, chunk],
-                    go_recvs.at[number, chunk],
-                    span[0] * few,
-                    (span[1] - span[0]) * few,
-                )
-            )
+            span_spectra(span, chunk)
+            made.append(span_exchange(number, span, chunk))
         return made
 
     def send_near(number, from_ref, one_select_ref, one_picks_ref, into_ref, out_ref, owner):
@@ -753,9 +753,14 @@
     def level_at(index, chunk):
         return level_of(levels_ref, index, (mine * chunks + chunk) * few, few, all_rcv)
 
-    going = [
-        send_span(number, span, blocks_ref, None) for number, span in enumerate(early_spans)
-    ]
+    first_span, second_span = early_spans
+    correlate_span(first_span, blocks_ref, None, select_ref, picks_ref, traces_ref)
+    going = [send_span(0, first_span), []]
+    correlate_span(second_span, blocks_ref, None, select_ref, picks_ref, traces_ref)
+    for chunk in range(chunks):
+        span_spectra(second_span, chunk)
+        if chunk == 0:
+            going[1].append(span_exchange(1, second_span, chunk))
 
     going.append(send_near(0, blocks_ref, select_ref, picks_ref, traces_ref, sent_ref, mine))
     choose(partner_slab, other_picks_ref, other_select_ref)
@@ -779,6 +784,8 @@
             1, other_blocks_ref, other_select_ref, other_picks_ref, other_traces_ref, other_sent_ref, partner
         )
     )
+    for chunk in range(1, chunks):
+        going[1].append(span_exchange(1, second_span, chunk))
     place_ref[...] = select.T.astype(jnp.bfloat16)
     build_taps(signatures_ref, False, forward_ref)
     repeated = key
@@ -826,9 +833,7 @@
             place, 1, got_ref.at[chunk], slot_table_ref, slot_table_ref, cosine_ref[...], sine_ref[...], level_at(0, chunk), answer_ref.at[chunk]
         )
         send_back(0, chunk)
-    for number in range(1, len(late_halves)):
-        for chunk in range(chunks):
-            send_back(number, chunk)
+    send_back(1, 0)
     for copy in row_copies:
         copy.wait_send()
 
@@ -867,9 +872,9 @@
 
     def subtract(number):
         low, high = late_spans[number]
-        if number % 2 == 0:
+        if True:
             for chunk in range(chunks):
-                for copy in coming[number // 2, chunk]:
+                for copy in coming[number, chunk]:
                     copy.wait_recv()
         together = math.gcd(high - low, 4)
         for first in range(low, high, together):
@@ -924,14 +929,22 @@
         def _():
             backward.wait_send()
 
-        return send_span(number, late_spans[number], rest_ref, field_ref)
-
-    again = []
-    for number in range(0, len(late_spans), 2):
-        subtract(number)
-        subtract(number + 1)
-        again.append(correlate_rest(number))
-        again.append(correlate_rest(number + 1))
+        correlate_span((low, high), rest_ref, field_ref, select_ref, picks_ref, traces_ref)
+
+    again = [[], []]
+    subtract(0)
+    for chunk in range(1, chunks):
+        send_back(1, chunk)
+    correlate_rest(0)
+    span_spectra(late_halves[0], 0)
+    again[0].append(span_exchange(0, late_halves[0], 0))
+    for chunk in range(1, chunks):
+        span_spectra(late_halves[0], chunk)
+    subtract(1)
+    for chunk in range(1, chunks):
+        again[0].append(span_exchange(0, late_halves[0], chunk))
+    correlate_rest(1)
+    again[1] = send_span(1, late_halves[1])
 
     for block in range(blocks):
         left_ref[:, block * width : (block + 1) * width] = rest_ref[
@@ -1100,7 +1113,7 @@
         ]
         + [pltpu.SemaphoreType.DMA((len(big),))]
         + [pltpu.SemaphoreType.DMA((slab_count - 1,))] * 2
-        + [pltpu.SemaphoreType.DMA((SPANS, chunks, parts - 1))] * 4
+        + [pltpu.SemaphoreType.DMA((2, chunks, parts - 1))] * 4
         + [pltpu.SemaphoreType.DMA((SPANS + 1, 2))] * 2
         + [pltpu.SemaphoreType.DMA((2, chunks, parts // 2 - 1))] * 2
         + [pltpu.SemaphoreType.DMA((2,))],

time: 103 us -> 97.1 us (0.943)
  Pallas kernels: 102 us -> 96.1 us
    pallas_call x1, Pallas kernels: 101 us -> 94.3 us  [body_by_slots(): pl.pallas_call(functools.partial(whole_kernel, sizes, place), out_shape=(...]
where the time goes in v8:
time: 97.1 us; the launch traced here: 97 us
  Pallas kernels  96.1 us (99%)
    pallas_call x1, Pallas kernels, body_by_slots(): pl.pallas_call(functools.partial(whole_kernel, sizes, place), out_shape=(...  94.3 us

profile of v8, /device:TPU:0, one launch (start us, length us, event | category | flops | bytes accessed | tf_op | source)
XLA Modules:
  0.0 97.0 jit_solution(5083701255568969962)
XLA Ops:
  0.6 0.0 copy-start
  0.6 94.3 %shard_map.104 = (bf16[2,16,64,128]{3,2,1,0:T(8,128)(2,1)S(1)}, f32[16,16384]{1,0:T(8,128)S(1)}) custom-call(s32[1,32]{1,0:T(1,128)} %offsets_ref.1, s32[1,32]{1,0:T(1,128)} %filters_ref.1, bf16[8,128]{1,0:T(8,128)(2,1)} %signatures_ref.1, f32[2,256]{1,0:T(2,128)} %levels_ref.1, f32[16,16384]{1,0:T(8,128)} %records_hbm.1, ...), custom_call_target="tpu_custom_call" | custom-call | tf_op jit(solution)/shard_map/pallas_call | solution.py:1076
  94.9 0.0 copy-done
  95.0 1.8 %shard_map.105 = (f32[2,8,32,512]{3,2,1,0:T(8,128)}, f32[16,16384]{1,0:T(8,128)}) custom-call(bf16[2,16,64,128]{3,2,1,0:T(8,128)(2,1)S(1)} %get-tuple-element.6.spectra_ref, f32[16,16384]{1,0:T(8,128)S(1)} %get-tuple-element.7.left_ref, bf16[2,256,512]{2,1,0:T(8,128)(2,1)S(1)} %copy-done), custom_call_target="tpu_custom_call" | custom-call | tf_op jit(solution)/shard_map/pallas_call | solution.py:1009
Async XLA Ops:
  0.6 94.3 %copy-start = (bf16[2,256,512]{2,1,0:T(8,128)(2,1)S(1)}, bf16[2,256,512]{2,1,0:T(8,128)(2,1)}, u32[]{:S(2)}) copy-start(bf16[2,256,512]{2,1,0:T(8,128)(2,1)} %constant.8.clone.table_hbm.table_ref) | copy-start | bytes 1572868

commit v9 on v8

--- a/solution.py
+++ b/solution.py
@@ -756,13 +756,13 @@
     first_span, second_span = early_spans
     correlate_span(first_span, blocks_ref, None, select_ref, picks_ref, traces_ref)
     going = [send_span(0, first_span), []]
+    going.append(send_near(0, blocks_ref, select_ref, picks_ref, traces_ref, sent_ref, mine))
     correlate_span(second_span, blocks_ref, None, select_ref, picks_ref, traces_ref)
     for chunk in range(chunks):
         span_spectra(second_span, chunk)
         if chunk == 0:
             going[1].append(span_exchange(1, second_span, chunk))
 
-    going.append(send_near(0, blocks_ref, select_ref, picks_ref, traces_ref, sent_ref, mine))
     choose(partner_slab, other_picks_ref, other_select_ref)
     raw.wait_recv()
     for line in range(quarter):
@@ -872,17 +872,17 @@
 
     def subtract(number):
         low, high = late_spans[number]
-        if True:
-            for chunk in range(chunks):
-                for copy in coming[number, chunk]:
-                    copy.wait_recv()
         together = math.gcd(high - low, 4)
-        for first in range(low, high, together):
-            lines = range(first, first + together)
-            field_ref[first * slots : (first + together) * slots] = sum(
-                dot(upright(home_ref, chunk, lines, few, 2 * slots), table_ref[chunk])
-                for chunk in range(chunks)
-            )
+        for chunk in range(chunks):
+            for copy in coming[number, chunk]:
+                copy.wait_recv()
+            for first in range(low, high, together):
+                where = slice(first * slots, (first + together) * slots)
+                lines = range(first, first + together)
+                field = dot(upright(home_ref, chunk, lines, few, 2 * slots), table_ref[chunk])
+                if chunk:
+                    field = field + field_ref[where]
+                field_ref[where] = field
 
         def one(line, carry):
             blended = blend_line(line, place_ref, field_ref, forward_ref, picks_ref)

time: 97.1 us -> 96.9 us (level)
  no operation moved by 1% of the time
where the time goes in v9:
time: 96.9 us; the launch traced here: 96.7 us
  Pallas kernels  95.9 us (99%)
    pallas_call x1, Pallas kernels, body_by_slots(): pl.pallas_call(functools.partial(whole_kernel, sizes, place), out_shape=(...  94 us

profile of v9, /device:TPU:0, one launch (start us, length us, event | category | flops | bytes accessed | tf_op | source)
XLA Modules:
  0.0 96.7 jit_solution(1788562393830962612)
XLA Ops:
  0.6 0.0 copy-start
  0.6 94.0 %shard_map.104 = (bf16[2,16,64,128]{3,2,1,0:T(8,128)(2,1)S(1)}, f32[16,16384]{1,0:T(8,128)S(1)}) custom-call(s32[1,32]{1,0:T(1,128)} %offsets_ref.1, s32[1,32]{1,0:T(1,128)} %filters_ref.1, bf16[8,128]{1,0:T(8,128)(2,1)} %signatures_ref.1, f32[2,256]{1,0:T(2,128)} %levels_ref.1, f32[16,16384]{1,0:T(8,128)} %records_hbm.1, ...), custom_call_target="tpu_custom_call" | custom-call | tf_op jit(solution)/shard_map/pallas_call | solution.py:1076
  94.7 0.0 copy-done
  94.7 1.8 %shard_map.105 = (f32[2,8,32,512]{3,2,1,0:T(8,128)}, f32[16,16384]{1,0:T(8,128)}) custom-call(bf16[2,16,64,128]{3,2,1,0:T(8,128)(2,1)S(1)} %get-tuple-element.6.spectra_ref, f32[16,16384]{1,0:T(8,128)S(1)} %get-tuple-element.7.left_ref, bf16[2,256,512]{2,1,0:T(8,128)(2,1)S(1)} %copy-done), custom_call_target="tpu_custom_call" | custom-call | tf_op jit(solution)/shard_map/pallas_call | solution.py:1009
Async XLA Ops:
  0.6 94.0 %copy-start = (bf16[2,256,512]{2,1,0:T(8,128)(2,1)S(1)}, bf16[2,256,512]{2,1,0:T(8,128)(2,1)}, u32[]{:S(2)}) copy-start(bf16[2,256,512]{2,1,0:T(8,128)(2,1)} %constant.8.clone.table_hbm.table_ref) | copy-start | bytes 1572868
